TPU v7x, 32 devices: a whole 2x2x4 slice. The times are simulated.
32 devices in a mesh: jobs: 2 (over y), gr: 4 (over x, core), gc: 4 (over z).
Axes of the slice: x: 2, y: 2, z: 4, core: 2. Of those that a mesh axis runs over, the one named last changes fastest.
Arguments:
- pair: bfloat16 [160, 80, 128], P(('jobs', 'gr'), 'gc'), parts along dimension 0, may hold values from -6 to 6
- mask: int32 [160], P('jobs'), parts along dimension 0, may hold values 0 or 1
- chain_ids: int32 [160], P('jobs'), parts along dimension 0, may hold values from 0 to 3, never falling along the last dimension, each value on 1 to 40 neighbouring positions
- attn_in: bfloat16 [2, 128, 512], replicated, may hold values from -0.5 to 0.5
- attn_out: bfloat16 [2, 128, 128], replicated, may hold values from -0.5 to 0.5
- bias_weight: bfloat16 [2, 128, 4], replicated, may hold values from -16 to 16
- chain_bias: float32 [2, 4], replicated, may hold values from -6 to 6
- trans_up: bfloat16 [128, 512], replicated, may hold values from -0.5 to 0.5
- trans_down: bfloat16 [512, 128], replicated, may hold values from -0.25 to 0.25
Outputs:
- result: bfloat16 [160, 80, 128], P(('jobs', 'gr'), 'gc'), parts along dimension 0
There are 2 independent parts, one for each index of `jobs`. A program takes and returns all parts, laid end to end along the dimension named above; an argument that names none is the same for every part. Nothing has to cross between parts.
All inputs are finite; a program needn't handle non-finite values.
Results may differ from a plain program's by a relative error of at most 0.008.
The roundings to bfloat16 on the way count: a program that leaves them out, or rounds other values in their place, can miss the bound.
Values may be sent and summed in bfloat16 or wider, within the bound.
No kernel may reach another device: no remote copies, remote signals or barrier semaphores. Data moves between devices by JAX's collectives and lax.ppermute only.
A program may use at most 64 MiB of HBM per device.

v0:
```python
import jax
import jax.numpy as jnp
from jax import lax
from jax.sharding import PartitionSpec as P


def layer_norm(values):
    floats = values.astype(jnp.float32)
    center = jnp.mean(floats, axis=-1, keepdims=True)
    spread = jnp.mean((floats - center) ** 2, axis=-1, keepdims=True)
    return ((floats - center) * lax.rsqrt(spread + 1e-05)).astype(jnp.bfloat16)


def bias_terms(normed, weight, offset, chain_left, chain_right):
    first, second, width = normed.shape
    heads = weight.shape[1]
    terms = jnp.dot(normed.reshape(-1, width), weight, preferred_element_type=jnp.float32)
    same = (chain_left[:, None] == chain_right[None, :]).astype(jnp.float32)
    return terms.reshape(first, second, heads) + offset[None, None, :] * same[:, :, None]


def attention(rows, normed, in_w, out_w, bias_full, maskadd):
    count, length, width = rows.shape
    heads = bias_full.shape[0]
    head_width = width // heads
    scale = head_width ** (-0.5)
    proj = jnp.dot(normed.reshape(-1, width), in_w, preferred_element_type=jnp.float32)
    proj = proj.astype(jnp.bfloat16).reshape(count, length, 4 * width)

    def one_row(piece):
        query = piece[:, 0:width].reshape(length, heads, head_width)
        keys = piece[:, width : 2 * width].reshape(length, heads, head_width)
        vals = piece[:, 2 * width : 3 * width].reshape(length, heads, head_width)
        gate = piece[:, 3 * width :].astype(jnp.float32)
        scores = jnp.einsum("jhd,khd->hjk", query, keys, preferred_element_type=jnp.float32) * scale
        scores = scores + bias_full + maskadd[None, None, :]
        probs = jax.nn.softmax(scores, axis=-1).astype(jnp.bfloat16)
        mixed = jnp.einsum("hjk,khd->jhd", probs, vals, preferred_element_type=jnp.float32)
        return (jax.nn.sigmoid(gate) * mixed.reshape(length, width)).astype(jnp.bfloat16)

    gated = lax.map(one_row, proj)
    update = jnp.dot(gated.reshape(-1, width), out_w, preferred_element_type=jnp.float32)
    return (rows.astype(jnp.float32) + update.reshape(rows.shape)).astype(jnp.bfloat16)


def transition(rows, trans_up, trans_down):
    width = rows.shape[-1]
    normed = layer_norm(rows).reshape(-1, width)
    hidden = jax.nn.relu(jnp.dot(normed, trans_up, preferred_element_type=jnp.float32)).astype(
        jnp.bfloat16
    )
    update = jnp.dot(hidden, trans_down, preferred_element_type=jnp.float32)
    return (rows.astype(jnp.float32) + update.reshape(rows.shape)).astype(jnp.bfloat16)


def per_device(
    pair, mask, chain_ids, attn_in, attn_out, bias_weight, chain_bias, trans_up, trans_down
):
    across = lax.axis_size("gc")
    rows = lax.all_to_all(pair, "gc", split_axis=0, concat_axis=1, tiled=True)
    count = rows.shape[0]
    first_row = (lax.axis_index("gr") * across + lax.axis_index("gc")) * count
    maskadd = jnp.where(mask > 0, 0.0, -1000000000.0).astype(jnp.float32)
    own_chain = lax.dynamic_slice_in_dim(chain_ids, first_row, count)
    normed = layer_norm(rows)
    start_part = bias_terms(normed, bias_weight[0], chain_bias[0], own_chain, chain_ids)
    start_full = lax.all_gather(
        jnp.transpose(start_part, (2, 0, 1)), ("gr", "gc"), axis=1, tiled=True
    )
    rows = attention(rows, normed, attn_in[0], attn_out[0], start_full, maskadd)
    tile = lax.all_to_all(rows, "gc", split_axis=1, concat_axis=0, tiled=True)
    tile = transition(tile, trans_up, trans_down)
    tile_rows, tile_cols = (tile.shape[0], tile.shape[1])
    chain_rows = lax.dynamic_slice_in_dim(chain_ids, lax.axis_index("gr") * tile_rows, tile_rows)
    chain_cols = lax.dynamic_slice_in_dim(chain_ids, lax.axis_index("gc") * tile_cols, tile_cols)
    end_part = bias_terms(layer_norm(tile), bias_weight[1], chain_bias[1], chain_rows, chain_cols)
    end_part = lax.all_gather(jnp.transpose(end_part, (2, 1, 0)), "gc", axis=1, tiled=True)
    end_full = lax.all_gather(end_part, "gr", axis=2, tiled=True)
    columns = lax.all_to_all(
        jnp.transpose(tile, (1, 0, 2)), "gr", split_axis=0, concat_axis=1, tiled=True
    )
    columns = attention(columns, layer_norm(columns), attn_in[1], attn_out[1], end_full, maskadd)
    returned = lax.all_to_all(columns, "gr", split_axis=1, concat_axis=0, tiled=True)
    return jnp.transpose(returned, (1, 0, 2))


def solution(mesh):
    in_specs = (P(("jobs", "gr"), "gc", None), P("jobs"), P("jobs"), P(), P(), P(), P(), P(), P())
    out_specs = P(("jobs", "gr"), "gc", None)
    return jax.shard_map(
        per_device, mesh=mesh, in_specs=in_specs, out_specs=out_specs, check_vma=False
    )
```

profile of v0, /device:TPU:0, one launch (start us, length us, event | category | flops | bytes accessed | tf_op | source)
XLA Modules:
  0.0 99.6 jit_solution(12495822166500596514)
XLA Ops:
  0.0 6.5 %all-to-all-start = ((bf16[20,20,128]{2,1,0:T(8,128)(2,1)}), bf16[20,20,128]{2,1,0:T(8,128)(2,1)S(1)}, u32[]{:S(2)}, u32[]{:S(2)}) async-start(bf16[20,20,128]{2,1,0:T(8,128)(2,1)} %param.13), calls=%async_computation | async-start | bytes 245760 | tf_op jit(solution)/shard_map/all_to_all | solution.py:60
  6.5 0.7 copy-done.3
  7.3 0.6 copy-done.4
  7.9 0.6 copy-done.7
  8.6 3.8 %all-to-all-done = bf16[20,20,128]{2,1,0:T(8,128)(2,1)S(1)} async-done(((bf16[20,20,128]{2,1,0:T(8,128)(2,1)}), bf16[20,20,128]{2,1,0:T(8,128)(2,1)S(1)}, u32[]{:S(2)}, u32[]{:S(2)}) %all-to-all-start) | async-done | bytes 102432 | tf_op jit(solution)/shard_map/all_to_all | solution.py:60
  12.6 0.3 multiply_reduce_fusion.2
  12.9 0.2 multiply_convert_fusion.1
  13.2 0.6 copy-done.5
  13.9 0.2 fusion.21
  14.0 31.1 %all_gather.9 = f32[4,80,80]{2,0,1:T(4,128)S(1)} all-gather(f32[4,5,80]{2,0,1:T(4,128)S(1)} %fusion.21), channel_id=1, replica_groups=mesh['jobs'=2,'gr'=4,'gc'=4] {'gr','gc'}, dimensions={1}, use_global_device_ids=true | all-gather | bytes 108800 | tf_op jit(solution)/shard_map/all_gather | solution.py:67
  45.3 0.2 convolution_convert_fusion.1
  45.6 3.4 %while.20 = (s32[]{:T(128)}, bf16[5,80,128]{1,2,0:T(8,128)(2,1)S(1)}, bf16[5,80,512]{2,1,0:T(8,128)(2,1)S(1)}, f32[4,80,80]{1,2,0:T(8,128)S(1)}, f32[80]{0:T(128)S(1)}, /*index=5*/s32[]{:T(128)}) while((s32[]{:T(128)}, bf16[5,80,128]{1,2,0:T(8,128)(2,1)S(1)}, bf16[5,80,512]{2,1,0:T(8,128)(2,1)S(1)}, f32[4,80,80]{1,2,0:T(8,128)S(1)}, ...), condition=%wide.region_5.6_spmd, body=%wide.region_2.5_spmd.sunk | while | flops 3543520 | bytes 1096589 | solution.py:41
  45.7 0.2 fusion.98
  46.4 0.2 fusion.98
  46.7 0.2 fusion.100
  47.1 0.2 fusion.98
  47.4 0.2 fusion.100
  47.8 0.2 fusion.98
  48.4 0.2 fusion.98
  48.7 0.2 fusion.100
  49.0 0.8 copy-done.2
  49.8 0.2 fusion.18
  50.0 0.7 copy.97
  50.7 3.3 %all-to-all-start.1 = ((bf16[5,80,128]{2,0,1:T(8,128)(2,1)}), bf16[5,80,128]{2,0,1:T(8,128)(2,1)S(1)}, u32[]{:S(2)}, u32[]{:S(2)}) async-start(bf16[5,80,128]{2,0,1:T(8,128)(2,1)} %copy.97), calls=%async_computation.1 | async-start | bytes 327680 | tf_op jit(solution)/shard_map/all_to_all | solution.py:71
  54.2 5.9 %all-to-all-done.1 = bf16[5,80,128]{2,0,1:T(8,128)(2,1)S(1)} async-done(((bf16[5,80,128]{2,0,1:T(8,128)(2,1)}), bf16[5,80,128]{2,0,1:T(8,128)(2,1)S(1)}, u32[]{:S(2)}, u32[]{:S(2)}) %all-to-all-start.1) | async-done | bytes 102432 | tf_op jit(solution)/shard_map/all_to_all | solution.py:71
  60.3 0.3 multiply_reduce_fusion.1
  60.8 0.8 copy-done.6
  61.6 0.6 convert_reduce_fusion
  62.2 0.2 fusion.26
  62.4 0.2 fusion.27
  62.7 0.7 copy.103
  63.4 3.3 %all-to-all-start.2 = ((bf16[20,20,128]{2,1,0:T(8,128)(2,1)}), bf16[20,20,128]{2,1,0:T(8,128)(2,1)S(1)}, u32[]{:S(2)}, u32[]{:S(2)}) async-start(bf16[20,20,128]{2,1,0:T(8,128)(2,1)} %copy.103), calls=%async_computation.2 | async-start | bytes 245760 | tf_op jit(solution)/shard_map/all_to_all | solution.py:79
  66.7 0.3 fusion.20
  67.1 13.5 %all_gather.10 = f32[4,80,20]{2,0,1:T(4,128)S(1)} all-gather(f32[4,20,20]{2,0,1:T(4,128)S(1)} %copy.110), channel_id=1, replica_groups=mesh['jobs'=2,'gr'=4,'gc'=4] {'gc'}, dimensions={1}, use_global_device_ids=true | all-gather | bytes 32000 | tf_op jit(solution)/shard_map/all_gather | solution.py:77
  80.7 5.7 %all_gather.11 = f32[4,80,80]{1,0,2:T(4,128)S(1)} all-gather(f32[4,80,20]{1,0,2:T(4,128)S(1)} %copy.111), channel_id=1, replica_groups=mesh['jobs'=2,'gr'=4,'gc'=4] {'gr'}, dimensions={2}, use_global_device_ids=true | all-gather | bytes 128000 | tf_op jit(solution)/shard_map/all_gather | solution.py:78
  86.6 0.2 multiply_reduce_fusion
  86.9 0.2 multiply_convert_fusion
  87.1 0.2 convolution_convert_fusion
  87.4 3.4 %while.21 = (s32[]{:T(128)}, bf16[5,80,128]{1,2,0:T(8,128)(2,1)S(1)}, bf16[5,80,512]{2,1,0:T(8,128)(2,1)S(1)}, f32[4,80,80]{1,2,0:T(8,128)S(1)}, f32[80]{0:T(128)S(1)}, /*index=5*/s32[]{:T(128)}) while((s32[]{:T(128)}, bf16[5,80,128]{1,2,0:T(8,128)(2,1)S(1)}, bf16[5,80,512]{2,1,0:T(8,128)(2,1)S(1)}, f32[4,80,80]{1,2,0:T(8,128)S(1)}, ...), condition=%wide.region_15.16_spmd, body=%wide.region_12.15_spmd.sunk | while | flops 3543520 | bytes 1096589 | solution.py:41
  87.6 0.2 fusion.107
  87.9 0.2 fusion.109
  88.3 0.2 fusion.107
  88.9 0.2 fusion.107
  89.6 0.2 fusion.107
  90.3 0.2 fusion.107
  90.9 0.2 fusion.19
  91.1 7.8 %all_to_all.45 = bf16[5,80,128]{2,0,1:T(8,128)(2,1)S(1)} all-to-all(bf16[5,80,128]{2,0,1:T(8,128)(2,1)S(1)} %copy.115), channel_id=1, replica_groups=mesh['jobs'=2,'gr'=4,'gc'=4] {'gr'}, dimensions={1} | all-to-all | bytes 204800 | tf_op jit(solution)/shard_map/all_to_all | solution.py:83
  99.0 0.7 copy.118
  (112 shorter events, 5.2 us)
Async XLA Ops:
  0.0 60.8 %copy-start = (bf16[512,128]{1,0:T(8,128)(2,1)S(1)}, bf16[512,128]{1,0:T(8,128)(2,1)}, u32[]{:S(2)}) copy-start(bf16[512,128]{1,0:T(8,128)(2,1)} %param.21) | copy-start | bytes 393220
  0.0 12.5 %all-to-all-start = ((bf16[20,20,128]{2,1,0:T(8,128)(2,1)}), bf16[20,20,128]{2,1,0:T(8,128)(2,1)S(1)}, u32[]{:S(2)}, u32[]{:S(2)}) async-start(bf16[20,20,128]{2,1,0:T(8,128)(2,1)} %param.13), calls=%async_computation | async-start | bytes 245760 | tf_op jit(solution)/shard_map/all_to_all | solution.py:60
  6.5 0.7 copy-start.3
  7.2 0.7 copy-start.4
  7.9 0.7 copy-start.7
  13.2 0.7 copy-start.5
  14.0 31.2 %copy-start.1 = (bf16[2,128,512]{2,1,0:T(8,128)(2,1)S(1)}, bf16[2,128,512]{2,1,0:T(8,128)(2,1)}, u32[]{:S(2)}) copy-start(bf16[2,128,512]{2,1,0:T(8,128)(2,1)} %param.16) | copy-start | bytes 786436
  49.0 0.8 copy-start.2
  50.7 9.3 %all-to-all-start.1 = ((bf16[5,80,128]{2,0,1:T(8,128)(2,1)}), bf16[5,80,128]{2,0,1:T(8,128)(2,1)S(1)}, u32[]{:S(2)}, u32[]{:S(2)}) async-start(bf16[5,80,128]{2,0,1:T(8,128)(2,1)} %copy.97), calls=%async_computation.1 | async-start | bytes 327680 | tf_op jit(solution)/shard_map/all_to_all | solution.py:71
  60.7 0.9 copy-start.6
  63.4 23.1 %all-to-all-start.2 = ((bf16[20,20,128]{2,1,0:T(8,128)(2,1)}), bf16[20,20,128]{2,1,0:T(8,128)(2,1)S(1)}, u32[]{:S(2)}, u32[]{:S(2)}) async-start(bf16[20,20,128]{2,1,0:T(8,128)(2,1)} %copy.103), calls=%async_computation.2 | async-start | bytes 245760 | tf_op jit(solution)/shard_map/all_to_all | solution.py:79
where the time goes:
time: 100 us; the launch traced here: 99.6 us
  blocking collectives  58.1 us (58%)
  starting transfers between devices  13.1 us (13%)
  waiting for transfers between devices  9.75 us (10%)
  local copies, waits for them, and re-layouts  8.6 us (9%)
  matrix products  5.88 us (6%)
  other arithmetic  3.36 us (3%)
    all_gather x1, blocking collectives, per_device(): lax.all_gather(jnp.transpose(start_part, (2, 0, 1)), ('gr', 'gc'), axis=1...  31.1 us
    all_gather x1, blocking collectives, per_device(): lax.all_gather(jnp.transpose(end_part, (2, 1, 0)), 'gc', axis=1, tiled=True)  13.5 us
    all_to_all x1, blocking collectives, per_device(): lax.all_to_all(columns, 'gr', split_axis=1, concat_axis=0, tiled=True)  7.8 us
    all_to_all x1, starting transfers between devices, per_device(): rows = lax.all_to_all(pair, 'gc', split_axis=0, concat_axis=1, tiled=True)  6.48 us
    all_to_all x1, waiting for transfers between devices, per_device(): tile = lax.all_to_all(rows, 'gc', split_axis=1, concat_axis=0, tiled=True)  5.9 us
    all_gather x1, blocking collectives, per_device(): end_full = lax.all_gather(end_part, 'gr', axis=2, tiled=True)  5.66 us
    unnamed x16, local copies, waits for them, and re-layouts  4.15 us
    all_to_all x1, waiting for transfers between devices, per_device(): rows = lax.all_to_all(pair, 'gc', split_axis=0, concat_axis=1, tiled=True)  3.84 us
  transfers between devices with their start and end apart: 3, of which 2 were waited for; matrix products, arithmetic and copies ran while one was open for 1% of the time, Pallas kernels for 0%

commit v1 on v0

v1 whole, which is shorter than its diff:
```python
import functools

import jax
import jax.numpy as jnp
from jax import lax
from jax.experimental import pallas as pl
from jax.experimental.pallas import tpu as pltpu
from jax.sharding import PartitionSpec as P

BF = jnp.bfloat16
F32 = jnp.float32


def layer_norm(values):
    floats = values.astype(F32)
    center = jnp.mean(floats, axis=-1, keepdims=True)
    spread = jnp.mean((floats - center) ** 2, axis=-1, keepdims=True)
    return ((floats - center) * lax.rsqrt(spread + 1e-05)).astype(BF)


def bias_terms(normed, weight, offset, chain_left, chain_right):
    first, second, width = normed.shape
    heads = weight.shape[1]
    terms = jnp.dot(normed.reshape(-1, width), weight, preferred_element_type=F32)
    same = (chain_left[:, None] == chain_right[None, :]).astype(F32)
    return terms.reshape(first, second, heads) + offset[None, None, :] * same[:, :, None]


def attention(rows, normed, in_w, out_w, bias_full, maskadd):
    count, length, width = rows.shape
    heads = bias_full.shape[0]
    head_width = width // heads
    scale = head_width ** (-0.5)
    proj = jnp.dot(normed.reshape(-1, width), in_w, preferred_element_type=F32)
    proj = proj.astype(BF).reshape(count, length, 4 * width)

    def one_row(piece):
        query = piece[:, 0:width].reshape(length, heads, head_width)
        keys = piece[:, width : 2 * width].reshape(length, heads, head_width)
        vals = piece[:, 2 * width : 3 * width].reshape(length, heads, head_width)
        gate = piece[:, 3 * width :].astype(F32)
        scores = jnp.einsum("jhd,khd->hjk", query, keys, preferred_element_type=F32) * scale
        scores = scores + bias_full + maskadd[None, None, :]
        probs = jax.nn.softmax(scores, axis=-1).astype(BF)
        mixed = jnp.einsum("hjk,khd->jhd", probs, vals, preferred_element_type=F32)
        return (jax.nn.sigmoid(gate) * mixed.reshape(length, width)).astype(BF)

    gated = lax.map(one_row, proj)
    update = jnp.dot(gated.reshape(-1, width), out_w, preferred_element_type=F32)
    return (rows.astype(F32) + update.reshape(rows.shape)).astype(BF)


def transition(rows, trans_up, trans_down):
    width = rows.shape[-1]
    normed = layer_norm(rows).reshape(-1, width)
    hidden = jax.nn.relu(jnp.dot(normed, trans_up, preferred_element_type=F32)).astype(BF)
    update = jnp.dot(hidden, trans_down, preferred_element_type=F32)
    return (rows.astype(F32) + update.reshape(rows.shape)).astype(BF)


def plain_device(
    pair, mask, chain_ids, attn_in, attn_out, bias_weight, chain_bias, trans_up, trans_down
):
    across = lax.axis_size("gc")
    rows = lax.all_to_all(pair, "gc", split_axis=0, concat_axis=1, tiled=True)
    count = rows.shape[0]
    first_row = (lax.axis_index("gr") * across + lax.axis_index("gc")) * count
    maskadd = jnp.where(mask > 0, 0.0, -1000000000.0).astype(F32)
    own_chain = lax.dynamic_slice_in_dim(chain_ids, first_row, count)
    normed = layer_norm(rows)
    start_part = bias_terms(normed, bias_weight[0], chain_bias[0], own_chain, chain_ids)
    start_full = lax.all_gather(
        jnp.transpose(start_part, (2, 0, 1)), ("gr", "gc"), axis=1, tiled=True
    )
    rows = attention(rows, normed, attn_in[0], attn_out[0], start_full, maskadd)
    tile = lax.all_to_all(rows, "gc", split_axis=1, concat_axis=0, tiled=True)
    tile = transition(tile, trans_up, trans_down)
    tile_rows, tile_cols = (tile.shape[0], tile.shape[1])
    chain_rows = lax.dynamic_slice_in_dim(chain_ids, lax.axis_index("gr") * tile_rows, tile_rows)
    chain_cols = lax.dynamic_slice_in_dim(chain_ids, lax.axis_index("gc") * tile_cols, tile_cols)
    end_part = bias_terms(layer_norm(tile), bias_weight[1], chain_bias[1], chain_rows, chain_cols)
    end_part = lax.all_gather(jnp.transpose(end_part, (2, 1, 0)), "gc", axis=1, tiled=True)
    end_full = lax.all_gather(end_part, "gr", axis=2, tiled=True)
    columns = lax.all_to_all(
        jnp.transpose(tile, (1, 0, 2)), "gr", split_axis=0, concat_axis=1, tiled=True
    )
    columns = attention(columns, layer_norm(columns), attn_in[1], attn_out[1], end_full, maskadd)
    returned = lax.all_to_all(columns, "gr", split_axis=1, concat_axis=0, tiled=True)
    return jnp.transpose(returned, (1, 0, 2))


def norm32(x):
    center = jnp.mean(x, axis=-1, keepdims=True)
    off = x - center
    spread = jnp.mean(off * off, axis=-1, keepdims=True)
    return (off * lax.rsqrt(spread + 1e-05)).astype(BF)


def tile_bias(normed, wrep, left, right, chain_w, span):
    count, _, width = normed.shape
    lanes = wrep.shape[1]
    place = lax.broadcasted_iota(jnp.int32, (width, lanes), 1) % span
    zero = jnp.zeros((width, lanes), BF)
    spread = jnp.concatenate([jnp.where(place == j, wrep, zero) for j in range(count)], axis=0)
    tokens = jnp.concatenate([normed[j] for j in range(count)], axis=1)
    terms = jnp.dot(tokens, spread, preferred_element_type=F32)
    return terms + jnp.where(left == right, chain_w, 0.0)


def first_bias_kernel(span, x_ref, wrep_ref, left_ref, right_ref, chain_ref, o_ref, pad):
    nb, nt, _ = x_ref.shape
    pad[...] = jnp.zeros_like(pad)
    pad[:, 0:nt, :] = x_ref[...].astype(F32)
    terms = tile_bias(
        norm32(pad[...]), wrep_ref[...], left_ref[...], right_ref[...], chain_ref[...], span
    )
    o_ref[...] = terms[0:nt]


def attend(spin, heads, span, chunks, bias_refs, mask_ref, in_ref, out_ref, own, gather, table):
    nb, nt, width = chunks[0].shape
    pieces = len(chunks)
    length = pieces * nt
    scale = (width // heads) ** (-0.5)
    own[...] = jnp.zeros_like(own)
    own[:, 0:nt, :] = chunks[0][...].astype(F32)
    for k in range(pieces):
        gather[:, k * nt : (k + 1) * nt, :] = chunks[k][...].astype(F32)
    for slot in range(pieces):
        for k in range(pieces):

            @pl.when(spin == (slot ^ k))
            def _():
                table[k * nt : (k + 1) * nt, :] = bias_refs[slot][...]

    weights = in_ref[...]
    mine = norm32(own[...].reshape(nb * span, width))
    w_query = jnp.concatenate([weights[:, 0:width], weights[:, 3 * width :]], axis=1)
    ask = jnp.dot(mine, w_query, preferred_element_type=F32).astype(BF)
    query, gate = ask[:, 0:width], ask[:, width:].astype(F32)
    everyone = norm32(gather[...].reshape(nb * length, width))
    both = jnp.dot(
        everyone, weights[:, width : 3 * width], preferred_element_type=F32
    ).astype(BF)
    keys, vals = both[:, 0:width], both[:, width:]
    head_of = lax.broadcasted_iota(jnp.int32, (span, width), 1) // (width // heads)
    bias = table[...]
    away = mask_ref[...]
    mixed = []
    for b in range(nb):
        q = query[b * span : (b + 1) * span]
        wide = jnp.concatenate(
            [jnp.where(head_of == h, q, jnp.zeros_like(q)) for h in range(heads)], axis=0
        )
        k = keys[b * length : (b + 1) * length]
        v = vals[b * length : (b + 1) * length]
        s = lax.dot_general(k, wide, (((1,), (1,)), ((), ())), preferred_element_type=F32)
        s = s * scale + bias + away
        top = jnp.max(s, axis=0, keepdims=True)
        e = jnp.exp(s - top)
        p = (e * (1.0 / jnp.sum(e, axis=0, keepdims=True))).astype(BF)
        o = lax.dot_general(p, v, (((0,), (0,)), ((), ())), preferred_element_type=F32)
        got = jnp.zeros((span, width), F32)
        for h in range(heads):
            got = jnp.where(head_of == h, o[h * span : (h + 1) * span], got)
        mixed.append(got)
    mixed = jnp.concatenate(mixed, axis=0)
    gated = (jax.nn.sigmoid(gate) * mixed).astype(BF)
    update = jnp.dot(gated, out_ref[...], preferred_element_type=F32)
    return (own[...].reshape(nb * span, width) + update).astype(BF).astype(F32)


def first_kernel(heads, span, pieces, *refs):
    spin_ref = refs[0]
    chunks = refs[1 : 1 + pieces]
    bias_refs = refs[1 + pieces : 1 + 2 * pieces]
    (
        mask_ref, in_ref, out_ref, up_ref, down_ref, wrep_ref, left_ref, right_ref, chain_ref,
        tile_ref, bias_ref, own, gather, table, flip,
    ) = refs[1 + 2 * pieces :]
    nb, nt, width = chunks[0].shape
    first = attend(
        spin_ref[0], heads, span, chunks, bias_refs, mask_ref, in_ref, out_ref, own, gather, table
    )
    hidden = jnp.dot(norm32(first), up_ref[...], preferred_element_type=F32)
    hidden = jnp.maximum(hidden, 0.0).astype(BF)
    update = jnp.dot(hidden, down_ref[...], preferred_element_type=F32)
    second = (first + update).astype(BF).astype(F32)
    flip[...] = jnp.zeros_like(flip)
    for b in range(nb):
        flip[:, b, :] = second[b * span : b * span + nt]
    turned = flip[...]
    tile_ref[...] = turned[:, 0:nb].astype(BF)
    terms = tile_bias(
        norm32(turned), wrep_ref[...], left_ref[...], right_ref[...], chain_ref[...], span
    )
    bias_ref[...] = terms[0:nb]


def second_kernel(heads, span, pieces, *refs):
    spin_ref = refs[0]
    chunks = refs[1 : 1 + pieces]
    bias_refs = refs[1 + pieces : 1 + 2 * pieces]
    mask_ref, in_ref, out_ref, tile_ref, own, gather, table, flip = refs[1 + 2 * pieces :]
    nb, nt, width = chunks[0].shape
    last = attend(
        spin_ref[0], heads, span, chunks, bias_refs, mask_ref, in_ref, out_ref, own, gather, table
    )
    for b in range(nb):
        flip[:, b, :] = last[b * span : b * span + nt]
    tile_ref[...] = flip[...].astype(BF)


VMEM = pl.BlockSpec(memory_space=pltpu.VMEM)
SMEM = pl.BlockSpec(memory_space=pltpu.SMEM)


def layer_of(array, index):
    rest = array.shape[1:]
    return pl.BlockSpec((None, *rest), lambda i: (index,) + (0,) * len(rest))


def whole(array):
    return pl.BlockSpec(array.shape, lambda i: (0,) * array.ndim)


def swap(array, axis, k):
    size = lax.axis_size(axis)
    return lax.ppermute(array, axis, [(i, i ^ k) for i in range(size)])


def fast_device(
    span, pair, mask, chain_ids, attn_in, attn_out, bias_weight, chain_bias, trans_up, trans_down
):
    side = lax.axis_size("gc")
    nr, nc, width = pair.shape
    heads = bias_weight.shape[2]
    lanes = heads * span
    gr, gc = lax.axis_index("gr"), lax.axis_index("gc")
    spin = (gr ^ gc).astype(jnp.int32).reshape(1)
    cells = [(r, c) for r in range(side) for c in range(side)]
    params = pltpu.CompilerParams(dimension_semantics=("arbitrary",))

    chunks = [pair] + [swap(pair, "gc", k) for k in range(1, side)]

    wrep = jnp.repeat(bias_weight, span, axis=2)
    chain_lane = jnp.repeat(chain_bias, span, axis=1)[:, None, :]
    rows_chain = lax.dynamic_slice_in_dim(chain_ids, gr * nr, nr)
    cols_chain = lax.dynamic_slice_in_dim(chain_ids, gc * nc, nc)

    def as_query(ids):
        return jnp.tile(jnp.pad(ids, (0, span - ids.shape[0])), heads)[None, :]

    def as_key(ids):
        return jnp.broadcast_to(jnp.pad(ids, (0, span - ids.shape[0]))[:, None], (span, lanes))

    maskadd = jnp.where(mask > 0, 0.0, -1000000000.0).astype(F32)

    def mask_for(start, count):
        part = [lax.dynamic_slice_in_dim(maskadd, (start ^ k) * count, count) for k in range(side)]
        return jnp.broadcast_to(jnp.concatenate(part)[:, None], (side * count, lanes))

    piece = pl.pallas_call(
        functools.partial(first_bias_kernel, span),
        out_shape=jax.ShapeDtypeStruct((nc, lanes), F32),
        grid=(1,),
        in_specs=[whole(pair), layer_of(wrep, 0)]
        + [pl.BlockSpec((1, lanes), lambda i: (0, 0)), pl.BlockSpec((span, lanes), lambda i: (0, 0))]
        + [layer_of(chain_lane, 0)],
        out_specs=pl.BlockSpec((nc, lanes), lambda i: (0, 0)),
        scratch_shapes=[pltpu.VMEM((nr, span, width), F32)],
        compiler_params=params,
    )(pair, wrep, as_query(rows_chain), as_key(cols_chain), chain_lane)
    pieces = [
        lax.ppermute(piece, ("gr", "gc"), [(r * side + c, (c ^ k) * side + r) for r, c in cells])
        for k in range(side)
    ]
    args = [spin, *chunks, *pieces, mask_for(gc, nc), attn_in, attn_out, trans_up, trans_down, wrep]
    args += [as_query(cols_chain), as_key(rows_chain), chain_lane]
    specs = [SMEM] + [whole(a) for a in args[1 : 2 + 2 * side]]
    specs += [layer_of(attn_in, 0), layer_of(attn_out, 0), whole(trans_up), whole(trans_down)]
    specs += [layer_of(wrep, 1), whole(args[-3]), whole(args[-2]), layer_of(chain_lane, 1)]
    tile, piece = pl.pallas_call(
        functools.partial(first_kernel, heads, span, side),
        out_shape=(
            jax.ShapeDtypeStruct((nc, nr, width), BF),
            jax.ShapeDtypeStruct((nr, lanes), F32),
        ),
        grid=(1,),
        in_specs=specs,
        out_specs=(
            pl.BlockSpec((nc, nr, width), lambda i: (0, 0, 0)),
            pl.BlockSpec((nr, lanes), lambda i: (0, 0)),
        ),
        scratch_shapes=[
            pltpu.VMEM((nr, span, width), F32),
            pltpu.VMEM((nr, side * nc, width), F32),
            pltpu.VMEM((side * nc, lanes), F32),
            pltpu.VMEM((nc, span, width), F32),
        ],
        compiler_params=params,
    )(*args)

    chunks = [tile, swap(tile, "gr", 1)]
    for k in range(2, side, 2):
        far = swap(tile, "gr", k)
        chunks += [far, swap(far, "gr", 1)]
    pieces = [
        lax.ppermute(piece, ("gr", "gc"), [(r * side + c, c * side + (r ^ k)) for r, c in cells])
        for k in range(side)
    ]
    args = [spin, *chunks, *pieces, mask_for(gr, nr), attn_in, attn_out]
    specs = [SMEM] + [whole(a) for a in args[1 : 2 + 2 * side]]
    specs += [layer_of(attn_in, 1), layer_of(attn_out, 1)]
    return pl.pallas_call(
        functools.partial(second_kernel, heads, span, side),
        out_shape=jax.ShapeDtypeStruct((nr, nc, width), BF),
        grid=(1,),
        in_specs=specs,
        out_specs=pl.BlockSpec((nr, nc, width), lambda i: (0, 0, 0)),
        scratch_shapes=[
            pltpu.VMEM((nc, span, width), F32),
            pltpu.VMEM((nc, side * nr, width), F32),
            pltpu.VMEM((side * nr, lanes), F32),
            pltpu.VMEM((nr, nc, width), F32),
        ],
        compiler_params=params,
    )(*args)


def solution(mesh):
    shape = dict(mesh.shape)
    in_specs = (P(("jobs", "gr"), "gc", None), P("jobs"), P("jobs"), P(), P(), P(), P(), P(), P())
    out_specs = P(("jobs", "gr"), "gc", None)
    side = shape["gc"]
    square = shape["gr"] == side and side & (side - 1) == 0

    def per_device(*args):
        nr, nc, width = args[0].shape
        heads = args[5].shape[2]
        span = 128 // heads
        fits = nr == nc and nr <= span and (side * nr) % 16 == 0 and width == 128
        if square and fits:
            return fast_device(span, *args)
        return plain_device(*args)

    return jax.shard_map(
        per_device, mesh=mesh, in_specs=in_specs, out_specs=out_specs, check_vma=False
    )
```

time: 100 us -> 58.9 us (0.59)
  blocking collectives: 58.1 us -> 0 us
  Pallas kernels: 0 us -> 16.1 us
  starting transfers between devices: 13.1 us -> 25 us
  matrix products: 5.88 us -> 0 us
  other arithmetic: 3.36 us -> 0.16 us
  local copies, waits for them, and re-layouts: 8.6 us -> 7.06 us
    all_gather x3 -> x0, blocking collectives: 50.3 us -> none  [the longest x1 31.1 us: per_device(): lax.all_gather(jnp.transpose(start_part, (2, 0, 1)), ('gr', 'gc'), axis=1...]
    ppermute x0 -> x14, starting transfers between devices: none -> 25 us  [the longest x6 10 us: swap(): return lax.ppermute(array, axis, [(i, i ^ k) for i in range(size)])]
    pallas_call x0 -> x3, Pallas kernels: none -> 16.1 us  [the longest x1 7.61 us: fast_device(): pl.pallas_call(functools.partial(first_kernel, heads, span, side), out_sh...]
    all_to_all x3 -> x0, starting transfers between devices: 13.1 us -> none  [the longest x1 6.48 us: per_device(): rows = lax.all_to_all(pair, 'gc', split_axis=0, concat_axis=1, tiled=True)]
    ppermute x0 -> x14, waiting for transfers between devices: none -> 10.1 us  [the longest x6 9.67 us: swap(): return lax.ppermute(array, axis, [(i, i ^ k) for i in range(size)])]
    all_to_all x3 -> x0, waiting for transfers between devices: 9.75 us -> none  [the longest x1 5.9 us: per_device(): tile = lax.all_to_all(rows, 'gc', split_axis=1, concat_axis=0, tiled=True)]
    all_to_all x1 -> x0, blocking collectives: 7.8 us -> none  [per_device(): lax.all_to_all(columns, 'gr', split_axis=1, concat_axis=0, tiled=True)]
    dot_general x27 -> x0, matrix products: 5.88 us -> none  [the longest x10 2.2 us: one_row(): jnp.einsum('jhd,khd->hjk', query, keys, preferred_element_type=jnp.float32)]
  transfers between devices with their start and end apart: 3 -> 14, of which waited for: 2 -> 4; matrix products, arithmetic and copies ran while one was open for 1% -> 1% of each run, Pallas kernels for 0% -> 0%
where the time goes in v1:
time: 58.9 us; the launch traced here: 58.6 us
  starting transfers between devices  25 us (42%)
  Pallas kernels  16.1 us (27%)
  waiting for transfers between devices  10.1 us (17%)
  local copies, waits for them, and re-layouts  7.06 us (12%)
    ppermute x6, starting transfers between devices, swap(): return lax.ppermute(array, axis, [(i, i ^ k) for i in range(size)])  10 us
    ppermute x6, waiting for transfers between devices, swap(): return lax.ppermute(array, axis, [(i, i ^ k) for i in range(size)])  9.67 us
    ppermute x4, starting transfers between devices, fast_device(): lax.ppermute(piece, ('gr', 'gc'), [(r * side + c, (c ^ k) * side + r) for...  8.65 us
    pallas_call x1, Pallas kernels, fast_device(): pl.pallas_call(functools.partial(first_kernel, heads, span, side), out_sh...  7.61 us
    pallas_call x1, Pallas kernels, fast_device(): pl.pallas_call(functools.partial(second_kernel, heads, span, side), out_s...  6.53 us
    ppermute x4, starting transfers between devices, fast_device(): lax.ppermute(piece, ('gr', 'gc'), [(r * side + c, c * side + (r ^ k)) for...  6.33 us
    pallas_call x1, Pallas kernels, fast_device(): pl.pallas_call(functools.partial(first_bias_kernel, span), out_shape=jax....  1.98 us
    unnamed x38, local copies, waits for them, and re-layouts  1.45 us
  transfers between devices with their start and end apart: 14, of which 4 were waited for; matrix products, arithmetic and copies ran while one was open for 1% of the time, Pallas kernels for 0%

profile of v1, /device:TPU:0, one launch (start us, length us, event | category | flops | bytes accessed | tf_op | source)
XLA Modules:
  0.0 58.6 jit_solution(7718422930194389575)
XLA Ops:
  0.0 0.7 %copy-done.16 = s32[80]{0:T(128)S(1)} copy-done((s32[80]{0:T(128)S(1)}, s32[80]{0:T(128)}, u32[]{:S(2)}) %copy-start.16) | copy-done | bytes 344
  0.7 0.1 fusion.1
  0.8 0.6 %broadcast_in_dim_tile.6.left_ref = s32[1,128]{1,0:T(1,128)} reshape(s32[4,32]{1,0:T(4,128)S(1)} %tile.4) | data formatting | bytes 1024 | tf_op jit(solution)/shard_map/broadcast_in_dim;tile | solution.py:252
  1.4 0.1 copy-done.15
  1.4 0.0 copy-start.17
  1.4 0.7 %copy.11.wrep_ref.refs_14_ = bf16[2,128,128]{2,1,0:T(8,128)(2,1)} copy(bf16[2,128,128]{1,2,0:T(8,128)(2,1)S(1)} %bitcast.2) | data formatting | bytes 131072 | tf_op jit(solution)/shard_map/reshape | solution.py:246
  2.2 0.1 broadcast_in_dim.40
  2.3 0.7 %broadcast_in_dim_reshape.3.chain_ref.refs_17_ = f32[2,1,128]{2,1,0:T(1,128)} reshape(f32[2,4,32]{2,1,0:T(4,128)S(1)} %broadcast_in_dim.40) | data formatting | bytes 2048 | tf_op jit(solution)/shard_map/broadcast_in_dim;reshape | solution.py:247
  2.9 0.7 %broadcast_in_dim.21.right_ref = s32[32,128]{1,0:T(8,128)} broadcast(s32[32]{0:T(128)S(1)} %pad.10), dimensions={0} | broadcast | bytes 16512 | tf_op jit(solution)/shard_map/broadcast_in_dim | solution.py:255
  3.6 2.0 %shard_map.91 = f32[20,128]{1,0:T(8,128)} custom-call(bf16[20,20,128]{2,1,0:T(8,128)(2,1)} %refs_1_.1, bf16[2,128,128]{2,1,0:T(8,128)(2,1)} %copy.11.wrep_ref.refs_14_, s32[1,128]{1,0:T(1,128)} %broadcast_in_dim_tile.6.left_ref, s32[32,128]{1,0:T(8,128)} %broadcast_in_dim.21.right_ref, f32[2,1,128]{2,1,0:T(1,128)} %broadcast_in_dim_reshape.3.chain_ref.refs_17_), custom_call_target="tpu_custom_call" | custom-call | tf_op jit(solution)/shard_map/pallas_call | solution.py:263
  5.6 1.4 %collective-permute-start.3 = (f32[20,128]{1,0:T(8,128)}, f32[20,128]{1,0:T(8,128)S(1)}, u32[]{:S(2)}, u32[]{:S(2)}) collective-permute-start(f32[20,128]{1,0:T(8,128)} %shard_map.91), channel_id=1, source_target_pairs={{0,0},{1,4},{2,8},{3,12},{4,1},{5,5},{6,9},{7,13},{8,2},{9,6},{10,... | collective-permute-start | bytes 30728 | tf_op jit(solution)/shard_map/ppermute | solution.py:275
  6.9 3.8 %collective-permute-start.4 = (f32[20,128]{1,0:T(8,128)}, f32[20,128]{1,0:T(8,128)S(1)}, u32[]{:S(2)}, u32[]{:S(2)}) collective-permute-start(f32[20,128]{1,0:T(8,128)} %shard_map.91), channel_id=1, source_target_pairs={{0,4},{1,0},{2,12},{3,8},{4,5},{5,1},{6,13},{7,9},{8,6},{9,2},{10,... | collective-permute-start | bytes 30728 | tf_op jit(solution)/shard_map/ppermute | solution.py:275
  10.7 3.5 %collective-permute-start.5 = (f32[20,128]{1,0:T(8,128)}, f32[20,128]{1,0:T(8,128)S(1)}, u32[]{:S(2)}, u32[]{:S(2)}) collective-permute-start(f32[20,128]{1,0:T(8,128)} %shard_map.91), channel_id=1, source_target_pairs={{0,8},{1,12},{2,0},{3,4},{4,9},{5,13},{6,1},{7,5},{8,10},{9,14},{1... | collective-permute-start | bytes 30728 | tf_op jit(solution)/shard_map/ppermute | solution.py:275
  14.2 0.1 collective-permute-start.6
  14.2 2.0 %collective-permute-start = (bf16[20,20,128]{2,1,0:T(8,128)(2,1)S(1)}, bf16[20,20,128]{2,1,0:T(8,128)(2,1)S(1)}, u32[]{:S(2)}, u32[]{:S(2)}) collective-permute-start(bf16[20,20,128]{2,1,0:T(8,128)(2,1)S(1)} %copy-done), channel_id=1, source_target_pairs={{0,1},{1,0},{2,3},{3,2},{4,5},{5,4},{6,7},{7,6},{8,9},{9,8},{10,11... | collective-permute-start | bytes 307208 | tf_op jit(solution)/shard_map/ppermute | solution.py:229
  16.3 0.7 %copy-done.18 = s32[80]{0:T(128)S(1)} copy-done((s32[80]{0:T(128)S(1)}, s32[80]{0:T(128)}, u32[]{:S(2)}) %copy-start.18) | copy-done | bytes 344
  16.9 0.1 fusion
  17.0 0.0 collective-permute-done.3.refs_5_
  17.0 2.4 %collective-permute-start.1 = (bf16[20,20,128]{2,1,0:T(8,128)(2,1)S(1)}, bf16[20,20,128]{2,1,0:T(8,128)(2,1)S(1)}, u32[]{:S(2)}, u32[]{:S(2)}) collective-permute-start(bf16[20,20,128]{2,1,0:T(8,128)(2,1)S(1)} %copy-done), channel_id=1, source_target_pairs={{0,2},{1,3},{2,0},{3,1},{4,6},{5,7},{6,4},{7,5},{8,10},{9,11},{10,... | collective-permute-start | bytes 307208 | tf_op jit(solution)/shard_map/ppermute | solution.py:229
  19.4 0.0 collective-permute-done.4.refs_6_
  19.4 0.1 collective-permute-start.2
  19.5 0.1 pad_maximum_fusion
  19.5 0.6 %broadcast_in_dim_tile.7.refs_15_ = s32[1,128]{1,0:T(1,128)} reshape(s32[4,32]{1,0:T(4,128)S(1)} %tile.5) | data formatting | bytes 1024 | tf_op jit(solution)/shard_map/broadcast_in_dim;tile | solution.py:252
  20.2 0.0 collective-permute-done.5.refs_7_
  20.2 0.0 collective-permute-done.6.refs_8_
  20.2 2.1 %collective-permute-done.refs_2_ = bf16[20,20,128]{2,1,0:T(8,128)(2,1)S(1)} collective-permute-done((bf16[20,20,128]{2,1,0:T(8,128)(2,1)S(1)}, bf16[20,20,128]{2,1,0:T(8,128)(2,1)S(1)}, u32[]{:S(2)}, u32[]{:S(2)}) %collective-permute-start) | collective-permute-done | bytes 102432 | tf_op jit(solution)/shard_map/ppermute | solution.py:229
  22.3 7.1 %collective-permute-done.1.refs_3_ = bf16[20,20,128]{2,1,0:T(8,128)(2,1)S(1)} collective-permute-done((bf16[20,20,128]{2,1,0:T(8,128)(2,1)S(1)}, bf16[20,20,128]{2,1,0:T(8,128)(2,1)S(1)}, u32[]{:S(2)}, u32[]{:S(2)}) %collective-permute-start.1) | collective-permute-done | bytes 102432 | tf_op jit(solution)/shard_map/ppermute | solution.py:229
  29.4 0.0 collective-permute-done.2.refs_4_
  29.4 0.7 %broadcast_in_dim.43.refs_9_ = f32[80,128]{1,0:T(8,128)} broadcast(f32[80]{0:T(128)S(1)} %pad_maximum_fusion), dimensions={0} | broadcast | bytes 41280 | tf_op jit(solution)/shard_map/broadcast_in_dim | solution.py:261
  30.1 0.7 %broadcast_in_dim.44.refs_16_ = s32[32,128]{1,0:T(8,128)} broadcast(s32[32]{0:T(128)S(1)} %pad.9), dimensions={0} | broadcast | bytes 16512 | tf_op jit(solution)/shard_map/broadcast_in_dim | solution.py:255
  30.8 7.6 %shard_map.92 = (bf16[20,20,128]{2,1,0:T(8,128)(2,1)}, f32[20,128]{1,0:T(8,128)}) custom-call(s32[1]{0:T(128)} %bitcast.refs_0_, bf16[20,20,128]{2,1,0:T(8,128)(2,1)} %refs_1_.1, bf16[20,20,128]{2,1,0:T(8,128)(2,1)} %copy-done.1, bf16[20,20,128]{2,1,0:T(8,128)(2,1)} %copy-done.4, bf16[20,20,128]{2,1,0:T(8,128)(2,1)} %copy-done.5, f32[20,128]{1,0:T(8,128)} %copy-done.7, ...), custom_call_target="tpu_custom_call" | custom-call | tf_op jit(solution)/shard_map/pallas_call | solution.py:283
  38.4 1.9 %collective-permute-start.8 = (bf16[20,20,128]{2,1,0:T(8,128)(2,1)}, bf16[20,20,128]{2,1,0:T(8,128)(2,1)S(1)}, u32[]{:S(2)}, u32[]{:S(2)}) collective-permute-start(bf16[20,20,128]{2,1,0:T(8,128)(2,1)} %get-tuple-element.7.refs_1_), channel_id=1, source_target_pairs={{0,8},{4,12},{8,0},{12,4},{1,9},{5,13},{9,1},{13,5},{2,10},{6,14},... | collective-permute-start | bytes 307208 | tf_op jit(solution)/shard_map/ppermute | solution.py:229
  40.3 1.4 %collective-permute-start.10 = (f32[20,128]{1,0:T(8,128)}, f32[20,128]{1,0:T(8,128)S(1)}, u32[]{:S(2)}, u32[]{:S(2)}) collective-permute-start(f32[20,128]{1,0:T(8,128)} %get-tuple-element.8), channel_id=1, source_target_pairs={{0,0},{1,4},{2,8},{3,12},{4,1},{5,5},{6,9},{7,13},{8,2},{9,6},{10,... | collective-permute-start | bytes 30728 | tf_op jit(solution)/shard_map/ppermute | solution.py:309
  41.6 2.6 %collective-permute-start.7 = (bf16[20,20,128]{2,1,0:T(8,128)(2,1)}, bf16[20,20,128]{2,1,0:T(8,128)(2,1)S(1)}, u32[]{:S(2)}, u32[]{:S(2)}) collective-permute-start(bf16[20,20,128]{2,1,0:T(8,128)(2,1)} %get-tuple-element.7.refs_1_), channel_id=1, source_target_pairs={{0,4},{4,0},{8,12},{12,8},{1,5},{5,1},{9,13},{13,9},{2,6},{6,2},{1... | collective-permute-start | bytes 307208 | tf_op jit(solution)/shard_map/ppermute | solution.py:229
  44.2 0.0 collective-permute-start.11
  44.2 2.3 %collective-permute-start.12 = (f32[20,128]{1,0:T(8,128)}, f32[20,128]{1,0:T(8,128)S(1)}, u32[]{:S(2)}, u32[]{:S(2)}) collective-permute-start(f32[20,128]{1,0:T(8,128)} %get-tuple-element.8), channel_id=1, source_target_pairs={{0,2},{1,6},{2,10},{3,14},{4,3},{5,7},{6,11},{7,15},{8,0},{9,4},{1... | collective-permute-start | bytes 30728 | tf_op jit(solution)/shard_map/ppermute | solution.py:309
  46.6 0.0 collective-permute-done.10.refs_5_
  46.6 2.6 %collective-permute-start.13 = (f32[20,128]{1,0:T(8,128)}, f32[20,128]{1,0:T(8,128)S(1)}, u32[]{:S(2)}, u32[]{:S(2)}) collective-permute-start(f32[20,128]{1,0:T(8,128)} %get-tuple-element.8), channel_id=1, source_target_pairs={{0,3},{1,7},{2,11},{3,15},{4,2},{5,6},{6,10},{7,14},{8,1},{9,5},{1... | collective-permute-start | bytes 30728 | tf_op jit(solution)/shard_map/ppermute | solution.py:309
  49.2 0.0 collective-permute-done.8.refs_3_
  49.2 1.1 %collective-permute-start.9 = (bf16[20,20,128]{2,1,0:T(8,128)(2,1)S(1)}, bf16[20,20,128]{2,1,0:T(8,128)(2,1)S(1)}, u32[]{:S(2)}, u32[]{:S(2)}) collective-permute-start(bf16[20,20,128]{2,1,0:T(8,128)(2,1)S(1)} %collective-permute-done.8.refs_3_), channel_id=1, source_target_pairs={{0,4},{4,0},{8,12},{12,8},{1,5},{5,1},{9,13},{13,9},{2,6},{6,2},{1... | collective-permute-start | bytes 307208 | tf_op jit(solution)/shard_map/ppermute | solution.py:229
  50.3 0.1 pad_maximum_fusion.1
  50.4 0.0 collective-permute-done.11.refs_6_
  50.4 0.0 collective-permute-done.12.refs_7_
  50.4 0.4 collective-permute-done.13.refs_8_
  50.8 0.0 collective-permute-done.7.refs_2_
  50.8 0.4 collective-permute-done.9.refs_4_
  51.3 0.7 %broadcast_in_dim.45.refs_9_ = f32[80,128]{1,0:T(8,128)} broadcast(f32[80]{0:T(128)S(1)} %pad_maximum_fusion.1), dimensions={0} | broadcast | bytes 41280 | tf_op jit(solution)/shard_map/broadcast_in_dim | solution.py:261
  52.0 6.5 %shard_map.93 = bf16[20,20,128]{2,1,0:T(8,128)(2,1)} custom-call(s32[1]{0:T(128)} %bitcast.refs_0_, bf16[20,20,128]{2,1,0:T(8,128)(2,1)} %get-tuple-element.7.refs_1_, bf16[20,20,128]{2,1,0:T(8,128)(2,1)} %copy-done.3, bf16[20,20,128]{2,1,0:T(8,128)(2,1)} %copy-done.2, bf16[20,20,128]{2,1,0:T(8,128)(2,1)} %copy-done.6, f32[20,128]{1,0:T(8,128)} %copy-done.11, ...), custom_call_target="tpu_custom_call" | custom-call | tf_op jit(solution)/shard_map/pallas_call | solution.py:315
  (40 shorter events, 0.1 us)
Async XLA Ops:
  0.0 0.7 %copy-start.16 = (s32[80]{0:T(128)S(1)}, s32[80]{0:T(128)}, u32[]{:S(2)}) copy-start(s32[80]{0:T(128)} %param.11) | copy-start | bytes 964
  0.7 0.7 %copy-start.15 = (bf16[2,128,4]{1,2,0:T(4,128)(2,1)S(1)}, bf16[2,128,4]{1,2,0:T(4,128)(2,1)}, u32[]{:S(2)}) copy-start(bf16[2,128,4]{1,2,0:T(4,128)(2,1)} %param.14) | copy-start | bytes 6148
  1.4 0.8 %copy-start.17 = (f32[2,4]{1,0:T(2,128)S(1)}, f32[2,4]{1,0:T(2,128)}, u32[]{:S(2)}) copy-start(f32[2,4]{1,0:T(2,128)} %param.15) | copy-start | bytes 100
  2.2 12.0 %copy-start = (bf16[20,20,128]{2,1,0:T(8,128)(2,1)S(1)}, bf16[20,20,128]{2,1,0:T(8,128)(2,1)}, u32[]{:S(2)}) copy-start(bf16[20,20,128]{2,1,0:T(8,128)(2,1)} %refs_1_.1) | copy-start | bytes 307204
  5.6 11.4 %collective-permute-start.3 = (f32[20,128]{1,0:T(8,128)}, f32[20,128]{1,0:T(8,128)S(1)}, u32[]{:S(2)}, u32[]{:S(2)}) collective-permute-start(f32[20,128]{1,0:T(8,128)} %shard_map.91), channel_id=1, source_target_pairs={{0,0},{1,4},{2,8},{3,12},{4,1},{5,5},{6,9},{7,13},{8,2},{9,6},{10,... | collective-permute-start | bytes 30728 | tf_op jit(solution)/shard_map/ppermute | solution.py:275
  6.9 12.5 %collective-permute-start.4 = (f32[20,128]{1,0:T(8,128)}, f32[20,128]{1,0:T(8,128)S(1)}, u32[]{:S(2)}, u32[]{:S(2)}) collective-permute-start(f32[20,128]{1,0:T(8,128)} %shard_map.91), channel_id=1, source_target_pairs={{0,4},{1,0},{2,12},{3,8},{4,5},{5,1},{6,13},{7,9},{8,6},{9,2},{10,... | collective-permute-start | bytes 30728 | tf_op jit(solution)/shard_map/ppermute | solution.py:275
  10.7 9.5 %collective-permute-start.5 = (f32[20,128]{1,0:T(8,128)}, f32[20,128]{1,0:T(8,128)S(1)}, u32[]{:S(2)}, u32[]{:S(2)}) collective-permute-start(f32[20,128]{1,0:T(8,128)} %shard_map.91), channel_id=1, source_target_pairs={{0,8},{1,12},{2,0},{3,4},{4,9},{5,13},{6,1},{7,5},{8,10},{9,14},{1... | collective-permute-start | bytes 30728 | tf_op jit(solution)/shard_map/ppermute | solution.py:275
  14.2 6.0 %collective-permute-start.6 = (f32[20,128]{1,0:T(8,128)}, f32[20,128]{1,0:T(8,128)S(1)}, u32[]{:S(2)}, u32[]{:S(2)}) collective-permute-start(f32[20,128]{1,0:T(8,128)} %shard_map.91), channel_id=1, source_target_pairs={{0,12},{1,8},{2,4},{3,0},{4,13},{5,9},{6,5},{7,1},{8,14},{9,10},{1... | collective-permute-start | bytes 30728 | tf_op jit(solution)/shard_map/ppermute | solution.py:275
  14.2 8.1 %collective-permute-start = (bf16[20,20,128]{2,1,0:T(8,128)(2,1)S(1)}, bf16[20,20,128]{2,1,0:T(8,128)(2,1)S(1)}, u32[]{:S(2)}, u32[]{:S(2)}) collective-permute-start(bf16[20,20,128]{2,1,0:T(8,128)(2,1)S(1)} %copy-done), channel_id=1, source_target_pairs={{0,1},{1,0},{2,3},{3,2},{4,5},{5,4},{6,7},{7,6},{8,9},{9,8},{10,11... | collective-permute-start | bytes 307208 | tf_op jit(solution)/shard_map/ppermute | solution.py:229
  16.3 0.7 %copy-start.18 = (s32[80]{0:T(128)S(1)}, s32[80]{0:T(128)}, u32[]{:S(2)}) copy-start(s32[80]{0:T(128)} %param.10) | copy-start | bytes 964
  17.0 13.1 %copy-start.7 = (f32[20,128]{1,0:T(8,128)}, f32[20,128]{1,0:T(8,128)S(1)}, u32[]{:S(2)}) copy-start(f32[20,128]{1,0:T(8,128)S(1)} %collective-permute-done.3.refs_5_) | copy-start | bytes 30724
  17.0 12.4 %collective-permute-start.1 = (bf16[20,20,128]{2,1,0:T(8,128)(2,1)S(1)}, bf16[20,20,128]{2,1,0:T(8,128)(2,1)S(1)}, u32[]{:S(2)}, u32[]{:S(2)}) collective-permute-start(bf16[20,20,128]{2,1,0:T(8,128)(2,1)S(1)} %copy-done), channel_id=1, source_target_pairs={{0,2},{1,3},{2,0},{3,1},{4,6},{5,7},{6,4},{7,5},{8,10},{9,11},{10,... | collective-permute-start | bytes 307208 | tf_op jit(solution)/shard_map/ppermute | solution.py:229
  19.4 10.7 %copy-start.8 = (f32[20,128]{1,0:T(8,128)}, f32[20,128]{1,0:T(8,128)S(1)}, u32[]{:S(2)}) copy-start(f32[20,128]{1,0:T(8,128)S(1)} %collective-permute-done.4.refs_6_) | copy-start | bytes 30724
  19.4 10.0 %collective-permute-start.2 = (bf16[20,20,128]{2,1,0:T(8,128)(2,1)S(1)}, bf16[20,20,128]{2,1,0:T(8,128)(2,1)S(1)}, u32[]{:S(2)}, u32[]{:S(2)}) collective-permute-start(bf16[20,20,128]{2,1,0:T(8,128)(2,1)S(1)} %copy-done), channel_id=1, source_target_pairs={{0,3},{1,2},{2,1},{3,0},{4,7},{5,6},{6,5},{7,4},{8,11},{9,10},{10,... | collective-permute-start | bytes 307208 | tf_op jit(solution)/shard_map/ppermute | solution.py:229
  20.2 9.9 %copy-start.9 = (f32[20,128]{1,0:T(8,128)}, f32[20,128]{1,0:T(8,128)S(1)}, u32[]{:S(2)}) copy-start(f32[20,128]{1,0:T(8,128)S(1)} %collective-permute-done.5.refs_7_) | copy-start | bytes 30724
  20.2 9.9 %copy-start.10 = (f32[20,128]{1,0:T(8,128)}, f32[20,128]{1,0:T(8,128)S(1)}, u32[]{:S(2)}) copy-start(f32[20,128]{1,0:T(8,128)S(1)} %collective-permute-done.6.refs_8_) | copy-start | bytes 30724
  22.3 8.5 %copy-start.1 = (bf16[20,20,128]{2,1,0:T(8,128)(2,1)}, bf16[20,20,128]{2,1,0:T(8,128)(2,1)S(1)}, u32[]{:S(2)}) copy-start(bf16[20,20,128]{2,1,0:T(8,128)(2,1)S(1)} %collective-permute-done.refs_2_) | copy-start | bytes 307204
  29.4 1.4 %copy-start.4 = (bf16[20,20,128]{2,1,0:T(8,128)(2,1)}, bf16[20,20,128]{2,1,0:T(8,128)(2,1)S(1)}, u32[]{:S(2)}) copy-start(bf16[20,20,128]{2,1,0:T(8,128)(2,1)S(1)} %collective-permute-done.1.refs_3_) | copy-start | bytes 307204
  29.4 1.4 %copy-start.5 = (bf16[20,20,128]{2,1,0:T(8,128)(2,1)}, bf16[20,20,128]{2,1,0:T(8,128)(2,1)S(1)}, u32[]{:S(2)}) copy-start(bf16[20,20,128]{2,1,0:T(8,128)(2,1)S(1)} %collective-permute-done.2.refs_4_) | copy-start | bytes 307204
  38.4 10.8 %collective-permute-start.8 = (bf16[20,20,128]{2,1,0:T(8,128)(2,1)}, bf16[20,20,128]{2,1,0:T(8,128)(2,1)S(1)}, u32[]{:S(2)}, u32[]{:S(2)}) collective-permute-start(bf16[20,20,128]{2,1,0:T(8,128)(2,1)} %get-tuple-element.7.refs_1_), channel_id=1, source_target_pairs={{0,8},{4,12},{8,0},{12,4},{1,9},{5,13},{9,1},{13,5},{2,10},{6,14},... | collective-permute-start | bytes 307208 | tf_op jit(solution)/shard_map/ppermute | solution.py:229
  40.3 6.3 %collective-permute-start.10 = (f32[20,128]{1,0:T(8,128)}, f32[20,128]{1,0:T(8,128)S(1)}, u32[]{:S(2)}, u32[]{:S(2)}) collective-permute-start(f32[20,128]{1,0:T(8,128)} %get-tuple-element.8), channel_id=1, source_target_pairs={{0,0},{1,4},{2,8},{3,12},{4,1},{5,5},{6,9},{7,13},{8,2},{9,6},{10,... | collective-permute-start | bytes 30728 | tf_op jit(solution)/shard_map/ppermute | solution.py:309
  41.6 9.2 %collective-permute-start.7 = (bf16[20,20,128]{2,1,0:T(8,128)(2,1)}, bf16[20,20,128]{2,1,0:T(8,128)(2,1)S(1)}, u32[]{:S(2)}, u32[]{:S(2)}) collective-permute-start(bf16[20,20,128]{2,1,0:T(8,128)(2,1)} %get-tuple-element.7.refs_1_), channel_id=1, source_target_pairs={{0,4},{4,0},{8,12},{12,8},{1,5},{5,1},{9,13},{13,9},{2,6},{6,2},{1... | collective-permute-start | bytes 307208 | tf_op jit(solution)/shard_map/ppermute | solution.py:229
  44.2 6.2 %collective-permute-start.11 = (f32[20,128]{1,0:T(8,128)}, f32[20,128]{1,0:T(8,128)S(1)}, u32[]{:S(2)}, u32[]{:S(2)}) collective-permute-start(f32[20,128]{1,0:T(8,128)} %get-tuple-element.8), channel_id=1, source_target_pairs={{0,1},{1,5},{2,9},{3,13},{4,0},{5,4},{6,8},{7,12},{8,3},{9,7},{10,... | collective-permute-start | bytes 30728 | tf_op jit(solution)/shard_map/ppermute | solution.py:309
  44.2 6.2 %collective-permute-start.12 = (f32[20,128]{1,0:T(8,128)}, f32[20,128]{1,0:T(8,128)S(1)}, u32[]{:S(2)}, u32[]{:S(2)}) collective-permute-start(f32[20,128]{1,0:T(8,128)} %get-tuple-element.8), channel_id=1, source_target_pairs={{0,2},{1,6},{2,10},{3,14},{4,3},{5,7},{6,11},{7,15},{8,0},{9,4},{1... | collective-permute-start | bytes 30728 | tf_op jit(solution)/shard_map/ppermute | solution.py:309
  46.6 5.4 %copy-start.11 = (f32[20,128]{1,0:T(8,128)}, f32[20,128]{1,0:T(8,128)S(1)}, u32[]{:S(2)}) copy-start(f32[20,128]{1,0:T(8,128)S(1)} %collective-permute-done.10.refs_5_) | copy-start | bytes 30724
  46.6 4.2 %collective-permute-start.13 = (f32[20,128]{1,0:T(8,128)}, f32[20,128]{1,0:T(8,128)S(1)}, u32[]{:S(2)}, u32[]{:S(2)}) collective-permute-start(f32[20,128]{1,0:T(8,128)} %get-tuple-element.8), channel_id=1, source_target_pairs={{0,3},{1,7},{2,11},{3,15},{4,2},{5,6},{6,10},{7,14},{8,1},{9,5},{1... | collective-permute-start | bytes 30728 | tf_op jit(solution)/shard_map/ppermute | solution.py:309
  49.2 2.8 %copy-start.2 = (bf16[20,20,128]{2,1,0:T(8,128)(2,1)}, bf16[20,20,128]{2,1,0:T(8,128)(2,1)S(1)}, u32[]{:S(2)}) copy-start(bf16[20,20,128]{2,1,0:T(8,128)(2,1)S(1)} %collective-permute-done.8.refs_3_) | copy-start | bytes 307204
  49.2 2.1 %collective-permute-start.9 = (bf16[20,20,128]{2,1,0:T(8,128)(2,1)S(1)}, bf16[20,20,128]{2,1,0:T(8,128)(2,1)S(1)}, u32[]{:S(2)}, u32[]{:S(2)}) collective-permute-start(bf16[20,20,128]{2,1,0:T(8,128)(2,1)S(1)} %collective-permute-done.8.refs_3_), channel_id=1, source_target_pairs={{0,4},{4,0},{8,12},{12,8},{1,5},{5,1},{9,13},{13,9},{2,6},{6,2},{1... | collective-permute-start | bytes 307208 | tf_op jit(solution)/shard_map/ppermute | solution.py:229
  50.4 1.6 %copy-start.12 = (f32[20,128]{1,0:T(8,128)}, f32[20,128]{1,0:T(8,128)S(1)}, u32[]{:S(2)}) copy-start(f32[20,128]{1,0:T(8,128)S(1)} %collective-permute-done.11.refs_6_) | copy-start | bytes 30724
  50.4 1.6 %copy-start.13 = (f32[20,128]{1,0:T(8,128)}, f32[20,128]{1,0:T(8,128)S(1)}, u32[]{:S(2)}) copy-start(f32[20,128]{1,0:T(8,128)S(1)} %collective-permute-done.12.refs_7_) | copy-start | bytes 30724
  50.8 1.2 %copy-start.14 = (f32[20,128]{1,0:T(8,128)}, f32[20,128]{1,0:T(8,128)S(1)}, u32[]{:S(2)}) copy-start(f32[20,128]{1,0:T(8,128)S(1)} %collective-permute-done.13.refs_8_) | copy-start | bytes 30724
  50.8 1.2 %copy-start.3 = (bf16[20,20,128]{2,1,0:T(8,128)(2,1)}, bf16[20,20,128]{2,1,0:T(8,128)(2,1)S(1)}, u32[]{:S(2)}) copy-start(bf16[20,20,128]{2,1,0:T(8,128)(2,1)S(1)} %collective-permute-done.7.refs_2_) | copy-start | bytes 307204
  51.3 0.7 %copy-start.6 = (bf16[20,20,128]{2,1,0:T(8,128)(2,1)}, bf16[20,20,128]{2,1,0:T(8,128)(2,1)S(1)}, u32[]{:S(2)}) copy-start(bf16[20,20,128]{2,1,0:T(8,128)(2,1)S(1)} %collective-permute-done.9.refs_4_) | copy-start | bytes 307204

commit v2 on v0

v2 whole, which is shorter than its diff:
```python
import functools

import jax
import jax.numpy as jnp
from jax import lax
from jax.experimental import pallas as pl
from jax.experimental.pallas import tpu as pltpu
from jax.sharding import PartitionSpec as P


BF = jnp.bfloat16
F32 = jnp.float32


def layer_norm(values):
    floats = values.astype(F32)
    center = jnp.mean(floats, axis=-1, keepdims=True)
    spread = jnp.mean((floats - center) ** 2, axis=-1, keepdims=True)
    return ((floats - center) * lax.rsqrt(spread + 1e-05)).astype(BF)


def bias_terms(normed, weight, offset, chain_left, chain_right):
    first, second, width = normed.shape
    heads = weight.shape[1]
    terms = jnp.dot(normed.reshape(-1, width), weight, preferred_element_type=F32)
    same = (chain_left[:, None] == chain_right[None, :]).astype(F32)
    return terms.reshape(first, second, heads) + offset[None, None, :] * same[:, :, None]


def attention(rows, normed, in_w, out_w, bias_full, maskadd):
    count, length, width = rows.shape
    heads = bias_full.shape[0]
    head_width = width // heads
    scale = head_width ** (-0.5)
    proj = jnp.dot(normed.reshape(-1, width), in_w, preferred_element_type=F32)
    proj = proj.astype(BF).reshape(count, length, 4 * width)

    def one_row(piece):
        query = piece[:, 0:width].reshape(length, heads, head_width)
        keys = piece[:, width : 2 * width].reshape(length, heads, head_width)
        vals = piece[:, 2 * width : 3 * width].reshape(length, heads, head_width)
        gate = piece[:, 3 * width :].astype(F32)
        scores = jnp.einsum("jhd,khd->hjk", query, keys, preferred_element_type=F32) * scale
        scores = scores + bias_full + maskadd[None, None, :]
        probs = jax.nn.softmax(scores, axis=-1).astype(BF)
        mixed = jnp.einsum("hjk,khd->jhd", probs, vals, preferred_element_type=F32)
        return (jax.nn.sigmoid(gate) * mixed.reshape(length, width)).astype(BF)

    gated = lax.map(one_row, proj)
    update = jnp.dot(gated.reshape(-1, width), out_w, preferred_element_type=F32)
    return (rows.astype(F32) + update.reshape(rows.shape)).astype(BF)


def transition(rows, trans_up, trans_down):
    width = rows.shape[-1]
    normed = layer_norm(rows).reshape(-1, width)
    hidden = jax.nn.relu(jnp.dot(normed, trans_up, preferred_element_type=F32)).astype(BF)
    update = jnp.dot(hidden, trans_down, preferred_element_type=F32)
    return (rows.astype(F32) + update.reshape(rows.shape)).astype(BF)


def plain_device(
    pair, mask, chain_ids, attn_in, attn_out, bias_weight, chain_bias, trans_up, trans_down
):
    across = lax.axis_size("gc")
    rows = lax.all_to_all(pair, "gc", split_axis=0, concat_axis=1, tiled=True)
    count = rows.shape[0]
    first_row = (lax.axis_index("gr") * across + lax.axis_index("gc")) * count
    maskadd = jnp.where(mask > 0, 0.0, -1000000000.0).astype(F32)
    own_chain = lax.dynamic_slice_in_dim(chain_ids, first_row, count)
    normed = layer_norm(rows)
    start_part = bias_terms(normed, bias_weight[0], chain_bias[0], own_chain, chain_ids)
    start_full = lax.all_gather(
        jnp.transpose(start_part, (2, 0, 1)), ("gr", "gc"), axis=1, tiled=True
    )
    rows = attention(rows, normed, attn_in[0], attn_out[0], start_full, maskadd)
    tile = lax.all_to_all(rows, "gc", split_axis=1, concat_axis=0, tiled=True)
    tile = transition(tile, trans_up, trans_down)
    tile_rows, tile_cols = (tile.shape[0], tile.shape[1])
    chain_rows = lax.dynamic_slice_in_dim(chain_ids, lax.axis_index("gr") * tile_rows, tile_rows)
    chain_cols = lax.dynamic_slice_in_dim(chain_ids, lax.axis_index("gc") * tile_cols, tile_cols)
    end_part = bias_terms(layer_norm(tile), bias_weight[1], chain_bias[1], chain_rows, chain_cols)
    end_part = lax.all_gather(jnp.transpose(end_part, (2, 1, 0)), "gc", axis=1, tiled=True)
    end_full = lax.all_gather(end_part, "gr", axis=2, tiled=True)
    columns = lax.all_to_all(
        jnp.transpose(tile, (1, 0, 2)), "gr", split_axis=0, concat_axis=1, tiled=True
    )
    columns = attention(columns, layer_norm(columns), attn_in[1], attn_out[1], end_full, maskadd)
    returned = lax.all_to_all(columns, "gr", split_axis=1, concat_axis=0, tiled=True)
    return jnp.transpose(returned, (1, 0, 2))


def norm32(x):
    center = jnp.mean(x, axis=-1, keepdims=True)
    off = x - center
    spread = jnp.mean(off * off, axis=-1, keepdims=True)
    return (off * lax.rsqrt(spread + 1e-05)).astype(BF)


def contract(a, b, da, db):
    return lax.dot_general(a, b, (((da,), (db,)), ((), ())), preferred_element_type=F32)


def tile_bias(normed, weight, chain, span):
    count, _, width = normed.shape
    heads = weight.shape[0]
    rep = jnp.concatenate(
        [jnp.broadcast_to(weight[h : h + 1].astype(F32), (span, width)) for h in range(heads)], axis=0
    )
    place = lax.broadcasted_iota(jnp.int32, rep.shape, 0) % span
    spread = jnp.concatenate(
        [jnp.where(place == j, rep, 0.0).astype(BF) for j in range(count)], axis=1
    )
    tokens = jnp.concatenate([normed[j] for j in range(count)], axis=1)
    return contract(tokens, spread, 1, 1) + chain


def chain_terms(ids, query_at, key_at, weights, heads, span):
    lanes = heads * span
    reach = ids.shape[1]
    lane = lax.broadcasted_iota(jnp.int32, (reach, lanes), 1) % span
    spot = lax.broadcasted_iota(jnp.int32, (reach, lanes), 0)
    left = contract(ids, (spot == lane + query_at).astype(F32).astype(BF), 1, 0)[0:1]
    row = lax.broadcasted_iota(jnp.int32, (span, reach), 0)
    col = lax.broadcasted_iota(jnp.int32, (span, reach), 1)
    every = jnp.broadcast_to(ids[0:1].astype(F32), (lanes, reach)).astype(BF)
    right = contract((col == row + key_at).astype(F32).astype(BF), every, 1, 1)
    head = lax.broadcasted_iota(jnp.int32, (span, lanes), 1) // span
    term = jnp.zeros((span, lanes), F32)
    for h in range(heads):
        term = jnp.where(head == h, weights[h], term)
    return jnp.where(left == right, term, 0.0)


def key_mask(mask, block, pieces, count, lanes):
    reach = mask.shape[1]
    every = jnp.broadcast_to(mask[0:1].astype(F32), (lanes, reach)).astype(BF)
    shape = (pieces * count, reach)
    row = lax.broadcasted_iota(jnp.int32, shape, 0)
    col = lax.broadcasted_iota(jnp.int32, shape, 1)
    want = jnp.full(shape, -1, jnp.int32)
    for k in range(pieces):
        inside = (row >= k * count) & (row < (k + 1) * count)
        want = jnp.where(inside, row - k * count + (block ^ k) * count, want)
    found = contract((col == want).astype(F32).astype(BF), every, 1, 1)
    return jnp.where(found > 0.0, 0.0, -1000000000.0)


def spread_ids(ref, reach):
    ids = ref[...].astype(F32)
    pad = jnp.zeros((1, reach - ids.shape[1]), F32)
    return jnp.broadcast_to(jnp.concatenate([ids, pad], axis=1), (8, reach)).astype(BF)


def first_bias_kernel(
    heads, span, side, pair_ref, in_ref, out_ref, up_ref, down_ref, weight_ref, ids_ref, mask_ref,
    chain_ref, o_ref, chain_out, row_mask, col_mask, own, in_out, out_out, up_out, down_out,
    pad, sems,
):
    nr, nc, _ = pair_ref.shape
    lanes = heads * span
    copies = [
        pltpu.make_async_copy(a, b, sems.at[i])
        for i, (a, b) in enumerate(
            (
                (pair_ref, own), (in_ref, in_out), (out_ref, out_out),
                (up_ref, up_out), (down_ref, down_out),
            )
        )
    ]
    for copy in copies:
        copy.start()
    gr, gc = lax.axis_index("gr"), lax.axis_index("gc")
    ids = spread_ids(ids_ref, lanes)
    here = chain_terms(ids, gr * nr, gc * nc, [chain_ref[0, h] for h in range(heads)], heads, span)
    chain_out[...] = chain_terms(
        ids, gc * nc, gr * nr, [chain_ref[1, h] for h in range(heads)], heads, span
    )
    mask = spread_ids(mask_ref, lanes)
    row_mask[...] = key_mask(mask, gc, side, nc, lanes)
    col_mask[...] = key_mask(mask, gr, side, nr, lanes)
    pad[...] = jnp.zeros_like(pad)
    copies[0].wait()
    pad[:, 0:nc, :] = own[...].astype(F32)
    o_ref[...] = tile_bias(norm32(pad[...]), weight_ref[0], here, span)[0:nc]
    for copy in copies[1:]:
        copy.wait()


def score_kernel(layer, heads, span, pieces, *refs):
    chunks = refs[0:pieces]
    in_ref, s_ref, v_ref, g_ref, base_ref, gather = refs[pieces:]
    nb, nt, width = chunks[0].shape
    length = pieces * nt
    weights = in_ref[layer]
    for k in range(pieces):
        gather[:, k * nt : (k + 1) * nt, :] = chunks[k][...].astype(F32)
    everyone = norm32(gather[...].reshape(nb * length, width))
    mine = jnp.concatenate([everyone[b * length : b * length + span] for b in range(nb)], axis=0)
    base_ref[...] = jnp.concatenate([gather[b, 0:span, :] for b in range(nb)], axis=0)
    query = jnp.dot(mine, weights[:, 0:width], preferred_element_type=F32).astype(BF)
    g_ref[...] = jnp.dot(mine, weights[:, 3 * width :], preferred_element_type=F32).astype(BF)
    keys = jnp.dot(everyone, weights[:, width : 2 * width], preferred_element_type=F32).astype(BF)
    v_ref[...] = jnp.dot(
        everyone, weights[:, 2 * width : 3 * width], preferred_element_type=F32
    ).astype(BF)
    head_of = lax.broadcasted_iota(jnp.int32, (span, width), 1) // (width // heads)
    for b in range(nb):
        q = query[b * span : (b + 1) * span]
        wide = jnp.concatenate(
            [jnp.where(head_of == h, q, jnp.zeros_like(q)) for h in range(heads)], axis=0
        )
        s_ref[b * length : (b + 1) * length] = contract(
            keys[b * length : (b + 1) * length], wide, 1, 1
        )


def attend(heads, span, pieces, s_ref, v_ref, g_ref, base_ref, bias_refs, mask_ref, out_w, table, probs):
    width = v_ref.shape[1]
    length = mask_ref.shape[0]
    nt = length // pieces
    nb = v_ref.shape[0] // length
    scale = (width // heads) ** (-0.5)
    spin = lax.axis_index("gr") ^ lax.axis_index("gc")
    for slot in range(pieces):

        @pl.when(spin == slot)
        def _():
            for k in range(pieces):
                table[k * nt : (k + 1) * nt, :] = bias_refs[slot ^ k][...]

    for b in range(nb):
        s = s_ref[b * length : (b + 1) * length] * scale + table[...] + mask_ref[...]
        e = jnp.exp(s - jnp.max(s, axis=0, keepdims=True))
        probs[b * length : (b + 1) * length] = (
            e * (1.0 / jnp.sum(e, axis=0, keepdims=True))
        ).astype(BF)
    head_of = lax.broadcasted_iota(jnp.int32, (span, width), 1) // (width // heads)
    mixed = []
    for b in range(nb):
        rows = slice(b * length, (b + 1) * length)
        o = contract(probs[rows], v_ref[rows], 0, 0)
        got = o[0:span]
        for h in range(1, heads):
            got = jnp.where(head_of == h, o[h * span : (h + 1) * span], got)
        mixed.append(got)
    mixed = jnp.concatenate(mixed, axis=0)
    gated = (jax.nn.sigmoid(g_ref[...].astype(F32)) * mixed).astype(BF)
    update = jnp.dot(gated, out_w, preferred_element_type=F32)
    return (base_ref[...] + update).astype(BF).astype(F32)


def first_kernel(heads, span, pieces, *refs):
    bias_refs = refs[4 : 4 + pieces]
    (
        mask_ref, out_ref, up_ref, down_ref, weight_ref, chain_ref,
        tile_ref, bias_ref, table, probs, flip,
    ) = refs[4 + pieces :]
    nb = bias_ref.shape[0]
    nt = tile_ref.shape[0]
    first = attend(
        heads, span, pieces, *refs[0:4], bias_refs, mask_ref, out_ref[0], table, probs
    )
    hidden = jnp.dot(norm32(first), up_ref[...], preferred_element_type=F32)
    hidden = jnp.maximum(hidden, 0.0).astype(BF)
    update = jnp.dot(hidden, down_ref[...], preferred_element_type=F32)
    second = (first + update).astype(BF).astype(F32)
    flip[...] = jnp.zeros_like(flip)
    for b in range(nb):
        flip[:, b, :] = second[b * span : b * span + nt]
    turned = flip[...]
    tile_ref[...] = turned[:, 0:nb].astype(BF)
    bias_ref[...] = tile_bias(norm32(turned), weight_ref[1], chain_ref[...], span)[0:nb]


def second_kernel(heads, span, pieces, *refs):
    bias_refs = refs[4 : 4 + pieces]
    mask_ref, out_ref, tile_ref, table, probs, flip = refs[4 + pieces :]
    nt, nb, _ = tile_ref.shape
    last = attend(
        heads, span, pieces, *refs[0:4], bias_refs, mask_ref, out_ref[1], table, probs
    )
    for b in range(nb):
        flip[:, b, :] = last[b * span : b * span + nt]
    tile_ref[...] = flip[...].astype(BF)


VMEM = pl.BlockSpec(memory_space=pltpu.VMEM)
SMEM = pl.BlockSpec(memory_space=pltpu.SMEM)
HBM = pl.BlockSpec(memory_space=pltpu.HBM)
PARAMS = pltpu.CompilerParams(vmem_limit_bytes=24 * 1024 * 1024)


def swap(array, axis, k):
    size = lax.axis_size(axis)
    return lax.ppermute(array, axis, [(i, i ^ k) for i in range(size)])


def scores(layer, heads, span, chunks, weights):
    nb, nt, width = chunks[0].shape
    keys, own, lanes = nb * nt * len(chunks), nb * span, heads * span
    return pl.pallas_call(
        functools.partial(score_kernel, layer, heads, span, len(chunks)),
        out_shape=(
            jax.ShapeDtypeStruct((keys, lanes), F32),
            jax.ShapeDtypeStruct((keys, width), BF),
            jax.ShapeDtypeStruct((own, width), BF),
            jax.ShapeDtypeStruct((own, width), F32),
        ),
        in_specs=[VMEM] * (len(chunks) + 1),
        out_specs=(VMEM,) * 4,
        scratch_shapes=[pltpu.VMEM((nb, len(chunks) * nt, width), F32)],
        compiler_params=PARAMS,
    )(*chunks, weights)


def fast_device(
    span, pair, mask, chain_ids, attn_in, attn_out, bias_weight, chain_bias, trans_up, trans_down
):
    side = lax.axis_size("gc")
    nr, nc, width = pair.shape
    heads = bias_weight.shape[2]
    lanes = heads * span
    cells = [(r, c) for r in range(side) for c in range(side)]
    weight = jnp.transpose(bias_weight, (0, 2, 1))
    plain = (attn_in, attn_out, trans_up, trans_down)

    moved = [swap(pair, "gc", k) for k in range(1, side)]
    piece, chain_two, row_mask, col_mask, own, *plain = pl.pallas_call(
        functools.partial(first_bias_kernel, heads, span, side),
        out_shape=(
            jax.ShapeDtypeStruct((nc, lanes), F32),
            jax.ShapeDtypeStruct((span, lanes), F32),
            jax.ShapeDtypeStruct((side * nc, lanes), F32),
            jax.ShapeDtypeStruct((side * nr, lanes), F32),
            *(jax.ShapeDtypeStruct(a.shape, a.dtype) for a in (pair, *plain)),
        ),
        in_specs=[HBM] * 5 + [VMEM] * 3 + [SMEM],
        out_specs=(VMEM,) * 9,
        scratch_shapes=[
            pltpu.VMEM((nr, span, width), F32),
            pltpu.SemaphoreType.DMA((5,)),
        ],
        compiler_params=PARAMS,
    )(
        *(pltpu.with_memory_space_constraint(a, pltpu.HBM) for a in (pair, *plain)),
        weight, chain_ids[None, :], mask[None, :], chain_bias,
    )
    attn_in, attn_out, trans_up, trans_down = plain
    pieces = []
    for k in range(0, side, 2):
        got = lax.ppermute(
            piece, ("gr", "gc"), [(r * side + c, (c ^ k) * side + r) for r, c in cells]
        )
        pieces += [got, swap(got, "gr", 1)]
    heard = scores(0, heads, span, [own, *moved], attn_in)
    tile, piece = pl.pallas_call(
        functools.partial(first_kernel, heads, span, side),
        out_shape=(
            jax.ShapeDtypeStruct((nc, nr, width), BF),
            jax.ShapeDtypeStruct((nr, lanes), F32),
        ),
        in_specs=[VMEM] * (side + 10),
        out_specs=(VMEM, VMEM),
        scratch_shapes=[
            pltpu.VMEM((side * nc, lanes), F32),
            pltpu.VMEM((nr * side * nc, lanes), BF),
            pltpu.VMEM((nc, span, width), F32),
        ],
        compiler_params=PARAMS,
    )(*heard, *pieces, row_mask, attn_out, trans_up, trans_down, weight, chain_two)

    other = swap(piece, "gr", 1)
    chunks = [tile, swap(tile, "gr", 1)]
    for k in range(2, side, 2):
        far = swap(tile, "gr", k)
        chunks += [far, swap(far, "gr", 1)]
    both = jnp.stack([piece, other])
    pieces = []
    for k in range(0, side, 2):
        got = lax.ppermute(
            both, ("gr", "gc"), [(r * side + c, c * side + (r ^ k)) for r, c in cells]
        )
        pieces += [got[0], got[1]]
    heard = scores(1, heads, span, chunks, attn_in)
    return pl.pallas_call(
        functools.partial(second_kernel, heads, span, side),
        out_shape=jax.ShapeDtypeStruct((nr, nc, width), BF),
        in_specs=[VMEM] * (side + 6),
        out_specs=VMEM,
        scratch_shapes=[
            pltpu.VMEM((side * nr, lanes), F32),
            pltpu.VMEM((nc * side * nr, lanes), BF),
            pltpu.VMEM((nr, nc, width), F32),
        ],
        compiler_params=PARAMS,
    )(*heard, *pieces, col_mask, attn_out)


def solution(mesh):
    shape = dict(mesh.shape)
    in_specs = (P(("jobs", "gr"), "gc", None), P("jobs"), P("jobs"), P(), P(), P(), P(), P(), P())
    out_specs = P(("jobs", "gr"), "gc", None)
    side = shape["gc"]
    square = shape["gr"] == side and side & (side - 1) == 0

    def per_device(*args):
        nr, nc, width = args[0].shape
        heads = args[5].shape[2]
        span = 128 // heads
        fits = nr == nc and nr <= span and (side * nr) % 16 == 0 and width == 128
        if square and fits:
            return fast_device(span, *args)
        return plain_device(*args)

    return jax.shard_map(
        per_device, mesh=mesh, in_specs=in_specs, out_specs=out_specs, check_vma=False
    )
```

time: 100 us -> 35.5 us (0.35)
  blocking collectives: 58.1 us -> 0 us
  Pallas kernels: 0 us -> 8.41 us
  local copies, waits for them, and re-layouts: 8.6 us -> 0.7 us
  matrix products: 5.88 us -> 0 us
  other arithmetic: 3.36 us -> 0.01 us
  starting transfers between devices: 13.1 us -> 15.4 us
    all_gather x3 -> x0, blocking collectives: 50.3 us -> none  [the longest x1 31.1 us: per_device(): lax.all_gather(jnp.transpose(start_part, (2, 0, 1)), ('gr', 'gc'), axis=1...]
    ppermute x0 -> x13, starting transfers between devices: none -> 15.4 us  [the longest x9 7.22 us: swap(): return lax.ppermute(array, axis, [(i, i ^ k) for i in range(size)])]
    all_to_all x3 -> x0, starting transfers between devices: 13.1 us -> none  [the longest x1 6.48 us: per_device(): rows = lax.all_to_all(pair, 'gc', split_axis=0, concat_axis=1, tiled=True)]
    ppermute x0 -> x13, waiting for transfers between devices: none -> 10.3 us  [the longest x9 6.3 us: swap(): return lax.ppermute(array, axis, [(i, i ^ k) for i in range(size)])]
    all_to_all x3 -> x0, waiting for transfers between devices: 9.75 us -> none  [the longest x1 5.9 us: per_device(): tile = lax.all_to_all(rows, 'gc', split_axis=1, concat_axis=0, tiled=True)]
    pallas_call x0 -> x5, Pallas kernels: none -> 8.41 us  [the longest x2 2.65 us: scores(): pl.pallas_call(functools.partial(score_kernel, layer, heads, span, len(ch...]
    all_to_all x1 -> x0, blocking collectives: 7.8 us -> none  [per_device(): lax.all_to_all(columns, 'gr', split_axis=1, concat_axis=0, tiled=True)]
    dot_general x27 -> x0, matrix products: 5.88 us -> none  [the longest x10 2.2 us: one_row(): jnp.einsum('jhd,khd->hjk', query, keys, preferred_element_type=jnp.float32)]
  transfers between devices with their start and end apart: 3 -> 13, of which waited for: 2 -> 5; matrix products, arithmetic and copies ran while one was open for 1% -> 0% of each run, Pallas kernels for 0% -> 10%
where the time goes in v2:
time: 35.5 us; the launch traced here: 34.8 us
  starting transfers between devices  15.4 us (43%)
  waiting for transfers between devices  10.3 us (29%)
  Pallas kernels  8.41 us (24%)
  local copies, waits for them, and re-layouts  0.7 us (2%)
    ppermute x9, starting transfers between devices, swap(): return lax.ppermute(array, axis, [(i, i ^ k) for i in range(size)])  7.22 us
    ppermute x9, waiting for transfers between devices, swap(): return lax.ppermute(array, axis, [(i, i ^ k) for i in range(size)])  6.3 us
    ppermute x2, starting transfers between devices, fast_device(): lax.ppermute(piece, ('gr', 'gc'), [(r * side + c, (c ^ k) * side + r) for...  5.33 us
    ppermute x2, waiting for transfers between devices, fast_device(): lax.ppermute(piece, ('gr', 'gc'), [(r * side + c, (c ^ k) * side + r) for...  3.52 us
    ppermute x2, starting transfers between devices, fast_device(): lax.ppermute(both, ('gr', 'gc'), [(r * side + c, c * side + (r ^ k)) for...  2.83 us
    pallas_call x2, Pallas kernels, scores(): pl.pallas_call(functools.partial(score_kernel, layer, heads, span, len(ch...  2.65 us
    pallas_call x1, Pallas kernels, fast_device(): pl.pallas_call(functools.partial(first_bias_kernel, heads, span, side), o...  2.23 us
    pallas_call x1, Pallas kernels, fast_device(): pl.pallas_call(functools.partial(first_kernel, heads, span, side), out_sh...  2.13 us
  transfers between devices with their start and end apart: 13, of which 5 were waited for; matrix products, arithmetic and copies ran while one was open for 0% of the time, Pallas kernels for 10%

profile of v2, /device:TPU:0, one launch (start us, length us, event | category | flops | bytes accessed | tf_op | source)
XLA Modules:
  0.0 34.8 jit_solution(4961510220785964059)
XLA Ops:
  0.0 3.1 %collective-permute-start = (bf16[20,20,128]{2,1,0:T(8,128)(2,1)}, bf16[20,20,128]{2,1,0:T(8,128)(2,1)S(1)}, u32[]{:S(2)}, u32[]{:S(2)}) collective-permute-start(bf16[20,20,128]{2,1,0:T(8,128)(2,1)} %pair_ref.1), channel_id=1, source_target_pairs={{0,1},{1,0},{2,3},{3,2},{4,5},{5,4},{6,7},{7,6},{8,9},{9,8},{10,11... | collective-permute-start | bytes 307208 | tf_op jit(solution)/shard_map/ppermute | solution.py:296
  3.1 2.6 %collective-permute-start.1 = (bf16[20,20,128]{2,1,0:T(8,128)(2,1)}, bf16[20,20,128]{2,1,0:T(8,128)(2,1)S(1)}, u32[]{:S(2)}, u32[]{:S(2)}) collective-permute-start(bf16[20,20,128]{2,1,0:T(8,128)(2,1)} %pair_ref.1), channel_id=1, source_target_pairs={{0,2},{1,3},{2,0},{3,1},{4,6},{5,7},{6,4},{7,5},{8,10},{9,11},{10,... | collective-permute-start | bytes 307208 | tf_op jit(solution)/shard_map/ppermute | solution.py:296
  5.6 0.0 collective-permute-start.2
  5.6 0.0 copy-start.3
  5.6 0.0 copy-start
  5.7 0.0 copy-start.1
  5.7 0.0 copy-start.2
  5.7 0.6 %copy-done.3 = s32[80]{0:T(128)S(1)} copy-done((s32[80]{0:T(128)S(1)}, s32[80]{0:T(128)}, u32[]{:S(2)}) %copy-start.3) | copy-done | bytes 344
  6.3 0.0 copy-done
  6.3 0.0 copy-done.1
  6.4 0.0 copy-done.2
  6.4 2.2 %shard_map.91 = (f32[20,128]{1,0:T(8,128)S(1)}, f32[32,128]{1,0:T(8,128)S(1)}, f32[80,128]{1,0:T(8,128)S(1)}, f32[80,128]{1,0:T(8,128)S(1)}, bf16[20,20,128]{2,1...) custom-call(bf16[20,20,128]{2,1,0:T(8,128)(2,1)} %pair_ref.1, ...), custom_call_target="tpu_custom_call" | custom-call | tf_op jit(solution)/shard_map/pallas_call | solution.py:329
  8.6 0.7 %collective-permute-start.3 = (f32[20,128]{1,0:T(8,128)S(1)}, f32[20,128]{1,0:T(8,128)S(1)}, u32[]{:S(2)}, u32[]{:S(2)}) collective-permute-start(f32[20,128]{1,0:T(8,128)S(1)} %get-tuple-element.30), channel_id=1, source_target_pairs={{0,0},{1,4},{2,8},{3,12},{4,1},{5,5},{6,9},{7,13},{8,2},{9,6},{10,... | collective-permute-start | bytes 30728 | tf_op jit(solution)/shard_map/ppermute | solution.py:352
  9.3 4.7 %collective-permute-start.5 = (f32[20,128]{1,0:T(8,128)S(1)}, f32[20,128]{1,0:T(8,128)S(1)}, u32[]{:S(2)}, u32[]{:S(2)}) collective-permute-start(f32[20,128]{1,0:T(8,128)S(1)} %get-tuple-element.30), channel_id=1, source_target_pairs={{0,8},{1,12},{2,0},{3,4},{4,9},{5,13},{6,1},{7,5},{8,10},{9,14},{1... | collective-permute-start | bytes 30728 | tf_op jit(solution)/shard_map/ppermute | solution.py:352
  13.9 0.0 collective-permute-done.3.refs_4_
  13.9 0.5 %collective-permute-start.4 = (f32[20,128]{1,0:T(8,128)S(1)}, f32[20,128]{1,0:T(8,128)S(1)}, u32[]{:S(2)}, u32[]{:S(2)}) collective-permute-start(f32[20,128]{1,0:T(8,128)S(1)} %collective-permute-done.3.refs_4_), channel_id=1, source_target_pairs={{0,4},{4,0},{8,12},{12,8},{1,5},{5,1},{9,13},{13,9},{2,6},{6,2},{1... | collective-permute-start | bytes 30728 | tf_op jit(solution)/shard_map/ppermute | solution.py:296
  14.4 3.5 %collective-permute-done.5.refs_6_ = f32[20,128]{1,0:T(8,128)S(1)} collective-permute-done((f32[20,128]{1,0:T(8,128)S(1)}, f32[20,128]{1,0:T(8,128)S(1)}, u32[]{:S(2)}, u32[]{:S(2)}) %collective-permute-start.5) | collective-permute-done | bytes 10272 | tf_op jit(solution)/shard_map/ppermute | solution.py:352
  18.0 0.0 collective-permute-start.6
  18.0 0.0 collective-permute-done.refs_1_
  18.0 0.0 collective-permute-done.1.refs_2_
  18.0 0.0 collective-permute-done.2.refs_3_
  18.0 1.3 %shard_map.92 = (f32[1600,128]{1,0:T(8,128)S(1)}, bf16[1600,128]{1,0:T(8,128)(2,1)S(1)}, bf16[640,128]{1,0:T(8,128)(2,1)S(1)}, f32[640,128]{1,0:T(8,128)S(1)}) custom-call(bf16[20,20,128]{2,1,0:T(8,128)(2,1)S(1)} %get-tuple-element.24.refs_0_, bf16[20,20,128]{2,1,0:T(8,128)(2,1)S(1)} %collective-permute-done.refs_1_, ...), custom_call_target="tpu_custom_call" | custom-call | tf_op jit(solution)/shard_map/pallas_call | solution.py:302
  19.3 0.0 collective-permute-done.4.refs_5_
  19.3 0.0 collective-permute-done.6.refs_7_
  19.3 2.1 %shard_map.93 = (bf16[20,20,128]{2,1,0:T(8,128)(2,1)S(1)}, f32[20,128]{1,0:T(8,128)S(1)}) custom-call(f32[1600,128]{1,0:T(8,128)S(1)} %get-tuple-element.26.refs_0_, bf16[1600,128]{1,0:T(8,128)(2,1)S(1)} %get-tuple-element.27.refs_1_, bf16[640,128]{1,0:T(8,128)(2,1)S(1)} %get-tuple-element.28.refs_2_, f32[640,128]{1,0:T(8,128)S(1)} %get-tuple-element.29.refs_3_, ...), custom_call_target="tpu_custom_call" | custom-call | tf_op jit(solution)/shard_map/pallas_call | solution.py:357
  21.5 0.5 %collective-permute-start.10 = (f32[20,128]{1,0:T(8,128)S(1)}, f32[20,128]{1,0:T(8,128)S(1)}, u32[]{:S(2)}, u32[]{:S(2)}) collective-permute-start(f32[20,128]{1,0:T(8,128)S(1)} %get-tuple-element.41), channel_id=1, source_target_pairs={{0,4},{4,0},{8,12},{12,8},{1,5},{5,1},{9,13},{13,9},{2,6},{6,2},{1... | collective-permute-start | bytes 30728 | tf_op jit(solution)/shard_map/ppermute | solution.py:296
  22.0 0.8 %collective-permute-done.10 = f32[20,128]{1,0:T(8,128)S(1)} collective-permute-done((f32[20,128]{1,0:T(8,128)S(1)}, f32[20,128]{1,0:T(8,128)S(1)}, u32[]{:S(2)}, u32[]{:S(2)}) %collective-permute-start.10) | collective-permute-done | bytes 10272 | tf_op jit(solution)/shard_map/ppermute | solution.py:296
  22.8 2.2 %collective-permute-start.12 = (f32[2,20,128]{2,1,0:T(8,128)S(1)}, f32[2,20,128]{2,1,0:T(8,128)S(1)}, u32[]{:S(2)}, u32[]{:S(2)}) collective-permute-start(f32[2,20,128]{2,1,0:T(8,128)S(1)} %pad_maximum_fusion), channel_id=1, source_target_pairs={{0,2},{1,6},{2,10},{3,14},{4,3},{5,7},{6,11},{7,15},{8,0},{9,4},{1... | collective-permute-start | bytes 61448 | tf_op jit(solution)/shard_map/ppermute | solution.py:381
  25.0 0.0 collective-permute-start.8
  25.0 0.6 %collective-permute-start.7 = (bf16[20,20,128]{2,1,0:T(8,128)(2,1)S(1)}, bf16[20,20,128]{2,1,0:T(8,128)(2,1)S(1)}, u32[]{:S(2)}, u32[]{:S(2)}) collective-permute-start(bf16[20,20,128]{2,1,0:T(8,128)(2,1)S(1)} %get-tuple-element.36.refs_0_), channel_id=1, source_target_pairs={{0,4},{4,0},{8,12},{12,8},{1,5},{5,1},{9,13},{13,9},{2,6},{6,2},{1... | collective-permute-start | bytes 307208 | tf_op jit(solution)/shard_map/ppermute | solution.py:296
  25.6 0.7 %collective-permute-start.11 = (f32[2,20,128]{2,1,0:T(8,128)S(1)}, f32[2,20,128]{2,1,0:T(8,128)S(1)}, u32[]{:S(2)}, u32[]{:S(2)}) collective-permute-start(f32[2,20,128]{2,1,0:T(8,128)S(1)} %pad_maximum_fusion), channel_id=1, source_target_pairs={{0,0},{1,4},{2,8},{3,12},{4,1},{5,5},{6,9},{7,13},{8,2},{9,6},{10,... | collective-permute-start | bytes 61448 | tf_op jit(solution)/shard_map/ppermute | solution.py:381
  26.2 0.4 %collective-permute-done.12 = f32[2,20,128]{2,1,0:T(8,128)S(1)} collective-permute-done((f32[2,20,128]{2,1,0:T(8,128)S(1)}, f32[2,20,128]{2,1,0:T(8,128)S(1)}, u32[]{:S(2)}, u32[]{:S(2)}) %collective-permute-start.12) | collective-permute-done | bytes 20512 | tf_op jit(solution)/shard_map/ppermute | solution.py:381
  26.6 4.1 %collective-permute-done.8.refs_2_ = bf16[20,20,128]{2,1,0:T(8,128)(2,1)S(1)} collective-permute-done((bf16[20,20,128]{2,1,0:T(8,128)(2,1)S(1)}, bf16[20,20,128]{2,1,0:T(8,128)(2,1)S(1)}, u32[]{:S(2)}, u32[]{:S(2)}) %collective-permute-start.8) | collective-permute-done | bytes 102432 | tf_op jit(solution)/shard_map/ppermute | solution.py:296
  30.8 0.0 collective-permute-start.9
  30.8 0.0 collective-permute-done.11
  30.8 0.0 collective-permute-done.7.refs_1_
  30.8 1.3 %collective-permute-done.9.refs_3_ = bf16[20,20,128]{2,1,0:T(8,128)(2,1)S(1)} collective-permute-done((bf16[20,20,128]{2,1,0:T(8,128)(2,1)S(1)}, bf16[20,20,128]{2,1,0:T(8,128)(2,1)S(1)}, u32[]{:S(2)}, u32[]{:S(2)}) %collective-permute-start.9) | collective-permute-done | bytes 102432 | tf_op jit(solution)/shard_map/ppermute | solution.py:296
  32.1 1.3 %shard_map.94 = (f32[1600,128]{1,0:T(8,128)S(1)}, bf16[1600,128]{1,0:T(8,128)(2,1)S(1)}, bf16[640,128]{1,0:T(8,128)(2,1)S(1)}, f32[640,128]{1,0:T(8,128)S(1)}) custom-call(bf16[20,20,128]{2,1,0:T(8,128)(2,1)S(1)} %get-tuple-element.36.refs_0_, bf16[20,20,128]{2,1,0:T(8,128)(2,1)S(1)} %collective-permute-done.7.refs_1_, ...), custom_call_target="tpu_custom_call" | custom-call | tf_op jit(solution)/shard_map/pallas_call | solution.py:302
  33.5 1.4 %shard_map.95 = bf16[20,20,128]{2,1,0:T(8,128)(2,1)} custom-call(f32[1600,128]{1,0:T(8,128)S(1)} %get-tuple-element.37.refs_0_, bf16[1600,128]{1,0:T(8,128)(2,1)S(1)} %get-tuple-element.38.refs_1_, bf16[640,128]{1,0:T(8,128)(2,1)S(1)} %get-tuple-element.39.refs_2_, f32[640,128]{1,0:T(8,128)S(1)} %get-tuple-element.40.refs_3_, ...), custom_call_target="tpu_custom_call" | custom-call | tf_op jit(solution)/shard_map/pallas_call | solution.py:386
  (3 shorter events, 0.0 us)
Async XLA Ops:
  0.0 18.0 %collective-permute-start = (bf16[20,20,128]{2,1,0:T(8,128)(2,1)}, bf16[20,20,128]{2,1,0:T(8,128)(2,1)S(1)}, u32[]{:S(2)}, u32[]{:S(2)}) collective-permute-start(bf16[20,20,128]{2,1,0:T(8,128)(2,1)} %pair_ref.1), channel_id=1, source_target_pairs={{0,1},{1,0},{2,3},{3,2},{4,5},{5,4},{6,7},{7,6},{8,9},{9,8},{10,11... | collective-permute-start | bytes 307208 | tf_op jit(solution)/shard_map/ppermute | solution.py:296
  3.1 14.9 %collective-permute-start.1 = (bf16[20,20,128]{2,1,0:T(8,128)(2,1)}, bf16[20,20,128]{2,1,0:T(8,128)(2,1)S(1)}, u32[]{:S(2)}, u32[]{:S(2)}) collective-permute-start(bf16[20,20,128]{2,1,0:T(8,128)(2,1)} %pair_ref.1), channel_id=1, source_target_pairs={{0,2},{1,3},{2,0},{3,1},{4,6},{5,7},{6,4},{7,5},{8,10},{9,11},{10,... | collective-permute-start | bytes 307208 | tf_op jit(solution)/shard_map/ppermute | solution.py:296
  5.6 12.3 %collective-permute-start.2 = (bf16[20,20,128]{2,1,0:T(8,128)(2,1)}, bf16[20,20,128]{2,1,0:T(8,128)(2,1)S(1)}, u32[]{:S(2)}, u32[]{:S(2)}) collective-permute-start(bf16[20,20,128]{2,1,0:T(8,128)(2,1)} %pair_ref.1), channel_id=1, source_target_pairs={{0,3},{1,2},{2,1},{3,0},{4,7},{5,6},{6,5},{7,4},{8,11},{9,10},{10,... | collective-permute-start | bytes 307208 | tf_op jit(solution)/shard_map/ppermute | solution.py:296
  5.6 0.7 %copy-start.3 = (s32[80]{0:T(128)S(1)}, s32[80]{0:T(128)}, u32[]{:S(2)}) copy-start(s32[80]{0:T(128)} %param.10) | copy-start | bytes 964
  5.6 0.7 %copy-start = (bf16[2,128,4]{1,2,0:T(4,128)(2,1)S(1)}, bf16[2,128,4]{1,2,0:T(4,128)(2,1)}, u32[]{:S(2)}) copy-start(bf16[2,128,4]{1,2,0:T(4,128)(2,1)} %param.14) | copy-start | bytes 6148
  5.7 0.7 %copy-start.1 = (f32[2,4]{1,0:T(2,128)S(1)}, f32[2,4]{1,0:T(2,128)}, u32[]{:S(2)}) copy-start(f32[2,4]{1,0:T(2,128)} %chain_ref.1) | copy-start | bytes 100
  5.7 0.7 %copy-start.2 = (s32[80]{0:T(128)S(1)}, s32[80]{0:T(128)}, u32[]{:S(2)}) copy-start(s32[80]{0:T(128)} %param.11) | copy-start | bytes 964
  8.6 5.3 %collective-permute-start.3 = (f32[20,128]{1,0:T(8,128)S(1)}, f32[20,128]{1,0:T(8,128)S(1)}, u32[]{:S(2)}, u32[]{:S(2)}) collective-permute-start(f32[20,128]{1,0:T(8,128)S(1)} %get-tuple-element.30), channel_id=1, source_target_pairs={{0,0},{1,4},{2,8},{3,12},{4,1},{5,5},{6,9},{7,13},{8,2},{9,6},{10,... | collective-permute-start | bytes 30728 | tf_op jit(solution)/shard_map/ppermute | solution.py:352
  9.3 8.7 %collective-permute-start.5 = (f32[20,128]{1,0:T(8,128)S(1)}, f32[20,128]{1,0:T(8,128)S(1)}, u32[]{:S(2)}, u32[]{:S(2)}) collective-permute-start(f32[20,128]{1,0:T(8,128)S(1)} %get-tuple-element.30), channel_id=1, source_target_pairs={{0,8},{1,12},{2,0},{3,4},{4,9},{5,13},{6,1},{7,5},{8,10},{9,14},{1... | collective-permute-start | bytes 30728 | tf_op jit(solution)/shard_map/ppermute | solution.py:352
  13.9 5.4 %collective-permute-start.4 = (f32[20,128]{1,0:T(8,128)S(1)}, f32[20,128]{1,0:T(8,128)S(1)}, u32[]{:S(2)}, u32[]{:S(2)}) collective-permute-start(f32[20,128]{1,0:T(8,128)S(1)} %collective-permute-done.3.refs_4_), channel_id=1, source_target_pairs={{0,4},{4,0},{8,12},{12,8},{1,5},{5,1},{9,13},{13,9},{2,6},{6,2},{1... | collective-permute-start | bytes 30728 | tf_op jit(solution)/shard_map/ppermute | solution.py:296
  18.0 1.4 %collective-permute-start.6 = (f32[20,128]{1,0:T(8,128)S(1)}, f32[20,128]{1,0:T(8,128)S(1)}, u32[]{:S(2)}, u32[]{:S(2)}) collective-permute-start(f32[20,128]{1,0:T(8,128)S(1)} %collective-permute-done.5.refs_6_), channel_id=1, source_target_pairs={{0,4},{4,0},{8,12},{12,8},{1,5},{5,1},{9,13},{13,9},{2,6},{6,2},{1... | collective-permute-start | bytes 30728 | tf_op jit(solution)/shard_map/ppermute | solution.py:296
  21.5 1.3 %collective-permute-start.10 = (f32[20,128]{1,0:T(8,128)S(1)}, f32[20,128]{1,0:T(8,128)S(1)}, u32[]{:S(2)}, u32[]{:S(2)}) collective-permute-start(f32[20,128]{1,0:T(8,128)S(1)} %get-tuple-element.41), channel_id=1, source_target_pairs={{0,4},{4,0},{8,12},{12,8},{1,5},{5,1},{9,13},{13,9},{2,6},{6,2},{1... | collective-permute-start | bytes 30728 | tf_op jit(solution)/shard_map/ppermute | solution.py:296
  22.8 3.8 %collective-permute-start.12 = (f32[2,20,128]{2,1,0:T(8,128)S(1)}, f32[2,20,128]{2,1,0:T(8,128)S(1)}, u32[]{:S(2)}, u32[]{:S(2)}) collective-permute-start(f32[2,20,128]{2,1,0:T(8,128)S(1)} %pad_maximum_fusion), channel_id=1, source_target_pairs={{0,2},{1,6},{2,10},{3,14},{4,3},{5,7},{6,11},{7,15},{8,0},{9,4},{1... | collective-permute-start | bytes 61448 | tf_op jit(solution)/shard_map/ppermute | solution.py:381
  25.0 5.8 %collective-permute-start.8 = (bf16[20,20,128]{2,1,0:T(8,128)(2,1)S(1)}, bf16[20,20,128]{2,1,0:T(8,128)(2,1)S(1)}, u32[]{:S(2)}, u32[]{:S(2)}) collective-permute-start(bf16[20,20,128]{2,1,0:T(8,128)(2,1)S(1)} %get-tuple-element.36.refs_0_), channel_id=1, source_target_pairs={{0,8},{4,12},{8,0},{12,4},{1,9},{5,13},{9,1},{13,5},{2,10},{6,14},... | collective-permute-start | bytes 307208 | tf_op jit(solution)/shard_map/ppermute | solution.py:296
  25.0 5.8 %collective-permute-start.7 = (bf16[20,20,128]{2,1,0:T(8,128)(2,1)S(1)}, bf16[20,20,128]{2,1,0:T(8,128)(2,1)S(1)}, u32[]{:S(2)}, u32[]{:S(2)}) collective-permute-start(bf16[20,20,128]{2,1,0:T(8,128)(2,1)S(1)} %get-tuple-element.36.refs_0_), channel_id=1, source_target_pairs={{0,4},{4,0},{8,12},{12,8},{1,5},{5,1},{9,13},{13,9},{2,6},{6,2},{1... | collective-permute-start | bytes 307208 | tf_op jit(solution)/shard_map/ppermute | solution.py:296
  25.6 5.2 %collective-permute-start.11 = (f32[2,20,128]{2,1,0:T(8,128)S(1)}, f32[2,20,128]{2,1,0:T(8,128)S(1)}, u32[]{:S(2)}, u32[]{:S(2)}) collective-permute-start(f32[2,20,128]{2,1,0:T(8,128)S(1)} %pad_maximum_fusion), channel_id=1, source_target_pairs={{0,0},{1,4},{2,8},{3,12},{4,1},{5,5},{6,9},{7,13},{8,2},{9,6},{10,... | collective-permute-start | bytes 61448 | tf_op jit(solution)/shard_map/ppermute | solution.py:381
  30.8 1.3 %collective-permute-start.9 = (bf16[20,20,128]{2,1,0:T(8,128)(2,1)S(1)}, bf16[20,20,128]{2,1,0:T(8,128)(2,1)S(1)}, u32[]{:S(2)}, u32[]{:S(2)}) collective-permute-start(bf16[20,20,128]{2,1,0:T(8,128)(2,1)S(1)} %collective-permute-done.8.refs_2_), channel_id=1, source_target_pairs={{0,4},{4,0},{8,12},{12,8},{1,5},{5,1},{9,13},{13,9},{2,6},{6,2},{1... | collective-permute-start | bytes 307208 | tf_op jit(solution)/shard_map/ppermute | solution.py:296

commit v3 on v2

--- a/solution.py
+++ b/solution.py
@@ -90,29 +90,27 @@
     return jnp.transpose(returned, (1, 0, 2))
 
 
-def norm32(x):
+def normal(x):
     center = jnp.mean(x, axis=-1, keepdims=True)
     off = x - center
     spread = jnp.mean(off * off, axis=-1, keepdims=True)
-    return (off * lax.rsqrt(spread + 1e-05)).astype(BF)
+    return off * lax.rsqrt(spread + 1e-05)
+
+
+def norm32(x):
+    return normal(x).astype(BF)
 
 
 def contract(a, b, da, db):
     return lax.dot_general(a, b, (((da,), (db,)), ((), ())), preferred_element_type=F32)
 
 
-def tile_bias(normed, weight, chain, span):
-    count, _, width = normed.shape
-    heads = weight.shape[0]
+def every_head(normed, weight, span):
+    heads, width = weight.shape
     rep = jnp.concatenate(
         [jnp.broadcast_to(weight[h : h + 1].astype(F32), (span, width)) for h in range(heads)], axis=0
     )
-    place = lax.broadcasted_iota(jnp.int32, rep.shape, 0) % span
-    spread = jnp.concatenate(
-        [jnp.where(place == j, rep, 0.0).astype(BF) for j in range(count)], axis=1
-    )
-    tokens = jnp.concatenate([normed[j] for j in range(count)], axis=1)
-    return contract(tokens, spread, 1, 1) + chain
+    return contract(normed, rep.astype(BF), 1, 1)
 
 
 def chain_terms(ids, query_at, key_at, weights, heads, span):
@@ -154,52 +152,70 @@
 
 def first_bias_kernel(
     heads, span, side, pair_ref, in_ref, out_ref, up_ref, down_ref, weight_ref, ids_ref, mask_ref,
-    chain_ref, o_ref, chain_out, row_mask, col_mask, own, in_out, out_out, up_out, down_out,
-    pad, sems,
+    chain_ref, o_ref, chain_out, row_mask, col_mask, tight, in_out, out_out, up_out, down_out,
+    weight_out, own, pad, packed, ids_in, mask_in, chain_in, sems,
 ):
-    nr, nc, _ = pair_ref.shape
+    nr, nc, width = pair_ref.shape
+    rows = pad.shape[1]
     lanes = heads * span
-    copies = [
-        pltpu.make_async_copy(a, b, sems.at[i])
-        for i, (a, b) in enumerate(
-            (
-                (pair_ref, own), (in_ref, in_out), (out_ref, out_out),
-                (up_ref, up_out), (down_ref, down_out),
-            )
-        )
-    ]
+    moves = (
+        (ids_ref, ids_in), (mask_ref, mask_in), (chain_ref, chain_in), (weight_ref, weight_out),
+        (pair_ref, own), (in_ref, in_out), (out_ref, out_out), (up_ref, up_out),
+        (down_ref, down_out),
+    )
+    copies = [pltpu.make_async_copy(a, b, sems.at[i]) for i, (a, b) in enumerate(moves)]
     for copy in copies:
         copy.start()
     gr, gc = lax.axis_index("gr"), lax.axis_index("gc")
-    ids = spread_ids(ids_ref, lanes)
-    here = chain_terms(ids, gr * nr, gc * nc, [chain_ref[0, h] for h in range(heads)], heads, span)
-    chain_out[...] = chain_terms(
-        ids, gc * nc, gr * nr, [chain_ref[1, h] for h in range(heads)], heads, span
-    )
-    mask = spread_ids(mask_ref, lanes)
+    pad[...] = jnp.zeros_like(pad)
+    for copy in copies[0:4]:
+        copy.wait()
+    ids = spread_ids(ids_in, lanes)
+    weights = [[chain_in[a : a + 1, h : h + 1] for h in range(heads)] for a in range(2)]
+    here = chain_terms(ids, gr * nr, gc * nc, weights[0], heads, span)
+    chain_out[...] = chain_terms(ids, gc * nc, gr * nr, weights[1], heads, span)
+    mask = spread_ids(mask_in, lanes)
     row_mask[...] = key_mask(mask, gc, side, nc, lanes)
     col_mask[...] = key_mask(mask, gr, side, nr, lanes)
-    pad[...] = jnp.zeros_like(pad)
-    copies[0].wait()
-    pad[:, 0:nc, :] = own[...].astype(F32)
-    o_ref[...] = tile_bias(norm32(pad[...]), weight_ref[0], here, span)[0:nc]
-    for copy in copies[1:]:
+    copies[4].wait()
+    exact = own[...].astype(F32)
+    pad[:, 0:nc, :] = exact
+    for j in range(nr):
+        packed[j * nc : (j + 1) * nc, :] = exact[j]
+    tight[...] = packed[...].astype(BF)
+    terms = every_head(norm32(pad[...].reshape(nr * rows, width)), weight_out[0], span)
+    query_of = lax.broadcasted_iota(jnp.int32, (rows, lanes), 1) % span
+    got = here[0:rows]
+    for j in range(nr):
+        got = got + jnp.where(query_of == j, terms[j * rows : (j + 1) * rows], 0.0)
+    o_ref[...] = got[0:nc]
+    for copy in copies[5:]:
         copy.wait()
 
 
-def score_kernel(layer, heads, span, pieces, *refs):
-    chunks = refs[0:pieces]
+def score_kernel(layer, heads, span, pieces, shape, *refs):
+    nb, nt = shape
     in_ref, s_ref, v_ref, g_ref, base_ref, gather = refs[pieces:]
-    nb, nt, width = chunks[0].shape
+    width = base_ref.shape[1]
     length = pieces * nt
     weights = in_ref[layer]
     for k in range(pieces):
-        gather[:, k * nt : (k + 1) * nt, :] = chunks[k][...].astype(F32)
-    everyone = norm32(gather[...].reshape(nb * length, width))
+        value = refs[k][...].astype(F32)
+        if value.ndim == 3:
+            gather[:, k * nt : (k + 1) * nt, :] = value
+        else:
+            for b in range(nb):
+                gather[b, k * nt : (k + 1) * nt, :] = value[b * nt : (b + 1) * nt]
+    rows = base_ref.shape[0] // nb
+    exact = normal(gather[...].reshape(nb * length, width))
+    everyone = exact.astype(BF)
     mine = jnp.concatenate([everyone[b * length : b * length + span] for b in range(nb)], axis=0)
-    base_ref[...] = jnp.concatenate([gather[b, 0:span, :] for b in range(nb)], axis=0)
+    base_ref[...] = jnp.concatenate([gather[b, 0:rows, :] for b in range(nb)], axis=0)
     query = jnp.dot(mine, weights[:, 0:width], preferred_element_type=F32).astype(BF)
-    g_ref[...] = jnp.dot(mine, weights[:, 3 * width :], preferred_element_type=F32).astype(BF)
+    tight = jnp.concatenate([exact[b * length : b * length + rows] for b in range(nb)], axis=0)
+    g_ref[...] = jnp.dot(
+        tight.astype(BF), weights[:, 3 * width :], preferred_element_type=F32
+    ).astype(BF)
     keys = jnp.dot(everyone, weights[:, width : 2 * width], preferred_element_type=F32).astype(BF)
     v_ref[...] = jnp.dot(
         everyone, weights[:, 2 * width : 3 * width], preferred_element_type=F32
@@ -235,14 +251,15 @@
         probs[b * length : (b + 1) * length] = (
             e * (1.0 / jnp.sum(e, axis=0, keepdims=True))
         ).astype(BF)
-    head_of = lax.broadcasted_iota(jnp.int32, (span, width), 1) // (width // heads)
+    rows = base_ref.shape[0] // nb
+    head_of = lax.broadcasted_iota(jnp.int32, (rows, width), 1) // (width // heads)
     mixed = []
     for b in range(nb):
-        rows = slice(b * length, (b + 1) * length)
-        o = contract(probs[rows], v_ref[rows], 0, 0)
-        got = o[0:span]
+        part = slice(b * length, (b + 1) * length)
+        o = contract(probs[part], v_ref[part], 0, 0)
+        got = o[0:rows]
         for h in range(1, heads):
-            got = jnp.where(head_of == h, o[h * span : (h + 1) * span], got)
+            got = jnp.where(head_of == h, o[h * span : h * span + rows], got)
         mixed.append(got)
     mixed = jnp.concatenate(mixed, axis=0)
     gated = (jax.nn.sigmoid(g_ref[...].astype(F32)) * mixed).astype(BF)
@@ -254,10 +271,10 @@
     bias_refs = refs[4 : 4 + pieces]
     (
         mask_ref, out_ref, up_ref, down_ref, weight_ref, chain_ref,
-        tile_ref, bias_ref, table, probs, flip,
+        tile_ref, bias_ref, table, probs,
     ) = refs[4 + pieces :]
-    nb = bias_ref.shape[0]
-    nt = tile_ref.shape[0]
+    nb, lanes = bias_ref.shape
+    rows = tile_ref.shape[0] // nb
     first = attend(
         heads, span, pieces, *refs[0:4], bias_refs, mask_ref, out_ref[0], table, probs
     )
@@ -265,12 +282,23 @@
     hidden = jnp.maximum(hidden, 0.0).astype(BF)
     update = jnp.dot(hidden, down_ref[...], preferred_element_type=F32)
     second = (first + update).astype(BF).astype(F32)
-    flip[...] = jnp.zeros_like(flip)
-    for b in range(nb):
-        flip[:, b, :] = second[b * span : b * span + nt]
-    turned = flip[...]
-    tile_ref[...] = turned[:, 0:nb].astype(BF)
-    bias_ref[...] = tile_bias(norm32(turned), weight_ref[1], chain_ref[...], span)[0:nb]
+    tile_ref[...] = second
+    terms = every_head(norm32(second), weight_ref[1], span)
+    shape = (rows, lanes)
+    pick = lax.broadcasted_iota(jnp.int32, shape, 1) % span == lax.broadcasted_iota(
+        jnp.int32, shape, 0
+    )
+    for b in range(nb):
+        line = jnp.where(pick, terms[b * rows : (b + 1) * rows], 0.0)
+        bias_ref[b : b + 1, :] = jnp.sum(line, axis=0, keepdims=True) + chain_ref[b : b + 1, :]
+
+
+def flip_kernel(nb, x_ref, o_ref, flip):
+    rows = x_ref.shape[0] // nb
+    nt = o_ref.shape[0] // nb
+    for b in range(nb):
+        flip[pl.ds(b, nt, stride=nb), :] = x_ref[b * rows : b * rows + nt]
+    o_ref[...] = flip[...].astype(BF)
 
 
 def second_kernel(heads, span, pieces, *refs):
@@ -280,8 +308,9 @@
     last = attend(
         heads, span, pieces, *refs[0:4], bias_refs, mask_ref, out_ref[1], table, probs
     )
-    for b in range(nb):
-        flip[:, b, :] = last[b * span : b * span + nt]
+    rows = last.shape[0] // nb
+    for b in range(nb):
+        flip[:, b, :] = last[b * rows : b * rows + nt]
     tile_ref[...] = flip[...].astype(BF)
 
 
@@ -291,16 +320,21 @@
 PARAMS = pltpu.CompilerParams(vmem_limit_bytes=24 * 1024 * 1024)
 
 
+def up_to_8(count):
+    return -(-count // 8) * 8
+
+
 def swap(array, axis, k):
     size = lax.axis_size(axis)
     return lax.ppermute(array, axis, [(i, i ^ k) for i in range(size)])
 
 
-def scores(layer, heads, span, chunks, weights):
-    nb, nt, width = chunks[0].shape
-    keys, own, lanes = nb * nt * len(chunks), nb * span, heads * span
+def scores(layer, heads, span, shape, chunks, weights):
+    nb, nt = shape
+    width = weights.shape[1]
+    keys, own, lanes = nb * nt * len(chunks), nb * up_to_8(nt), heads * span
     return pl.pallas_call(
-        functools.partial(score_kernel, layer, heads, span, len(chunks)),
+        functools.partial(score_kernel, layer, heads, span, len(chunks), shape),
         out_shape=(
             jax.ShapeDtypeStruct((keys, lanes), F32),
             jax.ShapeDtypeStruct((keys, width), BF),
@@ -325,27 +359,30 @@
     weight = jnp.transpose(bias_weight, (0, 2, 1))
     plain = (attn_in, attn_out, trans_up, trans_down)
 
-    moved = [swap(pair, "gc", k) for k in range(1, side)]
-    piece, chain_two, row_mask, col_mask, own, *plain = pl.pallas_call(
+    far = swap(pair, "gc", 2)
+    sources = (pair, *plain, weight, chain_ids[None, :], mask[None, :], chain_bias)
+    copied = (*plain, weight)
+    piece, chain_two, row_mask, col_mask, own, *plain, weight = pl.pallas_call(
         functools.partial(first_bias_kernel, heads, span, side),
         out_shape=(
             jax.ShapeDtypeStruct((nc, lanes), F32),
             jax.ShapeDtypeStruct((span, lanes), F32),
             jax.ShapeDtypeStruct((side * nc, lanes), F32),
             jax.ShapeDtypeStruct((side * nr, lanes), F32),
-            *(jax.ShapeDtypeStruct(a.shape, a.dtype) for a in (pair, *plain)),
+            jax.ShapeDtypeStruct((nr * nc, width), BF),
+            *(jax.ShapeDtypeStruct(a.shape, a.dtype) for a in copied),
         ),
-        in_specs=[HBM] * 5 + [VMEM] * 3 + [SMEM],
-        out_specs=(VMEM,) * 9,
+        in_specs=[HBM] * len(sources),
+        out_specs=(VMEM,) * (5 + len(copied)),
         scratch_shapes=[
-            pltpu.VMEM((nr, span, width), F32),
-            pltpu.SemaphoreType.DMA((5,)),
+            pltpu.VMEM(pair.shape, BF),
+            pltpu.VMEM((nr, up_to_8(nc), width), F32),
+            pltpu.VMEM((nr * nc, width), F32),
+            *(pltpu.VMEM(a.shape, a.dtype) for a in sources[-3:]),
+            pltpu.SemaphoreType.DMA((len(sources),)),
         ],
         compiler_params=PARAMS,
-    )(
-        *(pltpu.with_memory_space_constraint(a, pltpu.HBM) for a in (pair, *plain)),
-        weight, chain_ids[None, :], mask[None, :], chain_bias,
-    )
+    )(*(pltpu.with_memory_space_constraint(a, pltpu.HBM) for a in sources))
     attn_in, attn_out, trans_up, trans_down = plain
     pieces = []
     for k in range(0, side, 2):
@@ -353,11 +390,13 @@
             piece, ("gr", "gc"), [(r * side + c, (c ^ k) * side + r) for r, c in cells]
         )
         pieces += [got, swap(got, "gr", 1)]
-    heard = scores(0, heads, span, [own, *moved], attn_in)
-    tile, piece = pl.pallas_call(
+    last = swap(own, "gc", 3)
+    near = swap(own, "gc", 1)
+    heard = scores(0, heads, span, (nr, nc), [own, near, far, last], attn_in)
+    second, piece = pl.pallas_call(
         functools.partial(first_kernel, heads, span, side),
         out_shape=(
-            jax.ShapeDtypeStruct((nc, nr, width), BF),
+            jax.ShapeDtypeStruct((nr * up_to_8(nc), width), F32),
             jax.ShapeDtypeStruct((nr, lanes), F32),
         ),
         in_specs=[VMEM] * (side + 10),
@@ -365,10 +404,17 @@
         scratch_shapes=[
             pltpu.VMEM((side * nc, lanes), F32),
             pltpu.VMEM((nr * side * nc, lanes), BF),
-            pltpu.VMEM((nc, span, width), F32),
         ],
         compiler_params=PARAMS,
     )(*heard, *pieces, row_mask, attn_out, trans_up, trans_down, weight, chain_two)
+    tile = pl.pallas_call(
+        functools.partial(flip_kernel, nr),
+        out_shape=jax.ShapeDtypeStruct((nc * nr, width), BF),
+        in_specs=[VMEM],
+        out_specs=VMEM,
+        scratch_shapes=[pltpu.VMEM((nc * nr, width), F32)],
+        compiler_params=PARAMS,
+    )(second)
 
     other = swap(piece, "gr", 1)
     chunks = [tile, swap(tile, "gr", 1)]
@@ -382,7 +428,7 @@
             both, ("gr", "gc"), [(r * side + c, c * side + (r ^ k)) for r, c in cells]
         )
         pieces += [got[0], got[1]]
-    heard = scores(1, heads, span, chunks, attn_in)
+    heard = scores(1, heads, span, (nc, nr), chunks, attn_in)
     return pl.pallas_call(
         functools.partial(second_kernel, heads, span, side),
         out_shape=jax.ShapeDtypeStruct((nr, nc, width), BF),
@@ -402,7 +448,7 @@
     in_specs = (P(("jobs", "gr"), "gc", None), P("jobs"), P("jobs"), P(), P(), P(), P(), P(), P())
     out_specs = P(("jobs", "gr"), "gc", None)
     side = shape["gc"]
-    square = shape["gr"] == side and side & (side - 1) == 0
+    square = shape["gr"] == side and side == 4
 
     def per_device(*args):
         nr, nc, width = args[0].shape

time: 35.5 us -> 35.5 us (level)
  the two profiles are of different devices: /device:TPU:0 before, /device:TPU:7 now
where the time goes in v3:
time: 35.5 us; the launch traced here: 35.3 us
  starting transfers between devices  21 us (59%)
  waiting for transfers between devices  7.2 us (20%)
  Pallas kernels  7.04 us (20%)
    ppermute x9, starting transfers between devices, swap(): return lax.ppermute(array, axis, [(i, i ^ k) for i in range(size)])  11.4 us
    ppermute x2, starting transfers between devices, fast_device(): lax.ppermute(piece, ('gr', 'gc'), [(r * side + c, (c ^ k) * side + r) for...  5.72 us
    ppermute x2, starting transfers between devices, fast_device(): lax.ppermute(both, ('gr', 'gc'), [(r * side + c, c * side + (r ^ k)) for...  3.86 us
    ppermute x2, waiting for transfers between devices, fast_device(): lax.ppermute(both, ('gr', 'gc'), [(r * side + c, c * side + (r ^ k)) for...  3.86 us
    pallas_call x2, Pallas kernels, scores(): pl.pallas_call(functools.partial(score_kernel, layer, heads, span, len(ch...  2.59 us
    ppermute x2, waiting for transfers between devices, fast_device(): lax.ppermute(piece, ('gr', 'gc'), [(r * side + c, (c ^ k) * side + r) for...  2.49 us
    pallas_call x1, Pallas kernels, fast_device(): pl.pallas_call(functools.partial(first_kernel, heads, span, side), out_sh...  1.57 us
    pallas_call x1, Pallas kernels, fast_device(): pl.pallas_call(functools.partial(first_bias_kernel, heads, span, side), o...  1.47 us
  transfers between devices with their start and end apart: 13, of which 3 were waited for; matrix products, arithmetic and copies ran while one was open for 0% of the time, Pallas kernels for 4%

profile of v3, /device:TPU:7, one launch (start us, length us, event | category | flops | bytes accessed | tf_op | source)
XLA Modules:
  0.0 35.3 jit_solution(17731560655526643224)
XLA Ops:
  0.0 0.0 copy-start
  0.0 1.5 %shard_map.91 = (f32[20,128]{1,0:T(8,128)S(1)}, f32[32,128]{1,0:T(8,128)S(1)}, f32[80,128]{1,0:T(8,128)S(1)}, f32[80,128]{1,0:T(8,128)S(1)}, bf16[400,128]{1,0:T...) custom-call(bf16[20,20,128]{2,1,0:T(8,128)(2,1)} %pair_ref.1, ...), custom_call_target="tpu_custom_call" | custom-call | tf_op jit(solution)/shard_map/pallas_call | solution.py:365
  1.5 1.4 %collective-permute-start = (bf16[400,128]{1,0:T(8,128)(2,1)S(1)}, bf16[400,128]{1,0:T(8,128)(2,1)S(1)}, u32[]{:S(2)}, u32[]{:S(2)}) collective-permute-start(bf16[400,128]{1,0:T(8,128)(2,1)S(1)} %get-tuple-element.25.refs_0_), channel_id=1, source_target_pairs={{0,1},{1,0},{2,3},{3,2},{4,5},{5,4},{6,7},{7,6},{8,9},{9,8},{10,11... | collective-permute-start | bytes 307208 | tf_op jit(solution)/shard_map/ppermute | solution.py:329
  2.8 2.2 %collective-permute-start.2 = (bf16[400,128]{1,0:T(8,128)(2,1)S(1)}, bf16[400,128]{1,0:T(8,128)(2,1)S(1)}, u32[]{:S(2)}, u32[]{:S(2)}) collective-permute-start(bf16[400,128]{1,0:T(8,128)(2,1)S(1)} %get-tuple-element.25.refs_0_), channel_id=1, source_target_pairs={{0,3},{1,2},{2,1},{3,0},{4,7},{5,6},{6,5},{7,4},{8,11},{9,10},{10,... | collective-permute-start | bytes 307208 | tf_op jit(solution)/shard_map/ppermute | solution.py:329
  5.0 0.0 copy-done
  5.0 0.1 collective-permute-start.1
  5.2 5.6 %collective-permute-start.3 = (f32[20,128]{1,0:T(8,128)S(1)}, f32[20,128]{1,0:T(8,128)S(1)}, u32[]{:S(2)}, u32[]{:S(2)}) collective-permute-start(f32[20,128]{1,0:T(8,128)S(1)} %get-tuple-element.31), channel_id=1, source_target_pairs={{0,0},{1,4},{2,8},{3,12},{4,1},{5,5},{6,9},{7,13},{8,2},{9,6},{10,... | collective-permute-start | bytes 30728 | tf_op jit(solution)/shard_map/ppermute | solution.py:389
  10.8 0.1 collective-permute-start.5
  10.9 2.5 %collective-permute-done.3.refs_4_ = f32[20,128]{1,0:T(8,128)S(1)} collective-permute-done((f32[20,128]{1,0:T(8,128)S(1)}, f32[20,128]{1,0:T(8,128)S(1)}, u32[]{:S(2)}, u32[]{:S(2)}) %collective-permute-start.3) | collective-permute-done | bytes 10272 | tf_op jit(solution)/shard_map/ppermute | solution.py:389
  13.4 4.0 %collective-permute-start.4 = (f32[20,128]{1,0:T(8,128)S(1)}, f32[20,128]{1,0:T(8,128)S(1)}, u32[]{:S(2)}, u32[]{:S(2)}) collective-permute-start(f32[20,128]{1,0:T(8,128)S(1)} %collective-permute-done.3.refs_4_), channel_id=1, source_target_pairs={{0,4},{4,0},{8,12},{12,8},{1,5},{5,1},{9,13},{13,9},{2,6},{6,2},{1... | collective-permute-start | bytes 30728 | tf_op jit(solution)/shard_map/ppermute | solution.py:329
  17.3 0.0 collective-permute-done.5.refs_6_
  17.3 0.0 collective-permute-start.6
  17.3 0.0 collective-permute-done.refs_1_
  17.4 0.0 collective-permute-done.2.refs_3_
  17.4 0.0 collective-permute-done.1.refs_2_
  17.4 1.3 %shard_map.92 = (f32[1600,128]{1,0:T(8,128)S(1)}, bf16[1600,128]{1,0:T(8,128)(2,1)S(1)}, bf16[480,128]{1,0:T(8,128)(2,1)S(1)}, f32[480,128]{1,0:T(8,128)S(1)}) custom-call(bf16[400,128]{1,0:T(8,128)(2,1)S(1)} %get-tuple-element.25.refs_0_, bf16[400,128]{1,0:T(8,128)(2,1)S(1)} %collective-permute-done.refs_1_, ...), custom_call_target="tpu_custom_call" | custom-call | tf_op jit(solution)/shard_map/pallas_call | solution.py:336
  18.7 0.0 collective-permute-done.4.refs_5_
  18.7 0.0 collective-permute-done.6.refs_7_
  18.7 1.6 %shard_map.93 = (f32[480,128]{1,0:T(8,128)S(1)}, f32[20,128]{1,0:T(8,128)S(1)}) custom-call(f32[1600,128]{1,0:T(8,128)S(1)} %get-tuple-element.27.refs_0_, bf16[1600,128]{1,0:T(8,128)(2,1)S(1)} %get-tuple-element.28.refs_1_, bf16[480,128]{1,0:T(8,128)(2,1)S(1)} %get-tuple-element.29.refs_2_, f32[480,128]{1,0:T(8,128)S(1)} %get-tuple-element.30.refs_3_, ...), custom_call_target="tpu_custom_call" | custom-call | tf_op jit(solution)/shard_map/pallas_call | solution.py:396
  20.2 0.6 %collective-permute-start.10 = (f32[20,128]{1,0:T(8,128)S(1)}, f32[20,128]{1,0:T(8,128)S(1)}, u32[]{:S(2)}, u32[]{:S(2)}) collective-permute-start(f32[20,128]{1,0:T(8,128)S(1)} %get-tuple-element.43), channel_id=1, source_target_pairs={{0,4},{4,0},{8,12},{12,8},{1,5},{5,1},{9,13},{13,9},{2,6},{6,2},{1... | collective-permute-start | bytes 30728 | tf_op jit(solution)/shard_map/ppermute | solution.py:329
  20.8 0.8 %collective-permute-done.10 = f32[20,128]{1,0:T(8,128)S(1)} collective-permute-done((f32[20,128]{1,0:T(8,128)S(1)}, f32[20,128]{1,0:T(8,128)S(1)}, u32[]{:S(2)}, u32[]{:S(2)}) %collective-permute-start.10) | collective-permute-done | bytes 10272 | tf_op jit(solution)/shard_map/ppermute | solution.py:329
  21.6 0.0 collective-permute-start.12
  21.7 2.3 %collective-permute-start.8 = (bf16[400,128]{1,0:T(8,128)(2,1)S(1)}, bf16[400,128]{1,0:T(8,128)(2,1)S(1)}, u32[]{:S(2)}, u32[]{:S(2)}) collective-permute-start(bf16[400,128]{1,0:T(8,128)(2,1)S(1)} %shard_map.94.refs_0_), channel_id=1, source_target_pairs={{0,8},{4,12},{8,0},{12,4},{1,9},{5,13},{9,1},{13,5},{2,10},{6,14},... | collective-permute-start | bytes 307208 | tf_op jit(solution)/shard_map/ppermute | solution.py:329
  24.0 0.8 %collective-permute-start.7 = (bf16[400,128]{1,0:T(8,128)(2,1)S(1)}, bf16[400,128]{1,0:T(8,128)(2,1)S(1)}, u32[]{:S(2)}, u32[]{:S(2)}) collective-permute-start(bf16[400,128]{1,0:T(8,128)(2,1)S(1)} %shard_map.94.refs_0_), channel_id=1, source_target_pairs={{0,4},{4,0},{8,12},{12,8},{1,5},{5,1},{9,13},{13,9},{2,6},{6,2},{1... | collective-permute-start | bytes 307208 | tf_op jit(solution)/shard_map/ppermute | solution.py:329
  24.8 3.9 %collective-permute-start.11 = (f32[2,20,128]{2,1,0:T(8,128)S(1)}, f32[2,20,128]{2,1,0:T(8,128)S(1)}, u32[]{:S(2)}, u32[]{:S(2)}) collective-permute-start(f32[2,20,128]{2,1,0:T(8,128)S(1)} %pad_maximum_fusion), channel_id=1, source_target_pairs={{0,0},{1,4},{2,8},{3,12},{4,1},{5,5},{6,9},{7,13},{8,2},{9,6},{10,... | collective-permute-start | bytes 61448 | tf_op jit(solution)/shard_map/ppermute | solution.py:427
  28.7 0.0 collective-permute-done.12
  28.7 0.0 collective-permute-done.8.refs_2_
  28.7 0.1 collective-permute-start.9
  28.8 3.9 %collective-permute-done.11 = f32[2,20,128]{2,1,0:T(8,128)S(1)} collective-permute-done((f32[2,20,128]{2,1,0:T(8,128)S(1)}, f32[2,20,128]{2,1,0:T(8,128)S(1)}, u32[]{:S(2)}, u32[]{:S(2)}) %collective-permute-start.11) | collective-permute-done | bytes 20512 | tf_op jit(solution)/shard_map/ppermute | solution.py:427
  32.6 0.0 collective-permute-done.7.refs_1_
  32.6 0.0 collective-permute-done.9.refs_3_
  32.6 1.3 %shard_map.95 = (f32[1600,128]{1,0:T(8,128)S(1)}, bf16[1600,128]{1,0:T(8,128)(2,1)S(1)}, bf16[480,128]{1,0:T(8,128)(2,1)S(1)}, f32[480,128]{1,0:T(8,128)S(1)}) custom-call(bf16[400,128]{1,0:T(8,128)(2,1)S(1)} %shard_map.94.refs_0_, bf16[400,128]{1,0:T(8,128)(2,1)S(1)} %collective-permute-done.7.refs_1_, bf16[400,128]{1,0:T(8,128)(2,1)S(1)} %collective-permute-done.8.refs_2_, ...), custom_call_target="tpu_custom_call" | custom-call | tf_op jit(solution)/shard_map/pallas_call | solution.py:336
  33.9 1.4 %shard_map.96 = bf16[20,20,128]{2,1,0:T(8,128)(2,1)} custom-call(f32[1600,128]{1,0:T(8,128)S(1)} %get-tuple-element.39.refs_0_, bf16[1600,128]{1,0:T(8,128)(2,1)S(1)} %get-tuple-element.40.refs_1_, bf16[480,128]{1,0:T(8,128)(2,1)S(1)} %get-tuple-element.41.refs_2_, f32[480,128]{1,0:T(8,128)S(1)} %get-tuple-element.42.refs_3_, ...), custom_call_target="tpu_custom_call" | custom-call | tf_op jit(solution)/shard_map/pallas_call | solution.py:432
  (4 shorter events, 0.0 us)
Async XLA Ops:
  0.0 5.0 %copy-start = (bf16[20,20,128]{2,1,0:T(8,128)(2,1)S(1)}, bf16[20,20,128]{2,1,0:T(8,128)(2,1)}, u32[]{:S(2)}) copy-start(bf16[20,20,128]{2,1,0:T(8,128)(2,1)} %pair_ref.1) | copy-start | bytes 307204
  1.5 15.9 %collective-permute-start = (bf16[400,128]{1,0:T(8,128)(2,1)S(1)}, bf16[400,128]{1,0:T(8,128)(2,1)S(1)}, u32[]{:S(2)}, u32[]{:S(2)}) collective-permute-start(bf16[400,128]{1,0:T(8,128)(2,1)S(1)} %get-tuple-element.25.refs_0_), channel_id=1, source_target_pairs={{0,1},{1,0},{2,3},{3,2},{4,5},{5,4},{6,7},{7,6},{8,9},{9,8},{10,11... | collective-permute-start | bytes 307208 | tf_op jit(solution)/shard_map/ppermute | solution.py:329
  2.8 14.5 %collective-permute-start.2 = (bf16[400,128]{1,0:T(8,128)(2,1)S(1)}, bf16[400,128]{1,0:T(8,128)(2,1)S(1)}, u32[]{:S(2)}, u32[]{:S(2)}) collective-permute-start(bf16[400,128]{1,0:T(8,128)(2,1)S(1)} %get-tuple-element.25.refs_0_), channel_id=1, source_target_pairs={{0,3},{1,2},{2,1},{3,0},{4,7},{5,6},{6,5},{7,4},{8,11},{9,10},{10,... | collective-permute-start | bytes 307208 | tf_op jit(solution)/shard_map/ppermute | solution.py:329
  5.0 12.3 %collective-permute-start.1 = (bf16[20,20,128]{2,1,0:T(8,128)(2,1)S(1)}, bf16[20,20,128]{2,1,0:T(8,128)(2,1)S(1)}, u32[]{:S(2)}, u32[]{:S(2)}) collective-permute-start(bf16[20,20,128]{2,1,0:T(8,128)(2,1)S(1)} %copy-done), channel_id=1, source_target_pairs={{0,2},{1,3},{2,0},{3,1},{4,6},{5,7},{6,4},{7,5},{8,10},{9,11},{10,... | collective-permute-start | bytes 307208 | tf_op jit(solution)/shard_map/ppermute | solution.py:329
  5.2 8.2 %collective-permute-start.3 = (f32[20,128]{1,0:T(8,128)S(1)}, f32[20,128]{1,0:T(8,128)S(1)}, u32[]{:S(2)}, u32[]{:S(2)}) collective-permute-start(f32[20,128]{1,0:T(8,128)S(1)} %get-tuple-element.31), channel_id=1, source_target_pairs={{0,0},{1,4},{2,8},{3,12},{4,1},{5,5},{6,9},{7,13},{8,2},{9,6},{10,... | collective-permute-start | bytes 30728 | tf_op jit(solution)/shard_map/ppermute | solution.py:389
  10.8 6.5 %collective-permute-start.5 = (f32[20,128]{1,0:T(8,128)S(1)}, f32[20,128]{1,0:T(8,128)S(1)}, u32[]{:S(2)}, u32[]{:S(2)}) collective-permute-start(f32[20,128]{1,0:T(8,128)S(1)} %get-tuple-element.31), channel_id=1, source_target_pairs={{0,8},{1,12},{2,0},{3,4},{4,9},{5,13},{6,1},{7,5},{8,10},{9,14},{1... | collective-permute-start | bytes 30728 | tf_op jit(solution)/shard_map/ppermute | solution.py:389
  13.4 5.3 %collective-permute-start.4 = (f32[20,128]{1,0:T(8,128)S(1)}, f32[20,128]{1,0:T(8,128)S(1)}, u32[]{:S(2)}, u32[]{:S(2)}) collective-permute-start(f32[20,128]{1,0:T(8,128)S(1)} %collective-permute-done.3.refs_4_), channel_id=1, source_target_pairs={{0,4},{4,0},{8,12},{12,8},{1,5},{5,1},{9,13},{13,9},{2,6},{6,2},{1... | collective-permute-start | bytes 30728 | tf_op jit(solution)/shard_map/ppermute | solution.py:329
  17.3 1.3 %collective-permute-start.6 = (f32[20,128]{1,0:T(8,128)S(1)}, f32[20,128]{1,0:T(8,128)S(1)}, u32[]{:S(2)}, u32[]{:S(2)}) collective-permute-start(f32[20,128]{1,0:T(8,128)S(1)} %collective-permute-done.5.refs_6_), channel_id=1, source_target_pairs={{0,4},{4,0},{8,12},{12,8},{1,5},{5,1},{9,13},{13,9},{2,6},{6,2},{1... | collective-permute-start | bytes 30728 | tf_op jit(solution)/shard_map/ppermute | solution.py:329
  20.2 1.4 %collective-permute-start.10 = (f32[20,128]{1,0:T(8,128)S(1)}, f32[20,128]{1,0:T(8,128)S(1)}, u32[]{:S(2)}, u32[]{:S(2)}) collective-permute-start(f32[20,128]{1,0:T(8,128)S(1)} %get-tuple-element.43), channel_id=1, source_target_pairs={{0,4},{4,0},{8,12},{12,8},{1,5},{5,1},{9,13},{13,9},{2,6},{6,2},{1... | collective-permute-start | bytes 30728 | tf_op jit(solution)/shard_map/ppermute | solution.py:329
  21.6 7.0 %collective-permute-start.12 = (f32[2,20,128]{2,1,0:T(8,128)S(1)}, f32[2,20,128]{2,1,0:T(8,128)S(1)}, u32[]{:S(2)}, u32[]{:S(2)}) collective-permute-start(f32[2,20,128]{2,1,0:T(8,128)S(1)} %pad_maximum_fusion), channel_id=1, source_target_pairs={{0,2},{1,6},{2,10},{3,14},{4,3},{5,7},{6,11},{7,15},{8,0},{9,4},{1... | collective-permute-start | bytes 61448 | tf_op jit(solution)/shard_map/ppermute | solution.py:427
  21.7 7.0 %collective-permute-start.8 = (bf16[400,128]{1,0:T(8,128)(2,1)S(1)}, bf16[400,128]{1,0:T(8,128)(2,1)S(1)}, u32[]{:S(2)}, u32[]{:S(2)}) collective-permute-start(bf16[400,128]{1,0:T(8,128)(2,1)S(1)} %shard_map.94.refs_0_), channel_id=1, source_target_pairs={{0,8},{4,12},{8,0},{12,4},{1,9},{5,13},{9,1},{13,5},{2,10},{6,14},... | collective-permute-start | bytes 307208 | tf_op jit(solution)/shard_map/ppermute | solution.py:329
  24.0 8.7 %collective-permute-start.7 = (bf16[400,128]{1,0:T(8,128)(2,1)S(1)}, bf16[400,128]{1,0:T(8,128)(2,1)S(1)}, u32[]{:S(2)}, u32[]{:S(2)}) collective-permute-start(bf16[400,128]{1,0:T(8,128)(2,1)S(1)} %shard_map.94.refs_0_), channel_id=1, source_target_pairs={{0,4},{4,0},{8,12},{12,8},{1,5},{5,1},{9,13},{13,9},{2,6},{6,2},{1... | collective-permute-start | bytes 307208 | tf_op jit(solution)/shard_map/ppermute | solution.py:329
  24.8 7.8 %collective-permute-start.11 = (f32[2,20,128]{2,1,0:T(8,128)S(1)}, f32[2,20,128]{2,1,0:T(8,128)S(1)}, u32[]{:S(2)}, u32[]{:S(2)}) collective-permute-start(f32[2,20,128]{2,1,0:T(8,128)S(1)} %pad_maximum_fusion), channel_id=1, source_target_pairs={{0,0},{1,4},{2,8},{3,12},{4,1},{5,5},{6,9},{7,13},{8,2},{9,6},{10,... | collective-permute-start | bytes 61448 | tf_op jit(solution)/shard_map/ppermute | solution.py:427
  28.7 3.9 %collective-permute-start.9 = (bf16[400,128]{1,0:T(8,128)(2,1)S(1)}, bf16[400,128]{1,0:T(8,128)(2,1)S(1)}, u32[]{:S(2)}, u32[]{:S(2)}) collective-permute-start(bf16[400,128]{1,0:T(8,128)(2,1)S(1)} %collective-permute-done.8.refs_2_), channel_id=1, source_target_pairs={{0,4},{4,0},{8,12},{12,8},{1,5},{5,1},{9,13},{13,9},{2,6},{6,2},{1... | collective-permute-start | bytes 307208 | tf_op jit(solution)/shard_map/ppermute | solution.py:329

commit v4 on v3

--- a/solution.py
+++ b/solution.py
@@ -9,6 +9,8 @@
 
 
 BF = jnp.bfloat16
+GROUPS = 1
+LOG2E = 1.4426950408889634
 F32 = jnp.float32
 
 
@@ -111,6 +113,14 @@
         [jnp.broadcast_to(weight[h : h + 1].astype(F32), (span, width)) for h in range(heads)], axis=0
     )
     return contract(normed, rep.astype(BF), 1, 1)
+
+
+def select_terms(terms, chain, rows, count, span):
+    query_of = lax.broadcasted_iota(jnp.int32, (rows, terms.shape[1]), 1) % span
+    got = jnp.zeros((rows, terms.shape[1]), F32)
+    for j in range(count):
+        got = jnp.where(query_of == j, terms[j * rows : (j + 1) * rows], got)
+    return got + chain
 
 
 def chain_terms(ids, query_at, key_at, weights, heads, span):
@@ -173,7 +183,9 @@
     ids = spread_ids(ids_in, lanes)
     weights = [[chain_in[a : a + 1, h : h + 1] for h in range(heads)] for a in range(2)]
     here = chain_terms(ids, gr * nr, gc * nc, weights[0], heads, span)
-    chain_out[...] = chain_terms(ids, gc * nc, gr * nr, weights[1], heads, span)
+    chain_out[...] = chain_terms(ids, gc * nc, gr * nr, weights[1], heads, span)[
+        0 : chain_out.shape[0]
+    ]
     mask = spread_ids(mask_in, lanes)
     row_mask[...] = key_mask(mask, gc, side, nc, lanes)
     col_mask[...] = key_mask(mask, gr, side, nr, lanes)
@@ -184,11 +196,7 @@
         packed[j * nc : (j + 1) * nc, :] = exact[j]
     tight[...] = packed[...].astype(BF)
     terms = every_head(norm32(pad[...].reshape(nr * rows, width)), weight_out[0], span)
-    query_of = lax.broadcasted_iota(jnp.int32, (rows, lanes), 1) % span
-    got = here[0:rows]
-    for j in range(nr):
-        got = got + jnp.where(query_of == j, terms[j * rows : (j + 1) * rows], 0.0)
-    o_ref[...] = got[0:nc]
+    o_ref[...] = select_terms(terms, here[0:rows], rows, nr, span)[0:nc]
     for copy in copies[5:]:
         copy.wait()
 
@@ -221,12 +229,13 @@
         everyone, weights[:, 2 * width : 3 * width], preferred_element_type=F32
     ).astype(BF)
     head_of = lax.broadcasted_iota(jnp.int32, (span, width), 1) // (width // heads)
+    scale = LOG2E * (width // heads) ** (-0.5)
     for b in range(nb):
         q = query[b * span : (b + 1) * span]
         wide = jnp.concatenate(
             [jnp.where(head_of == h, q, jnp.zeros_like(q)) for h in range(heads)], axis=0
         )
-        s_ref[b * length : (b + 1) * length] = contract(
+        s_ref[b * length : (b + 1) * length] = scale * contract(
             keys[b * length : (b + 1) * length], wide, 1, 1
         )
 
@@ -236,7 +245,6 @@
     length = mask_ref.shape[0]
     nt = length // pieces
     nb = v_ref.shape[0] // length
-    scale = (width // heads) ** (-0.5)
     spin = lax.axis_index("gr") ^ lax.axis_index("gc")
     for slot in range(pieces):
 
@@ -245,52 +253,60 @@
             for k in range(pieces):
                 table[k * nt : (k + 1) * nt, :] = bias_refs[slot ^ k][...]
 
+    shift = LOG2E * (table[...] + mask_ref[...])
     for b in range(nb):
-        s = s_ref[b * length : (b + 1) * length] * scale + table[...] + mask_ref[...]
-        e = jnp.exp(s - jnp.max(s, axis=0, keepdims=True))
+        s = s_ref[b * length : (b + 1) * length] + shift
+        e = jnp.exp2(s - jnp.max(s, axis=0, keepdims=True))
         probs[b * length : (b + 1) * length] = (
             e * (1.0 / jnp.sum(e, axis=0, keepdims=True))
         ).astype(BF)
     rows = base_ref.shape[0] // nb
     head_of = lax.broadcasted_iota(jnp.int32, (rows, width), 1) // (width // heads)
-    mixed = []
-    for b in range(nb):
-        part = slice(b * length, (b + 1) * length)
-        o = contract(probs[part], v_ref[part], 0, 0)
-        got = o[0:rows]
-        for h in range(1, heads):
-            got = jnp.where(head_of == h, o[h * span : h * span + rows], got)
-        mixed.append(got)
-    mixed = jnp.concatenate(mixed, axis=0)
-    gated = (jax.nn.sigmoid(g_ref[...].astype(F32)) * mixed).astype(BF)
-    update = jnp.dot(gated, out_w, preferred_element_type=F32)
-    return (base_ref[...] + update).astype(BF).astype(F32)
+    done = []
+    for group in range(GROUPS):
+        mine = range(group * nb // GROUPS, (group + 1) * nb // GROUPS)
+        mixed = []
+        for b in mine:
+            part = slice(b * length, (b + 1) * length)
+            o = contract(probs[part], v_ref[part], 0, 0)
+            got = o[0:rows]
+            for h in range(1, heads):
+                got = jnp.where(head_of == h, o[h * span : h * span + rows], got)
+            mixed.append(got)
+        part = slice(mine[0] * rows, (mine[-1] + 1) * rows)
+        gate = jax.nn.sigmoid(g_ref[part].astype(F32))
+        gated = (gate * jnp.concatenate(mixed, axis=0)).astype(BF)
+        update = jnp.dot(gated, out_w, preferred_element_type=F32)
+        done.append((base_ref[part] + update).astype(BF).astype(F32))
+    return done
 
 
 def first_kernel(heads, span, pieces, *refs):
     bias_refs = refs[4 : 4 + pieces]
     (
         mask_ref, out_ref, up_ref, down_ref, weight_ref, chain_ref,
-        tile_ref, bias_ref, table, probs,
+        tile_ref, bias_ref, table, probs, turned,
     ) = refs[4 + pieces :]
-    nb, lanes = bias_ref.shape
+    nb, _ = bias_ref.shape
     rows = tile_ref.shape[0] // nb
-    first = attend(
+    done = attend(
         heads, span, pieces, *refs[0:4], bias_refs, mask_ref, out_ref[0], table, probs
     )
-    hidden = jnp.dot(norm32(first), up_ref[...], preferred_element_type=F32)
-    hidden = jnp.maximum(hidden, 0.0).astype(BF)
-    update = jnp.dot(hidden, down_ref[...], preferred_element_type=F32)
-    second = (first + update).astype(BF).astype(F32)
+    parts = []
+    for first in done:
+        hidden = jnp.dot(norm32(first), up_ref[...], preferred_element_type=F32)
+        hidden = jnp.maximum(hidden, 0.0).astype(BF)
+        update = jnp.dot(hidden, down_ref[...], preferred_element_type=F32)
+        parts.append((first + update).astype(BF).astype(F32))
+    second = jnp.concatenate(parts, axis=0)
     tile_ref[...] = second
-    terms = every_head(norm32(second), weight_ref[1], span)
-    shape = (rows, lanes)
-    pick = lax.broadcasted_iota(jnp.int32, shape, 1) % span == lax.broadcasted_iota(
-        jnp.int32, shape, 0
-    )
+    nt = turned.shape[0] // rows
+    turned[...] = jnp.zeros_like(turned)
     for b in range(nb):
-        line = jnp.where(pick, terms[b * rows : (b + 1) * rows], 0.0)
-        bias_ref[b : b + 1, :] = jnp.sum(line, axis=0, keepdims=True) + chain_ref[b : b + 1, :]
+        turned[pl.ds(b, nt, stride=rows), :] = second[b * rows : b * rows + nt]
+    bias_ref[...] = select_terms(
+        every_head(norm32(turned[...]), weight_ref[1], span), chain_ref[...], rows, nt, span
+    )[0:nb]
 
 
 def flip_kernel(nb, x_ref, o_ref, flip):
@@ -305,13 +321,15 @@
     bias_refs = refs[4 : 4 + pieces]
     mask_ref, out_ref, tile_ref, table, probs, flip = refs[4 + pieces :]
     nt, nb, _ = tile_ref.shape
-    last = attend(
+    done = attend(
         heads, span, pieces, *refs[0:4], bias_refs, mask_ref, out_ref[1], table, probs
     )
+    last = jnp.concatenate(done, axis=0)
     rows = last.shape[0] // nb
+    room = flip.shape[0] // nt
     for b in range(nb):
-        flip[:, b, :] = last[b * rows : b * rows + nt]
-    tile_ref[...] = flip[...].astype(BF)
+        flip[pl.ds(b, nt, stride=room), :] = last[b * rows : b * rows + nt]
+    tile_ref[...] = flip[...].reshape(nt, room, -1)[:, 0:nb].astype(BF)
 
 
 VMEM = pl.BlockSpec(memory_space=pltpu.VMEM)
@@ -366,7 +384,7 @@
         functools.partial(first_bias_kernel, heads, span, side),
         out_shape=(
             jax.ShapeDtypeStruct((nc, lanes), F32),
-            jax.ShapeDtypeStruct((span, lanes), F32),
+            jax.ShapeDtypeStruct((up_to_8(nr), lanes), F32),
             jax.ShapeDtypeStruct((side * nc, lanes), F32),
             jax.ShapeDtypeStruct((side * nr, lanes), F32),
             jax.ShapeDtypeStruct((nr * nc, width), BF),
@@ -404,6 +422,7 @@
         scratch_shapes=[
             pltpu.VMEM((side * nc, lanes), F32),
             pltpu.VMEM((nr * side * nc, lanes), BF),
+            pltpu.VMEM((nc * up_to_8(nr), width), F32),
         ],
         compiler_params=PARAMS,
     )(*heard, *pieces, row_mask, attn_out, trans_up, trans_down, weight, chain_two)
@@ -437,7 +456,7 @@
         scratch_shapes=[
             pltpu.VMEM((side * nr, lanes), F32),
             pltpu.VMEM((nc * side * nr, lanes), BF),
-            pltpu.VMEM((nr, nc, width), F32),
+            pltpu.VMEM((nr * up_to_8(nc), width), F32),
         ],
         compiler_params=PARAMS,
     )(*heard, *pieces, col_mask, attn_out)

time: 35.5 us -> 35.4 us (level)
  the two profiles are of different devices: /device:TPU:7 before, /device:TPU:3 now
where the time goes in v4:
time: 35.4 us; the launch traced here: 35.3 us
  starting transfers between devices  20.9 us (59%)
  waiting for transfers between devices  7.21 us (20%)
  Pallas kernels  7.01 us (20%)
    ppermute x9, starting transfers between devices, swap(): return lax.ppermute(array, axis, [(i, i ^ k) for i in range(size)])  11.4 us
    ppermute x2, starting transfers between devices, fast_device(): lax.ppermute(piece, ('gr', 'gc'), [(r * side + c, (c ^ k) * side + r) for...  5.72 us
    ppermute x2, waiting for transfers between devices, fast_device(): lax.ppermute(both, ('gr', 'gc'), [(r * side + c, c * side + (r ^ k)) for...  3.86 us
    ppermute x2, starting transfers between devices, fast_device(): lax.ppermute(both, ('gr', 'gc'), [(r * side + c, c * side + (r ^ k)) for...  3.85 us
    pallas_call x2, Pallas kernels, scores(): pl.pallas_call(functools.partial(score_kernel, layer, heads, span, len(ch...  2.61 us
    ppermute x2, waiting for transfers between devices, fast_device(): lax.ppermute(piece, ('gr', 'gc'), [(r * side + c, (c ^ k) * side + r) for...  2.49 us
    pallas_call x1, Pallas kernels, fast_device(): pl.pallas_call(functools.partial(first_kernel, heads, span, side), out_sh...  1.6 us
    pallas_call x1, Pallas kernels, fast_device(): pl.pallas_call(functools.partial(first_bias_kernel, heads, span, side), o...  1.47 us
  transfers between devices with their start and end apart: 13, of which 3 were waited for; matrix products, arithmetic and copies ran while one was open for 0% of the time, Pallas kernels for 4%

profile of v4, /device:TPU:3, one launch (start us, length us, event | category | flops | bytes accessed | tf_op | source)
XLA Modules:
  0.0 35.3 jit_solution(17108178193636305264)
XLA Ops:
  0.0 0.0 copy-start
  0.0 1.5 %shard_map.91 = (f32[20,128]{1,0:T(8,128)S(1)}, f32[24,128]{1,0:T(8,128)S(1)}, f32[80,128]{1,0:T(8,128)S(1)}, f32[80,128]{1,0:T(8,128)S(1)}, bf16[400,128]{1,0:T...) custom-call(bf16[20,20,128]{2,1,0:T(8,128)(2,1)} %pair_ref.1, ...), custom_call_target="tpu_custom_call" | custom-call | tf_op jit(solution)/shard_map/pallas_call | solution.py:383
  1.5 1.4 %collective-permute-start = (bf16[400,128]{1,0:T(8,128)(2,1)S(1)}, bf16[400,128]{1,0:T(8,128)(2,1)S(1)}, u32[]{:S(2)}, u32[]{:S(2)}) collective-permute-start(bf16[400,128]{1,0:T(8,128)(2,1)S(1)} %get-tuple-element.25.refs_0_), channel_id=1, source_target_pairs={{0,1},{1,0},{2,3},{3,2},{4,5},{5,4},{6,7},{7,6},{8,9},{9,8},{10,11... | collective-permute-start | bytes 307208 | tf_op jit(solution)/shard_map/ppermute | solution.py:347
  2.8 2.2 %collective-permute-start.2 = (bf16[400,128]{1,0:T(8,128)(2,1)S(1)}, bf16[400,128]{1,0:T(8,128)(2,1)S(1)}, u32[]{:S(2)}, u32[]{:S(2)}) collective-permute-start(bf16[400,128]{1,0:T(8,128)(2,1)S(1)} %get-tuple-element.25.refs_0_), channel_id=1, source_target_pairs={{0,3},{1,2},{2,1},{3,0},{4,7},{5,6},{6,5},{7,4},{8,11},{9,10},{10,... | collective-permute-start | bytes 307208 | tf_op jit(solution)/shard_map/ppermute | solution.py:347
  5.0 0.0 copy-done
  5.0 0.1 collective-permute-start.1
  5.2 5.6 %collective-permute-start.3 = (f32[20,128]{1,0:T(8,128)S(1)}, f32[20,128]{1,0:T(8,128)S(1)}, u32[]{:S(2)}, u32[]{:S(2)}) collective-permute-start(f32[20,128]{1,0:T(8,128)S(1)} %get-tuple-element.31), channel_id=1, source_target_pairs={{0,0},{1,4},{2,8},{3,12},{4,1},{5,5},{6,9},{7,13},{8,2},{9,6},{10,... | collective-permute-start | bytes 30728 | tf_op jit(solution)/shard_map/ppermute | solution.py:407
  10.8 0.1 collective-permute-start.5
  10.9 2.5 %collective-permute-done.3.refs_4_ = f32[20,128]{1,0:T(8,128)S(1)} collective-permute-done((f32[20,128]{1,0:T(8,128)S(1)}, f32[20,128]{1,0:T(8,128)S(1)}, u32[]{:S(2)}, u32[]{:S(2)}) %collective-permute-start.3) | collective-permute-done | bytes 10272 | tf_op jit(solution)/shard_map/ppermute | solution.py:407
  13.4 4.0 %collective-permute-start.4 = (f32[20,128]{1,0:T(8,128)S(1)}, f32[20,128]{1,0:T(8,128)S(1)}, u32[]{:S(2)}, u32[]{:S(2)}) collective-permute-start(f32[20,128]{1,0:T(8,128)S(1)} %collective-permute-done.3.refs_4_), channel_id=1, source_target_pairs={{0,4},{4,0},{8,12},{12,8},{1,5},{5,1},{9,13},{13,9},{2,6},{6,2},{1... | collective-permute-start | bytes 30728 | tf_op jit(solution)/shard_map/ppermute | solution.py:347
  17.3 0.0 collective-permute-done.5.refs_6_
  17.3 0.0 collective-permute-start.6
  17.3 0.0 collective-permute-done.refs_1_
  17.4 0.0 collective-permute-done.2.refs_3_
  17.4 0.0 collective-permute-done.1.refs_2_
  17.4 1.3 %shard_map.92 = (f32[1600,128]{1,0:T(8,128)S(1)}, bf16[1600,128]{1,0:T(8,128)(2,1)S(1)}, bf16[480,128]{1,0:T(8,128)(2,1)S(1)}, f32[480,128]{1,0:T(8,128)S(1)}) custom-call(bf16[400,128]{1,0:T(8,128)(2,1)S(1)} %get-tuple-element.25.refs_0_, bf16[400,128]{1,0:T(8,128)(2,1)S(1)} %collective-permute-done.refs_1_, ...), custom_call_target="tpu_custom_call" | custom-call | tf_op jit(solution)/shard_map/pallas_call | solution.py:354
  18.7 0.0 collective-permute-done.4.refs_5_
  18.7 0.0 collective-permute-done.6.refs_7_
  18.7 1.6 %shard_map.93 = (f32[480,128]{1,0:T(8,128)S(1)}, f32[20,128]{1,0:T(8,128)S(1)}) custom-call(f32[1600,128]{1,0:T(8,128)S(1)} %get-tuple-element.27.refs_0_, bf16[1600,128]{1,0:T(8,128)(2,1)S(1)} %get-tuple-element.28.refs_1_, bf16[480,128]{1,0:T(8,128)(2,1)S(1)} %get-tuple-element.29.refs_2_, f32[480,128]{1,0:T(8,128)S(1)} %get-tuple-element.30.refs_3_, ...), custom_call_target="tpu_custom_call" | custom-call | tf_op jit(solution)/shard_map/pallas_call | solution.py:414
  20.3 0.5 %collective-permute-start.10 = (f32[20,128]{1,0:T(8,128)S(1)}, f32[20,128]{1,0:T(8,128)S(1)}, u32[]{:S(2)}, u32[]{:S(2)}) collective-permute-start(f32[20,128]{1,0:T(8,128)S(1)} %get-tuple-element.43), channel_id=1, source_target_pairs={{0,4},{4,0},{8,12},{12,8},{1,5},{5,1},{9,13},{13,9},{2,6},{6,2},{1... | collective-permute-start | bytes 30728 | tf_op jit(solution)/shard_map/ppermute | solution.py:347
  20.8 0.8 %collective-permute-done.10 = f32[20,128]{1,0:T(8,128)S(1)} collective-permute-done((f32[20,128]{1,0:T(8,128)S(1)}, f32[20,128]{1,0:T(8,128)S(1)}, u32[]{:S(2)}, u32[]{:S(2)}) %collective-permute-start.10) | collective-permute-done | bytes 10272 | tf_op jit(solution)/shard_map/ppermute | solution.py:347
  21.6 0.0 collective-permute-start.12
  21.7 2.3 %collective-permute-start.8 = (bf16[400,128]{1,0:T(8,128)(2,1)S(1)}, bf16[400,128]{1,0:T(8,128)(2,1)S(1)}, u32[]{:S(2)}, u32[]{:S(2)}) collective-permute-start(bf16[400,128]{1,0:T(8,128)(2,1)S(1)} %shard_map.94.refs_0_), channel_id=1, source_target_pairs={{0,8},{4,12},{8,0},{12,4},{1,9},{5,13},{9,1},{13,5},{2,10},{6,14},... | collective-permute-start | bytes 307208 | tf_op jit(solution)/shard_map/ppermute | solution.py:347
  24.0 0.8 %collective-permute-start.7 = (bf16[400,128]{1,0:T(8,128)(2,1)S(1)}, bf16[400,128]{1,0:T(8,128)(2,1)S(1)}, u32[]{:S(2)}, u32[]{:S(2)}) collective-permute-start(bf16[400,128]{1,0:T(8,128)(2,1)S(1)} %shard_map.94.refs_0_), channel_id=1, source_target_pairs={{0,4},{4,0},{8,12},{12,8},{1,5},{5,1},{9,13},{13,9},{2,6},{6,2},{1... | collective-permute-start | bytes 307208 | tf_op jit(solution)/shard_map/ppermute | solution.py:347
  24.8 3.8 %collective-permute-start.11 = (f32[2,20,128]{2,1,0:T(8,128)S(1)}, f32[2,20,128]{2,1,0:T(8,128)S(1)}, u32[]{:S(2)}, u32[]{:S(2)}) collective-permute-start(f32[2,20,128]{2,1,0:T(8,128)S(1)} %pad_maximum_fusion), channel_id=1, source_target_pairs={{0,0},{1,4},{2,8},{3,12},{4,1},{5,5},{6,9},{7,13},{8,2},{9,6},{10,... | collective-permute-start | bytes 61448 | tf_op jit(solution)/shard_map/ppermute | solution.py:446
  28.7 0.0 collective-permute-done.12
  28.7 0.0 collective-permute-done.8.refs_2_
  28.7 0.1 collective-permute-start.9
  28.8 3.9 %collective-permute-done.11 = f32[2,20,128]{2,1,0:T(8,128)S(1)} collective-permute-done((f32[2,20,128]{2,1,0:T(8,128)S(1)}, f32[2,20,128]{2,1,0:T(8,128)S(1)}, u32[]{:S(2)}, u32[]{:S(2)}) %collective-permute-start.11) | collective-permute-done | bytes 20512 | tf_op jit(solution)/shard_map/ppermute | solution.py:446
  32.6 0.0 collective-permute-done.7.refs_1_
  32.6 0.0 collective-permute-done.9.refs_3_
  32.6 1.3 %shard_map.95 = (f32[1600,128]{1,0:T(8,128)S(1)}, bf16[1600,128]{1,0:T(8,128)(2,1)S(1)}, bf16[480,128]{1,0:T(8,128)(2,1)S(1)}, f32[480,128]{1,0:T(8,128)S(1)}) custom-call(bf16[400,128]{1,0:T(8,128)(2,1)S(1)} %shard_map.94.refs_0_, bf16[400,128]{1,0:T(8,128)(2,1)S(1)} %collective-permute-done.7.refs_1_, bf16[400,128]{1,0:T(8,128)(2,1)S(1)} %collective-permute-done.8.refs_2_, ...), custom_call_target="tpu_custom_call" | custom-call | tf_op jit(solution)/shard_map/pallas_call | solution.py:354
  34.0 1.3 %shard_map.96 = bf16[20,20,128]{2,1,0:T(8,128)(2,1)} custom-call(f32[1600,128]{1,0:T(8,128)S(1)} %get-tuple-element.39.refs_0_, bf16[1600,128]{1,0:T(8,128)(2,1)S(1)} %get-tuple-element.40.refs_1_, bf16[480,128]{1,0:T(8,128)(2,1)S(1)} %get-tuple-element.41.refs_2_, f32[480,128]{1,0:T(8,128)S(1)} %get-tuple-element.42.refs_3_, ...), custom_call_target="tpu_custom_call" | custom-call | tf_op jit(solution)/shard_map/pallas_call | solution.py:451
  (4 shorter events, 0.0 us)
Async XLA Ops:
  0.0 5.0 %copy-start = (bf16[20,20,128]{2,1,0:T(8,128)(2,1)S(1)}, bf16[20,20,128]{2,1,0:T(8,128)(2,1)}, u32[]{:S(2)}) copy-start(bf16[20,20,128]{2,1,0:T(8,128)(2,1)} %pair_ref.1) | copy-start | bytes 307204
  1.5 15.9 %collective-permute-start = (bf16[400,128]{1,0:T(8,128)(2,1)S(1)}, bf16[400,128]{1,0:T(8,128)(2,1)S(1)}, u32[]{:S(2)}, u32[]{:S(2)}) collective-permute-start(bf16[400,128]{1,0:T(8,128)(2,1)S(1)} %get-tuple-element.25.refs_0_), channel_id=1, source_target_pairs={{0,1},{1,0},{2,3},{3,2},{4,5},{5,4},{6,7},{7,6},{8,9},{9,8},{10,11... | collective-permute-start | bytes 307208 | tf_op jit(solution)/shard_map/ppermute | solution.py:347
  2.8 14.5 %collective-permute-start.2 = (bf16[400,128]{1,0:T(8,128)(2,1)S(1)}, bf16[400,128]{1,0:T(8,128)(2,1)S(1)}, u32[]{:S(2)}, u32[]{:S(2)}) collective-permute-start(bf16[400,128]{1,0:T(8,128)(2,1)S(1)} %get-tuple-element.25.refs_0_), channel_id=1, source_target_pairs={{0,3},{1,2},{2,1},{3,0},{4,7},{5,6},{6,5},{7,4},{8,11},{9,10},{10,... | collective-permute-start | bytes 307208 | tf_op jit(solution)/shard_map/ppermute | solution.py:347
  5.0 12.3 %collective-permute-start.1 = (bf16[20,20,128]{2,1,0:T(8,128)(2,1)S(1)}, bf16[20,20,128]{2,1,0:T(8,128)(2,1)S(1)}, u32[]{:S(2)}, u32[]{:S(2)}) collective-permute-start(bf16[20,20,128]{2,1,0:T(8,128)(2,1)S(1)} %copy-done), channel_id=1, source_target_pairs={{0,2},{1,3},{2,0},{3,1},{4,6},{5,7},{6,4},{7,5},{8,10},{9,11},{10,... | collective-permute-start | bytes 307208 | tf_op jit(solution)/shard_map/ppermute | solution.py:347
  5.2 8.2 %collective-permute-start.3 = (f32[20,128]{1,0:T(8,128)S(1)}, f32[20,128]{1,0:T(8,128)S(1)}, u32[]{:S(2)}, u32[]{:S(2)}) collective-permute-start(f32[20,128]{1,0:T(8,128)S(1)} %get-tuple-element.31), channel_id=1, source_target_pairs={{0,0},{1,4},{2,8},{3,12},{4,1},{5,5},{6,9},{7,13},{8,2},{9,6},{10,... | collective-permute-start | bytes 30728 | tf_op jit(solution)/shard_map/ppermute | solution.py:407
  10.8 6.5 %collective-permute-start.5 = (f32[20,128]{1,0:T(8,128)S(1)}, f32[20,128]{1,0:T(8,128)S(1)}, u32[]{:S(2)}, u32[]{:S(2)}) collective-permute-start(f32[20,128]{1,0:T(8,128)S(1)} %get-tuple-element.31), channel_id=1, source_target_pairs={{0,8},{1,12},{2,0},{3,4},{4,9},{5,13},{6,1},{7,5},{8,10},{9,14},{1... | collective-permute-start | bytes 30728 | tf_op jit(solution)/shard_map/ppermute | solution.py:407
  13.4 5.3 %collective-permute-start.4 = (f32[20,128]{1,0:T(8,128)S(1)}, f32[20,128]{1,0:T(8,128)S(1)}, u32[]{:S(2)}, u32[]{:S(2)}) collective-permute-start(f32[20,128]{1,0:T(8,128)S(1)} %collective-permute-done.3.refs_4_), channel_id=1, source_target_pairs={{0,4},{4,0},{8,12},{12,8},{1,5},{5,1},{9,13},{13,9},{2,6},{6,2},{1... | collective-permute-start | bytes 30728 | tf_op jit(solution)/shard_map/ppermute | solution.py:347
  17.3 1.3 %collective-permute-start.6 = (f32[20,128]{1,0:T(8,128)S(1)}, f32[20,128]{1,0:T(8,128)S(1)}, u32[]{:S(2)}, u32[]{:S(2)}) collective-permute-start(f32[20,128]{1,0:T(8,128)S(1)} %collective-permute-done.5.refs_6_), channel_id=1, source_target_pairs={{0,4},{4,0},{8,12},{12,8},{1,5},{5,1},{9,13},{13,9},{2,6},{6,2},{1... | collective-permute-start | bytes 30728 | tf_op jit(solution)/shard_map/ppermute | solution.py:347
  20.3 1.4 %collective-permute-start.10 = (f32[20,128]{1,0:T(8,128)S(1)}, f32[20,128]{1,0:T(8,128)S(1)}, u32[]{:S(2)}, u32[]{:S(2)}) collective-permute-start(f32[20,128]{1,0:T(8,128)S(1)} %get-tuple-element.43), channel_id=1, source_target_pairs={{0,4},{4,0},{8,12},{12,8},{1,5},{5,1},{9,13},{13,9},{2,6},{6,2},{1... | collective-permute-start | bytes 30728 | tf_op jit(solution)/shard_map/ppermute | solution.py:347
  21.6 7.0 %collective-permute-start.12 = (f32[2,20,128]{2,1,0:T(8,128)S(1)}, f32[2,20,128]{2,1,0:T(8,128)S(1)}, u32[]{:S(2)}, u32[]{:S(2)}) collective-permute-start(f32[2,20,128]{2,1,0:T(8,128)S(1)} %pad_maximum_fusion), channel_id=1, source_target_pairs={{0,2},{1,6},{2,10},{3,14},{4,3},{5,7},{6,11},{7,15},{8,0},{9,4},{1... | collective-permute-start | bytes 61448 | tf_op jit(solution)/shard_map/ppermute | solution.py:446
  21.7 7.0 %collective-permute-start.8 = (bf16[400,128]{1,0:T(8,128)(2,1)S(1)}, bf16[400,128]{1,0:T(8,128)(2,1)S(1)}, u32[]{:S(2)}, u32[]{:S(2)}) collective-permute-start(bf16[400,128]{1,0:T(8,128)(2,1)S(1)} %shard_map.94.refs_0_), channel_id=1, source_target_pairs={{0,8},{4,12},{8,0},{12,4},{1,9},{5,13},{9,1},{13,5},{2,10},{6,14},... | collective-permute-start | bytes 307208 | tf_op jit(solution)/shard_map/ppermute | solution.py:347
  24.0 8.7 %collective-permute-start.7 = (bf16[400,128]{1,0:T(8,128)(2,1)S(1)}, bf16[400,128]{1,0:T(8,128)(2,1)S(1)}, u32[]{:S(2)}, u32[]{:S(2)}) collective-permute-start(bf16[400,128]{1,0:T(8,128)(2,1)S(1)} %shard_map.94.refs_0_), channel_id=1, source_target_pairs={{0,4},{4,0},{8,12},{12,8},{1,5},{5,1},{9,13},{13,9},{2,6},{6,2},{1... | collective-permute-start | bytes 307208 | tf_op jit(solution)/shard_map/ppermute | solution.py:347
  24.8 7.8 %collective-permute-start.11 = (f32[2,20,128]{2,1,0:T(8,128)S(1)}, f32[2,20,128]{2,1,0:T(8,128)S(1)}, u32[]{:S(2)}, u32[]{:S(2)}) collective-permute-start(f32[2,20,128]{2,1,0:T(8,128)S(1)} %pad_maximum_fusion), channel_id=1, source_target_pairs={{0,0},{1,4},{2,8},{3,12},{4,1},{5,5},{6,9},{7,13},{8,2},{9,6},{10,... | collective-permute-start | bytes 61448 | tf_op jit(solution)/shard_map/ppermute | solution.py:446
  28.7 4.0 %collective-permute-start.9 = (bf16[400,128]{1,0:T(8,128)(2,1)S(1)}, bf16[400,128]{1,0:T(8,128)(2,1)S(1)}, u32[]{:S(2)}, u32[]{:S(2)}) collective-permute-start(bf16[400,128]{1,0:T(8,128)(2,1)S(1)} %collective-permute-done.8.refs_2_), channel_id=1, source_target_pairs={{0,4},{4,0},{8,12},{12,8},{1,5},{5,1},{9,13},{13,9},{2,6},{6,2},{1... | collective-permute-start | bytes 307208 | tf_op jit(solution)/shard_map/ppermute | solution.py:347

commit v5 on v4

--- a/solution.py
+++ b/solution.py
@@ -160,44 +160,67 @@
     return jnp.broadcast_to(jnp.concatenate([ids, pad], axis=1), (8, reach)).astype(BF)
 
 
+def copies_of(moves, sems):
+    copies = [pltpu.make_async_copy(a, b, sems.at[i]) for i, (a, b) in enumerate(moves)]
+    for copy in copies:
+        copy.start()
+    return copies
+
+
+def chain_weights(ref, layer, heads):
+    return [ref[layer : layer + 1, h : h + 1] for h in range(heads)]
+
+
 def first_bias_kernel(
-    heads, span, side, pair_ref, in_ref, out_ref, up_ref, down_ref, weight_ref, ids_ref, mask_ref,
-    chain_ref, o_ref, chain_out, row_mask, col_mask, tight, in_out, out_out, up_out, down_out,
-    weight_out, own, pad, packed, ids_in, mask_in, chain_in, sems,
+    heads, span, pair_ref, weight_ref, ids_ref, chain_ref, o_ref, tight,
+    own, pad, packed, weight_in, ids_in, chain_in, sems,
 ):
     nr, nc, width = pair_ref.shape
     rows = pad.shape[1]
     lanes = heads * span
-    moves = (
-        (ids_ref, ids_in), (mask_ref, mask_in), (chain_ref, chain_in), (weight_ref, weight_out),
-        (pair_ref, own), (in_ref, in_out), (out_ref, out_out), (up_ref, up_out),
-        (down_ref, down_out),
-    )
-    copies = [pltpu.make_async_copy(a, b, sems.at[i]) for i, (a, b) in enumerate(moves)]
-    for copy in copies:
-        copy.start()
+    copies = copies_of(
+        ((pair_ref, own), (weight_ref, weight_in), (ids_ref, ids_in), (chain_ref, chain_in)), sems
+    )
     gr, gc = lax.axis_index("gr"), lax.axis_index("gc")
     pad[...] = jnp.zeros_like(pad)
-    for copy in copies[0:4]:
+    for copy in copies[1:]:
         copy.wait()
     ids = spread_ids(ids_in, lanes)
-    weights = [[chain_in[a : a + 1, h : h + 1] for h in range(heads)] for a in range(2)]
-    here = chain_terms(ids, gr * nr, gc * nc, weights[0], heads, span)
-    chain_out[...] = chain_terms(ids, gc * nc, gr * nr, weights[1], heads, span)[
-        0 : chain_out.shape[0]
-    ]
-    mask = spread_ids(mask_in, lanes)
-    row_mask[...] = key_mask(mask, gc, side, nc, lanes)
-    col_mask[...] = key_mask(mask, gr, side, nr, lanes)
-    copies[4].wait()
+    here = chain_terms(ids, gr * nr, gc * nc, chain_weights(chain_in, 0, heads), heads, span)
+    copies[0].wait()
     exact = own[...].astype(F32)
     pad[:, 0:nc, :] = exact
     for j in range(nr):
         packed[j * nc : (j + 1) * nc, :] = exact[j]
     tight[...] = packed[...].astype(BF)
-    terms = every_head(norm32(pad[...].reshape(nr * rows, width)), weight_out[0], span)
+    terms = every_head(norm32(pad[...].reshape(nr * rows, width)), weight_in[0], span)
     o_ref[...] = select_terms(terms, here[0:rows], rows, nr, span)[0:nc]
-    for copy in copies[5:]:
+
+
+def stage_kernel(
+    heads, span, side, nr, nc, in_ref, out_ref, up_ref, down_ref, weight_ref, ids_ref, mask_ref,
+    chain_ref, in_out, out_out, up_out, down_out, weight_out, chain_out, row_mask, col_mask,
+    ids_in, mask_in, chain_in, sems,
+):
+    lanes = heads * span
+    copies = copies_of(
+        (
+            (ids_ref, ids_in), (mask_ref, mask_in), (chain_ref, chain_in), (in_ref, in_out),
+            (out_ref, out_out), (up_ref, up_out), (down_ref, down_out), (weight_ref, weight_out),
+        ),
+        sems,
+    )
+    gr, gc = lax.axis_index("gr"), lax.axis_index("gc")
+    for copy in copies[0:3]:
+        copy.wait()
+    ids = spread_ids(ids_in, lanes)
+    chain_out[...] = chain_terms(
+        ids, gc * nc, gr * nr, chain_weights(chain_in, 1, heads), heads, span
+    )[0 : chain_out.shape[0]]
+    mask = spread_ids(mask_in, lanes)
+    row_mask[...] = key_mask(mask, gc, side, nc, lanes)
+    col_mask[...] = key_mask(mask, gr, side, nr, lanes)
+    for copy in copies[3:]:
         copy.wait()
 
 
@@ -215,29 +238,37 @@
             for b in range(nb):
                 gather[b, k * nt : (k + 1) * nt, :] = value[b * nt : (b + 1) * nt]
     rows = base_ref.shape[0] // nb
-    exact = normal(gather[...].reshape(nb * length, width))
-    everyone = exact.astype(BF)
-    mine = jnp.concatenate([everyone[b * length : b * length + span] for b in range(nb)], axis=0)
-    base_ref[...] = jnp.concatenate([gather[b, 0:rows, :] for b in range(nb)], axis=0)
-    query = jnp.dot(mine, weights[:, 0:width], preferred_element_type=F32).astype(BF)
-    tight = jnp.concatenate([exact[b * length : b * length + rows] for b in range(nb)], axis=0)
-    g_ref[...] = jnp.dot(
-        tight.astype(BF), weights[:, 3 * width :], preferred_element_type=F32
-    ).astype(BF)
-    keys = jnp.dot(everyone, weights[:, width : 2 * width], preferred_element_type=F32).astype(BF)
-    v_ref[...] = jnp.dot(
-        everyone, weights[:, 2 * width : 3 * width], preferred_element_type=F32
-    ).astype(BF)
     head_of = lax.broadcasted_iota(jnp.int32, (span, width), 1) // (width // heads)
     scale = LOG2E * (width // heads) ** (-0.5)
-    for b in range(nb):
-        q = query[b * span : (b + 1) * span]
-        wide = jnp.concatenate(
-            [jnp.where(head_of == h, q, jnp.zeros_like(q)) for h in range(heads)], axis=0
+    step = nb // 2 if nb % 4 == 0 else nb
+    for g in range(0, nb, step):
+        exact = normal(gather[g : g + step].reshape(step * length, width))
+        everyone = exact.astype(BF)
+        part = slice(g * length, (g + step) * length)
+        mine = jnp.concatenate(
+            [everyone[b * length : b * length + span] for b in range(step)], axis=0
         )
-        s_ref[b * length : (b + 1) * length] = scale * contract(
-            keys[b * length : (b + 1) * length], wide, 1, 1
-        )
+        tight = jnp.concatenate([exact[b * length : b * length + rows] for b in range(step)], axis=0)
+        some = slice(g * rows, (g + step) * rows)
+        base_ref[some] = jnp.concatenate([gather[g + b, 0:rows, :] for b in range(step)], axis=0)
+        query = jnp.dot(mine, weights[:, 0:width], preferred_element_type=F32).astype(BF)
+        g_ref[some] = jnp.dot(
+            tight.astype(BF), weights[:, 3 * width :], preferred_element_type=F32
+        ).astype(BF)
+        keys = jnp.dot(
+            everyone, weights[:, width : 2 * width], preferred_element_type=F32
+        ).astype(BF)
+        v_ref[part] = jnp.dot(
+            everyone, weights[:, 2 * width : 3 * width], preferred_element_type=F32
+        ).astype(BF)
+        for b in range(step):
+            q = query[b * span : (b + 1) * span]
+            wide = jnp.concatenate(
+                [jnp.where(head_of == h, q, jnp.zeros_like(q)) for h in range(heads)], axis=0
+            )
+            s_ref[(g + b) * length : (g + b + 1) * length] = scale * contract(
+                keys[b * length : (b + 1) * length], wide, 1, 1
+            )
 
 
 def attend(heads, span, pieces, s_ref, v_ref, g_ref, base_ref, bias_refs, mask_ref, out_w, table, probs):
@@ -375,39 +406,55 @@
     lanes = heads * span
     cells = [(r, c) for r in range(side) for c in range(side)]
     weight = jnp.transpose(bias_weight, (0, 2, 1))
-    plain = (attn_in, attn_out, trans_up, trans_down)
+    ids, real = chain_ids[None, :], mask[None, :]
+
+    def in_hbm(*arrays):
+        return [pltpu.with_memory_space_constraint(a, pltpu.HBM) for a in arrays]
+
+    def scratch_for(*arrays):
+        return [pltpu.VMEM(a.shape, a.dtype) for a in arrays]
 
     far = swap(pair, "gc", 2)
-    sources = (pair, *plain, weight, chain_ids[None, :], mask[None, :], chain_bias)
-    copied = (*plain, weight)
-    piece, chain_two, row_mask, col_mask, own, *plain, weight = pl.pallas_call(
-        functools.partial(first_bias_kernel, heads, span, side),
+    piece, own = pl.pallas_call(
+        functools.partial(first_bias_kernel, heads, span),
         out_shape=(
             jax.ShapeDtypeStruct((nc, lanes), F32),
-            jax.ShapeDtypeStruct((up_to_8(nr), lanes), F32),
-            jax.ShapeDtypeStruct((side * nc, lanes), F32),
-            jax.ShapeDtypeStruct((side * nr, lanes), F32),
             jax.ShapeDtypeStruct((nr * nc, width), BF),
-            *(jax.ShapeDtypeStruct(a.shape, a.dtype) for a in copied),
         ),
-        in_specs=[HBM] * len(sources),
-        out_specs=(VMEM,) * (5 + len(copied)),
+        in_specs=[HBM] * 4,
+        out_specs=(VMEM,) * 2,
         scratch_shapes=[
-            pltpu.VMEM(pair.shape, BF),
+            *scratch_for(pair),
             pltpu.VMEM((nr, up_to_8(nc), width), F32),
             pltpu.VMEM((nr * nc, width), F32),
-            *(pltpu.VMEM(a.shape, a.dtype) for a in sources[-3:]),
-            pltpu.SemaphoreType.DMA((len(sources),)),
+            *scratch_for(weight, ids, chain_bias),
+            pltpu.SemaphoreType.DMA((4,)),
         ],
         compiler_params=PARAMS,
-    )(*(pltpu.with_memory_space_constraint(a, pltpu.HBM) for a in sources))
-    attn_in, attn_out, trans_up, trans_down = plain
-    pieces = []
-    for k in range(0, side, 2):
+    )(*in_hbm(pair, weight, ids, chain_bias))
+    plain = (attn_in, attn_out, trans_up, trans_down, weight)
+    small = (ids, real, chain_bias)
+    attn_in, attn_out, trans_up, trans_down, weight, chain_two, row_mask, col_mask = (
+        pl.pallas_call(
+            functools.partial(stage_kernel, heads, span, side, nr, nc),
+            out_shape=(
+                *(jax.ShapeDtypeStruct(a.shape, a.dtype) for a in plain),
+                jax.ShapeDtypeStruct((up_to_8(nr), lanes), F32),
+                jax.ShapeDtypeStruct((side * nc, lanes), F32),
+                jax.ShapeDtypeStruct((side * nr, lanes), F32),
+            ),
+            in_specs=[HBM] * 8,
+            out_specs=(VMEM,) * 8,
+            scratch_shapes=[*scratch_for(*small), pltpu.SemaphoreType.DMA((8,))],
+            compiler_params=PARAMS,
+        )(*in_hbm(*plain, *small))
+    )
+    pieces = [None] * side
+    for k in FIRST_MOVES:
         got = lax.ppermute(
             piece, ("gr", "gc"), [(r * side + c, (c ^ k) * side + r) for r, c in cells]
         )
-        pieces += [got, swap(got, "gr", 1)]
+        pieces[k], pieces[k ^ 1] = got, swap(got, "gr", 1)
     last = swap(own, "gc", 3)
     near = swap(own, "gc", 1)
     heard = scores(0, heads, span, (nr, nc), [own, near, far, last], attn_in)
@@ -441,12 +488,12 @@
         far = swap(tile, "gr", k)
         chunks += [far, swap(far, "gr", 1)]
     both = jnp.stack([piece, other])
-    pieces = []
-    for k in range(0, side, 2):
+    pieces = [None] * side
+    for k in LAST_MOVES:
         got = lax.ppermute(
             both, ("gr", "gc"), [(r * side + c, c * side + (r ^ k)) for r, c in cells]
         )
-        pieces += [got[0], got[1]]
+        pieces[k], pieces[k ^ 1] = got[0], got[1]
     heard = scores(1, heads, span, (nc, nr), chunks, attn_in)
     return pl.pallas_call(
         functools.partial(second_kernel, heads, span, side),
@@ -462,6 +509,10 @@
     )(*heard, *pieces, col_mask, attn_out)
 
 
+FIRST_MOVES = (0, 2)
+LAST_MOVES = (2, 1)
+
+
 def solution(mesh):
     shape = dict(mesh.shape)
     in_specs = (P(("jobs", "gr"), "gc", None), P("jobs"), P("jobs"), P(), P(), P(), P(), P(), P())

time: 35.4 us -> 35 us (0.989)
  the two profiles are of different devices: /device:TPU:3 before, /device:TPU:0 now
where the time goes in v5:
time: 35 us; the launch traced here: 34.8 us
  starting transfers between devices  16 us (46%)
  waiting for transfers between devices  10.7 us (31%)
  Pallas kernels  8.06 us (23%)
    ppermute x9, starting transfers between devices, swap(): return lax.ppermute(array, axis, [(i, i ^ k) for i in range(size)])  6.41 us
    ppermute x2, starting transfers between devices, fast_device(): lax.ppermute(piece, ('gr', 'gc'), [(r * side + c, (c ^ k) * side + r) for...  6.22 us
    ppermute x9, waiting for transfers between devices, swap(): return lax.ppermute(array, axis, [(i, i ^ k) for i in range(size)])  5.46 us
    ppermute x2, waiting for transfers between devices, fast_device(): lax.ppermute(piece, ('gr', 'gc'), [(r * side + c, (c ^ k) * side + r) for...  4.88 us
    ppermute x2, starting transfers between devices, fast_device(): lax.ppermute(both, ('gr', 'gc'), [(r * side + c, c * side + (r ^ k)) for...  3.35 us
    pallas_call x2, Pallas kernels, scores(): pl.pallas_call(functools.partial(score_kernel, layer, heads, span, len(ch...  2.55 us
    pallas_call x1, Pallas kernels, fast_device(): pl.pallas_call(functools.partial(first_kernel, heads, span, side), out_sh...  1.59 us
    pallas_call x1, Pallas kernels, fast_device(): pl.pallas_call(functools.partial(first_bias_kernel, heads, span), out_sha...  1.37 us
  transfers between devices with their start and end apart: 13, of which 5 were waited for; matrix products, arithmetic and copies ran while one was open for 0% of the time, Pallas kernels for 7%

profile of v5, /device:TPU:0, one launch (start us, length us, event | category | flops | bytes accessed | tf_op | source)
XLA Modules:
  0.0 34.8 jit_solution(7337384958175811288)
XLA Ops:
  0.0 0.0 copy-start
  0.0 1.4 %shard_map.91 = (f32[20,128]{1,0:T(8,128)S(1)}, bf16[400,128]{1,0:T(8,128)(2,1)S(1)}) custom-call(bf16[20,20,128]{2,1,0:T(8,128)(2,1)} %pair_ref.1, bf16[2,4,128]{2,1,0:T(4,128)(2,1)} %bitcast.15, s32[1,80]{1,0:T(1,128)} %bitcast.17, f32[2,4]{1,0:T(2,128)} %chain_ref.3), custom_call_target="tpu_custom_call" | custom-call | tf_op jit(solution)/shard_map/pallas_call | solution.py:418
  1.4 3.1 %collective-permute-start = (bf16[400,128]{1,0:T(8,128)(2,1)S(1)}, bf16[400,128]{1,0:T(8,128)(2,1)S(1)}, u32[]{:S(2)}, u32[]{:S(2)}) collective-permute-start(bf16[400,128]{1,0:T(8,128)(2,1)S(1)} %get-tuple-element.25.refs_0_), channel_id=1, source_target_pairs={{0,1},{1,0},{2,3},{3,2},{4,5},{5,4},{6,7},{7,6},{8,9},{9,8},{10,11... | collective-permute-start | bytes 307208 | tf_op jit(solution)/shard_map/ppermute | solution.py:378
  4.5 2.5 %collective-permute-start.2 = (bf16[400,128]{1,0:T(8,128)(2,1)S(1)}, bf16[400,128]{1,0:T(8,128)(2,1)S(1)}, u32[]{:S(2)}, u32[]{:S(2)}) collective-permute-start(bf16[400,128]{1,0:T(8,128)(2,1)S(1)} %get-tuple-element.25.refs_0_), channel_id=1, source_target_pairs={{0,3},{1,2},{2,1},{3,0},{4,7},{5,6},{6,5},{7,4},{8,11},{9,10},{10,... | collective-permute-start | bytes 307208 | tf_op jit(solution)/shard_map/ppermute | solution.py:378
  7.0 0.0 copy-done
  7.0 0.1 collective-permute-start.1
  7.1 0.7 %collective-permute-start.3 = (f32[20,128]{1,0:T(8,128)S(1)}, f32[20,128]{1,0:T(8,128)S(1)}, u32[]{:S(2)}, u32[]{:S(2)}) collective-permute-start(f32[20,128]{1,0:T(8,128)S(1)} %get-tuple-element.31), channel_id=1, source_target_pairs={{0,0},{1,4},{2,8},{3,12},{4,1},{5,5},{6,9},{7,13},{8,2},{9,6},{10,... | collective-permute-start | bytes 30728 | tf_op jit(solution)/shard_map/ppermute | solution.py:454
  7.7 5.6 %collective-permute-start.5 = (f32[20,128]{1,0:T(8,128)S(1)}, f32[20,128]{1,0:T(8,128)S(1)}, u32[]{:S(2)}, u32[]{:S(2)}) collective-permute-start(f32[20,128]{1,0:T(8,128)S(1)} %get-tuple-element.31), channel_id=1, source_target_pairs={{0,8},{1,12},{2,0},{3,4},{4,9},{5,13},{6,1},{7,5},{8,10},{9,14},{1... | collective-permute-start | bytes 30728 | tf_op jit(solution)/shard_map/ppermute | solution.py:454
  13.3 0.0 collective-permute-done.3.refs_4_
  13.3 0.0 collective-permute-start.4
  13.3 4.9 %collective-permute-done.5.refs_6_ = f32[20,128]{1,0:T(8,128)S(1)} collective-permute-done((f32[20,128]{1,0:T(8,128)S(1)}, f32[20,128]{1,0:T(8,128)S(1)}, u32[]{:S(2)}, u32[]{:S(2)}) %collective-permute-start.5) | collective-permute-done | bytes 10272 | tf_op jit(solution)/shard_map/ppermute | solution.py:454
  18.2 0.0 collective-permute-start.6
  18.2 1.2 %shard_map.92 = (bf16[2,128,512]{2,1,0:T(8,128)(2,1)S(1)}, bf16[2,128,128]{2,1,0:T(8,128)(2,1)S(1)}, bf16[128,512]{1,0:T(8,128)(2,1)S(1)}, bf16[512,128]{1,0:T(8...) custom-call(bf16[2,128,512]{2,1,0:T(8,128)(2,1)} %in_ref.1, ...), custom_call_target="tpu_custom_call" | custom-call | tf_op jit(solution)/shard_map/pallas_call | solution.py:438
  19.4 0.0 collective-permute-done.refs_1_
  19.4 0.0 collective-permute-done.2.refs_3_
  19.4 0.0 collective-permute-done.1.refs_2_
  19.4 1.3 %shard_map.93 = (f32[1600,128]{1,0:T(8,128)S(1)}, bf16[1600,128]{1,0:T(8,128)(2,1)S(1)}, bf16[480,128]{1,0:T(8,128)(2,1)S(1)}, f32[480,128]{1,0:T(8,128)S(1)}) custom-call(bf16[400,128]{1,0:T(8,128)(2,1)S(1)} %get-tuple-element.25.refs_0_, bf16[400,128]{1,0:T(8,128)(2,1)S(1)} %collective-permute-done.refs_1_, ...), custom_call_target="tpu_custom_call" | custom-call | tf_op jit(solution)/shard_map/pallas_call | solution.py:385
  20.7 0.0 collective-permute-done.4.refs_5_
  20.7 0.0 collective-permute-done.6.refs_7_
  20.7 1.6 %shard_map.94 = (f32[480,128]{1,0:T(8,128)S(1)}, f32[20,128]{1,0:T(8,128)S(1)}) custom-call(f32[1600,128]{1,0:T(8,128)S(1)} %get-tuple-element.27.refs_0_, bf16[1600,128]{1,0:T(8,128)(2,1)S(1)} %get-tuple-element.28.refs_1_, bf16[480,128]{1,0:T(8,128)(2,1)S(1)} %get-tuple-element.29.refs_2_, f32[480,128]{1,0:T(8,128)S(1)} %get-tuple-element.30.refs_3_, ...), custom_call_target="tpu_custom_call" | custom-call | tf_op jit(solution)/shard_map/pallas_call | solution.py:461
  22.3 0.5 %collective-permute-start.10 = (f32[20,128]{1,0:T(8,128)S(1)}, f32[20,128]{1,0:T(8,128)S(1)}, u32[]{:S(2)}, u32[]{:S(2)}) collective-permute-start(f32[20,128]{1,0:T(8,128)S(1)} %get-tuple-element.43), channel_id=1, source_target_pairs={{0,4},{4,0},{8,12},{12,8},{1,5},{5,1},{9,13},{13,9},{2,6},{6,2},{1... | collective-permute-start | bytes 30728 | tf_op jit(solution)/shard_map/ppermute | solution.py:378
  22.9 0.8 %collective-permute-done.10 = f32[20,128]{1,0:T(8,128)S(1)} collective-permute-done((f32[20,128]{1,0:T(8,128)S(1)}, f32[20,128]{1,0:T(8,128)S(1)}, u32[]{:S(2)}, u32[]{:S(2)}) %collective-permute-start.10) | collective-permute-done | bytes 10272 | tf_op jit(solution)/shard_map/ppermute | solution.py:378
  23.7 2.4 %collective-permute-start.12 = (f32[2,20,128]{2,1,0:T(8,128)S(1)}, f32[2,20,128]{2,1,0:T(8,128)S(1)}, u32[]{:S(2)}, u32[]{:S(2)}) collective-permute-start(f32[2,20,128]{2,1,0:T(8,128)S(1)} %pad_maximum_fusion), channel_id=1, source_target_pairs={{0,2},{1,6},{2,10},{3,14},{4,3},{5,7},{6,11},{7,15},{8,0},{9,4},{1... | collective-permute-start | bytes 61448 | tf_op jit(solution)/shard_map/ppermute | solution.py:493
  26.1 0.1 collective-permute-start.8
  26.2 0.1 collective-permute-start.7
  26.3 1.0 %collective-permute-start.11 = (f32[2,20,128]{2,1,0:T(8,128)S(1)}, f32[2,20,128]{2,1,0:T(8,128)S(1)}, u32[]{:S(2)}, u32[]{:S(2)}) collective-permute-start(f32[2,20,128]{2,1,0:T(8,128)S(1)} %pad_maximum_fusion), channel_id=1, source_target_pairs={{0,1},{1,5},{2,9},{3,13},{4,0},{5,4},{6,8},{7,12},{8,3},{9,7},{10,... | collective-permute-start | bytes 61448 | tf_op jit(solution)/shard_map/ppermute | solution.py:493
  27.3 0.3 collective-permute-done.12
  27.6 3.3 %collective-permute-done.8.refs_2_ = bf16[400,128]{1,0:T(8,128)(2,1)S(1)} collective-permute-done((bf16[400,128]{1,0:T(8,128)(2,1)S(1)}, bf16[400,128]{1,0:T(8,128)(2,1)S(1)}, u32[]{:S(2)}, u32[]{:S(2)}) %collective-permute-start.8) | collective-permute-done | bytes 102432 | tf_op jit(solution)/shard_map/ppermute | solution.py:378
  30.9 0.0 collective-permute-start.9
  30.9 0.0 collective-permute-done.11
  30.9 0.0 collective-permute-done.7.refs_1_
  31.0 1.3 %collective-permute-done.9.refs_3_ = bf16[400,128]{1,0:T(8,128)(2,1)S(1)} collective-permute-done((bf16[400,128]{1,0:T(8,128)(2,1)S(1)}, bf16[400,128]{1,0:T(8,128)(2,1)S(1)}, u32[]{:S(2)}, u32[]{:S(2)}) %collective-permute-start.9) | collective-permute-done | bytes 102432 | tf_op jit(solution)/shard_map/ppermute | solution.py:378
  32.2 1.3 %shard_map.96 = (f32[1600,128]{1,0:T(8,128)S(1)}, bf16[1600,128]{1,0:T(8,128)(2,1)S(1)}, bf16[480,128]{1,0:T(8,128)(2,1)S(1)}, f32[480,128]{1,0:T(8,128)S(1)}) custom-call(bf16[400,128]{1,0:T(8,128)(2,1)S(1)} %shard_map.95.refs_0_, bf16[400,128]{1,0:T(8,128)(2,1)S(1)} %collective-permute-done.7.refs_1_, bf16[400,128]{1,0:T(8,128)(2,1)S(1)} %collective-permute-done.8.refs_2_, ...), custom_call_target="tpu_custom_call" | custom-call | tf_op jit(solution)/shard_map/pallas_call | solution.py:385
  33.5 1.3 %shard_map.97 = bf16[20,20,128]{2,1,0:T(8,128)(2,1)} custom-call(f32[1600,128]{1,0:T(8,128)S(1)} %get-tuple-element.39.refs_0_, bf16[1600,128]{1,0:T(8,128)(2,1)S(1)} %get-tuple-element.40.refs_1_, bf16[480,128]{1,0:T(8,128)(2,1)S(1)} %get-tuple-element.41.refs_2_, f32[480,128]{1,0:T(8,128)S(1)} %get-tuple-element.42.refs_3_, ...), custom_call_target="tpu_custom_call" | custom-call | tf_op jit(solution)/shard_map/pallas_call | solution.py:498
  (4 shorter events, 0.0 us)
Async XLA Ops:
  0.0 7.0 %copy-start = (bf16[20,20,128]{2,1,0:T(8,128)(2,1)S(1)}, bf16[20,20,128]{2,1,0:T(8,128)(2,1)}, u32[]{:S(2)}) copy-start(bf16[20,20,128]{2,1,0:T(8,128)(2,1)} %pair_ref.1) | copy-start | bytes 307204
  1.4 18.0 %collective-permute-start = (bf16[400,128]{1,0:T(8,128)(2,1)S(1)}, bf16[400,128]{1,0:T(8,128)(2,1)S(1)}, u32[]{:S(2)}, u32[]{:S(2)}) collective-permute-start(bf16[400,128]{1,0:T(8,128)(2,1)S(1)} %get-tuple-element.25.refs_0_), channel_id=1, source_target_pairs={{0,1},{1,0},{2,3},{3,2},{4,5},{5,4},{6,7},{7,6},{8,9},{9,8},{10,11... | collective-permute-start | bytes 307208 | tf_op jit(solution)/shard_map/ppermute | solution.py:378
  4.5 14.9 %collective-permute-start.2 = (bf16[400,128]{1,0:T(8,128)(2,1)S(1)}, bf16[400,128]{1,0:T(8,128)(2,1)S(1)}, u32[]{:S(2)}, u32[]{:S(2)}) collective-permute-start(bf16[400,128]{1,0:T(8,128)(2,1)S(1)} %get-tuple-element.25.refs_0_), channel_id=1, source_target_pairs={{0,3},{1,2},{2,1},{3,0},{4,7},{5,6},{6,5},{7,4},{8,11},{9,10},{10,... | collective-permute-start | bytes 307208 | tf_op jit(solution)/shard_map/ppermute | solution.py:378
  7.0 12.5 %collective-permute-start.1 = (bf16[20,20,128]{2,1,0:T(8,128)(2,1)S(1)}, bf16[20,20,128]{2,1,0:T(8,128)(2,1)S(1)}, u32[]{:S(2)}, u32[]{:S(2)}) collective-permute-start(bf16[20,20,128]{2,1,0:T(8,128)(2,1)S(1)} %copy-done), channel_id=1, source_target_pairs={{0,2},{1,3},{2,0},{3,1},{4,6},{5,7},{6,4},{7,5},{8,10},{9,11},{10,... | collective-permute-start | bytes 307208 | tf_op jit(solution)/shard_map/ppermute | solution.py:378
  7.1 6.2 %collective-permute-start.3 = (f32[20,128]{1,0:T(8,128)S(1)}, f32[20,128]{1,0:T(8,128)S(1)}, u32[]{:S(2)}, u32[]{:S(2)}) collective-permute-start(f32[20,128]{1,0:T(8,128)S(1)} %get-tuple-element.31), channel_id=1, source_target_pairs={{0,0},{1,4},{2,8},{3,12},{4,1},{5,5},{6,9},{7,13},{8,2},{9,6},{10,... | collective-permute-start | bytes 30728 | tf_op jit(solution)/shard_map/ppermute | solution.py:454
  7.7 10.4 %collective-permute-start.5 = (f32[20,128]{1,0:T(8,128)S(1)}, f32[20,128]{1,0:T(8,128)S(1)}, u32[]{:S(2)}, u32[]{:S(2)}) collective-permute-start(f32[20,128]{1,0:T(8,128)S(1)} %get-tuple-element.31), channel_id=1, source_target_pairs={{0,8},{1,12},{2,0},{3,4},{4,9},{5,13},{6,1},{7,5},{8,10},{9,14},{1... | collective-permute-start | bytes 30728 | tf_op jit(solution)/shard_map/ppermute | solution.py:454
  13.3 7.4 %collective-permute-start.4 = (f32[20,128]{1,0:T(8,128)S(1)}, f32[20,128]{1,0:T(8,128)S(1)}, u32[]{:S(2)}, u32[]{:S(2)}) collective-permute-start(f32[20,128]{1,0:T(8,128)S(1)} %collective-permute-done.3.refs_4_), channel_id=1, source_target_pairs={{0,4},{4,0},{8,12},{12,8},{1,5},{5,1},{9,13},{13,9},{2,6},{6,2},{1... | collective-permute-start | bytes 30728 | tf_op jit(solution)/shard_map/ppermute | solution.py:378
  18.2 2.5 %collective-permute-start.6 = (f32[20,128]{1,0:T(8,128)S(1)}, f32[20,128]{1,0:T(8,128)S(1)}, u32[]{:S(2)}, u32[]{:S(2)}) collective-permute-start(f32[20,128]{1,0:T(8,128)S(1)} %collective-permute-done.5.refs_6_), channel_id=1, source_target_pairs={{0,4},{4,0},{8,12},{12,8},{1,5},{5,1},{9,13},{13,9},{2,6},{6,2},{1... | collective-permute-start | bytes 30728 | tf_op jit(solution)/shard_map/ppermute | solution.py:378
  22.3 1.4 %collective-permute-start.10 = (f32[20,128]{1,0:T(8,128)S(1)}, f32[20,128]{1,0:T(8,128)S(1)}, u32[]{:S(2)}, u32[]{:S(2)}) collective-permute-start(f32[20,128]{1,0:T(8,128)S(1)} %get-tuple-element.43), channel_id=1, source_target_pairs={{0,4},{4,0},{8,12},{12,8},{1,5},{5,1},{9,13},{13,9},{2,6},{6,2},{1... | collective-permute-start | bytes 30728 | tf_op jit(solution)/shard_map/ppermute | solution.py:378
  23.7 3.9 %collective-permute-start.12 = (f32[2,20,128]{2,1,0:T(8,128)S(1)}, f32[2,20,128]{2,1,0:T(8,128)S(1)}, u32[]{:S(2)}, u32[]{:S(2)}) collective-permute-start(f32[2,20,128]{2,1,0:T(8,128)S(1)} %pad_maximum_fusion), channel_id=1, source_target_pairs={{0,2},{1,6},{2,10},{3,14},{4,3},{5,7},{6,11},{7,15},{8,0},{9,4},{1... | collective-permute-start | bytes 61448 | tf_op jit(solution)/shard_map/ppermute | solution.py:493
  26.1 4.8 %collective-permute-start.8 = (bf16[400,128]{1,0:T(8,128)(2,1)S(1)}, bf16[400,128]{1,0:T(8,128)(2,1)S(1)}, u32[]{:S(2)}, u32[]{:S(2)}) collective-permute-start(bf16[400,128]{1,0:T(8,128)(2,1)S(1)} %shard_map.95.refs_0_), channel_id=1, source_target_pairs={{0,8},{4,12},{8,0},{12,4},{1,9},{5,13},{9,1},{13,5},{2,10},{6,14},... | collective-permute-start | bytes 307208 | tf_op jit(solution)/shard_map/ppermute | solution.py:378
  26.2 4.7 %collective-permute-start.7 = (bf16[400,128]{1,0:T(8,128)(2,1)S(1)}, bf16[400,128]{1,0:T(8,128)(2,1)S(1)}, u32[]{:S(2)}, u32[]{:S(2)}) collective-permute-start(bf16[400,128]{1,0:T(8,128)(2,1)S(1)} %shard_map.95.refs_0_), channel_id=1, source_target_pairs={{0,4},{4,0},{8,12},{12,8},{1,5},{5,1},{9,13},{13,9},{2,6},{6,2},{1... | collective-permute-start | bytes 307208 | tf_op jit(solution)/shard_map/ppermute | solution.py:378
  26.3 4.7 %collective-permute-start.11 = (f32[2,20,128]{2,1,0:T(8,128)S(1)}, f32[2,20,128]{2,1,0:T(8,128)S(1)}, u32[]{:S(2)}, u32[]{:S(2)}) collective-permute-start(f32[2,20,128]{2,1,0:T(8,128)S(1)} %pad_maximum_fusion), channel_id=1, source_target_pairs={{0,1},{1,5},{2,9},{3,13},{4,0},{5,4},{6,8},{7,12},{8,3},{9,7},{10,... | collective-permute-start | bytes 61448 | tf_op jit(solution)/shard_map/ppermute | solution.py:493
  30.9 1.3 %collective-permute-start.9 = (bf16[400,128]{1,0:T(8,128)(2,1)S(1)}, bf16[400,128]{1,0:T(8,128)(2,1)S(1)}, u32[]{:S(2)}, u32[]{:S(2)}) collective-permute-start(bf16[400,128]{1,0:T(8,128)(2,1)S(1)} %collective-permute-done.8.refs_2_), channel_id=1, source_target_pairs={{0,4},{4,0},{8,12},{12,8},{1,5},{5,1},{9,13},{13,9},{2,6},{6,2},{1... | collective-permute-start | bytes 307208 | tf_op jit(solution)/shard_map/ppermute | solution.py:378
